TPU v7x, 256 devices: a whole 4x4x8 slice. The times are simulated.
256 devices in a mesh: dp: 32 (over x, z), expert: 8 (over y, core).
Axes of the slice: x: 4, y: 4, z: 8, core: 2. Of those that a mesh axis runs over, the one named last changes fastest.
Arguments:
- tokens: bfloat16 [4096, 4096], P('dp', 'expert'), may hold values from -6 to 6
- expert_ids: int32 [4096, 8], P('dp'), may hold values from 0 to 31, all different within a row; in each aligned block of 128 rows (0 to 127, 128 to 255, ...) at most 40 rows name the same one
- scores: float32 [4096, 8], P('dp'), may hold values from 0.05 to 1
- weight_in: bfloat16 [32, 4096, 2048], P('dp', 'expert'), may hold values from -0.09375 to 0.09375
- weight_out: bfloat16 [32, 1024, 4096], P('dp', None, 'expert'), may hold values from -0.1875 to 0.1875
- out_grad: bfloat16 [4096, 4096], P('dp', 'expert'), may hold values from -6 to 6
Outputs:
- layer_out: bfloat16 [4096, 4096], P('dp', 'expert')
- tokens_grad: bfloat16 [4096, 4096], P('dp', 'expert')
- scores_grad: float32 [4096, 8], P('dp')
- w_in_grad: bfloat16 [32, 4096, 2048], P('dp', 'expert')
- w_out_grad: bfloat16 [32, 1024, 4096], P('dp', None, 'expert')
Inputs may be any that keep to these rules, and one draw needn't show every extreme that they name: `expert_ids`: the 8 experts of a token differ. Among the 128 consecutive tokens of one index of dp no expert is named by more than 40 choices, and in every draw some such block names some expert exactly 40 times.
All inputs are finite; a program needn't handle non-finite values.
Results may differ from a plain program's by a relative error of at most 0.0064.
Values may be sent and summed in bfloat16 or wider, within the bound.
No kernel may reach another device: no remote copies, remote signals or barrier semaphores. Data moves between devices by JAX's collectives and lax.ppermute only.
A program may use at most 128 MiB of HBM per device.

v0:
```python
import jax
import jax.numpy as jnp
from jax import lax
from jax.experimental import pallas as pl
from jax.sharding import PartitionSpec as P


ROUTE_SCALE = 2.5
BF = jnp.bfloat16
F32 = jnp.float32


def permute_y(v, step, n_y):
    return lax.ppermute(
        v, "expert", [(2 * y + c, 2 * ((y + step) % n_y) + c) for y in range(n_y) for c in range(2)]
    )


def permute_core(v, n_y):
    return lax.ppermute(
        v, "expert", [(2 * y + c, 2 * y + 1 - c) for y in range(n_y) for c in range(2)]
    )


def dot(a, b):
    return jnp.dot(a, b, preferred_element_type=F32)


def dot_t(a, b):
    return jnp.einsum("rd,fd->rf", a, b, preferred_element_type=F32)


def gather_dot(a, b):
    return jnp.einsum("rd,rf->df", a, b, preferred_element_type=F32)


def permute_xor(v, bit, n_y):
    return lax.ppermute(v, "expert", [(e, e ^ bit) for e in range(2 * n_y)])


def reduce_rows(product, own, part, w_own, w_part, n_y):
    rows = own.shape[0] // n_y
    far = (product(own[rows:], w_own) + product(part[rows:], w_part)).astype(BF)
    got = [permute_y(far[(d - 1) * rows : d * rows], d, n_y) for d in range(1, n_y)]
    return product(own[:rows], w_own) + product(part[:rows], w_part), got


def reduce_rows_relayed(product, own, part, w_own, w_part, core, n_y):
    rows = own.shape[0] // n_y
    far = product(own[rows:], w_own) + product(part[rows:], w_part)
    b1, b2, b3 = far[:rows], far[rows : 2 * rows], far[2 * rows :]
    relay = permute_by_core(b2.astype(BF), n_y).astype(F32)
    up = (b1 + jnp.where(core == 0, relay, 0.0)).astype(BF)
    dn = (b3 + jnp.where(core == 0, 0.0, relay)).astype(BF)
    got = [permute_y(up, 1, n_y), permute_y(dn, -1, n_y)]
    return product(own[:rows], w_own) + product(part[:rows], w_part), got


def gate_grad_kernel(near, first, second, third, factor, out):
    width = near.shape[1]
    grad = near[...] + first[...].astype(F32) + second[...].astype(F32) + third[...].astype(F32)
    out[:, :width] = (grad * factor[:, :width]).astype(BF)
    out[:, width:] = (grad * factor[:, width:]).astype(BF)


def gate_grad(near, got, factor):
    rows, width = near.shape
    tile = rows // 2
    narrow = pl.BlockSpec((tile, width), lambda i: (i, 0))
    wide = pl.BlockSpec((tile, 2 * width), lambda i: (i, 0))
    return pl.pallas_call(
        gate_grad_kernel,
        grid=(2,),
        in_specs=[narrow, narrow, narrow, narrow, wide],
        out_specs=wide,
        out_shape=jax.ShapeDtypeStruct((rows, 2 * width), BF),
    )(near, *got, factor)


def permute_by_core(v, n_y):
    return lax.ppermute(
        v,
        "expert",
        [(2 * y + c, 2 * ((y + 1 - 2 * c) % n_y) + c) for y in range(n_y) for c in range(2)],
    )


def gather_rows(v, core, n_y):
    dn = permute_y(v, 1, n_y)
    up = permute_y(v, -1, n_y)
    far = permute_by_core(jnp.where(core == 0, dn, up), n_y)
    return jnp.concatenate([v, up, far, dn], axis=0)


def relative(slab, half, y, n_y):
    rows = slab.shape[0] // (2 * n_y)
    return jnp.concatenate(
        [
            lax.dynamic_slice_in_dim(slab, (half * n_y + (y + d) % n_y) * rows, rows, 0)
            for d in range(n_y)
        ],
        axis=0,
    )


def absolute(part, y, n_y):
    rows = part.shape[0] // n_y
    return jnp.concatenate(
        [lax.dynamic_slice_in_dim(part, ((yy - y) % n_y) * rows, rows, 0) for yy in range(n_y)],
        axis=0,
    )


def both_halves(own, other, core):
    flat = jnp.where(core == 0, jnp.stack([own, other]), jnp.stack([other, own]))
    return flat.reshape(2 * own.shape[0], own.shape[1])


def body(tokens, expert_ids, scores, weight_in, weight_out, out_grad):
    n_data = lax.axis_size("dp")
    n_y = lax.axis_size("expert") // 2
    here = lax.axis_index("expert")
    y, core = lax.div(here, 2), lax.rem(here, 2)
    tok_count, width = tokens.shape
    top_count = expert_ids.shape[1]
    hidden_units = weight_out.shape[1]
    capacity = min(tok_count, 5 * tok_count * top_count // (4 * n_data))
    slots = n_data * capacity

    ids_t = expert_ids.T
    scores_t = scores.T
    named = ids_t[:, None, :] == jnp.arange(n_data, dtype=jnp.int32)[None, :, None]
    hot = jnp.sum(named.astype(F32), axis=0)
    before = (
        jnp.arange(tok_count, dtype=jnp.int32)[:, None] < jnp.arange(tok_count, dtype=jnp.int32)[None, :]
    ).astype(BF)
    rank = dot(hot.astype(BF), before)
    position = jnp.where(hot > 0.0, rank, -1.0).astype(jnp.int32)
    placed = position[:, None, :] == jnp.arange(capacity, dtype=jnp.int32)[None, :, None]
    place = placed.astype(BF).reshape(slots, tok_count)

    token_send = dot(place, tokens).astype(BF)

    def exchange(v):
        v = v.reshape(n_data, capacity, width)
        return lax.all_to_all(v, "dp", split_axis=0, concat_axis=0, tiled=True).reshape(slots, width)

    in_own, out_own = weight_in[0], weight_out[0]
    token_slab = exchange(token_send)
    in_part = permute_core(in_own, n_y)
    out_part = permute_core(out_own, n_y)

    scores_t, _ = lax.optimization_barrier((scores_t, token_send))
    score_total = jnp.sum(scores_t, axis=0, keepdims=True)
    weights_t = ROUTE_SCALE * scores_t / score_total
    weight_of = jnp.sum(jnp.where(named, weights_t[:, None, :], 0.0), axis=0)
    weight_place = jnp.where(placed, weight_of[:, None, :], 0.0).reshape(slots, tok_count)
    row_weight = jnp.sum(weight_place, axis=1, keepdims=True)
    grad_rows = dot(place, out_grad)
    grad_send = (row_weight * grad_rows).astype(BF)
    grad_send, grad_rows = lax.optimization_barrier((grad_send, grad_rows.astype(BF)))
    grad_slab = exchange(grad_send)

    tok_part = permute_core(relative(token_slab, 1 - core, y, n_y), n_y)
    tok_own = relative(token_slab, core, y, n_y)
    near, got = reduce_rows_relayed(dot, tok_own, tok_part, in_own, in_part, core, n_y)
    gate_up = near
    for piece in got:
        gate_up = gate_up + piece.astype(F32)
    gate, up = gate_up[:, :hidden_units], gate_up[:, hidden_units:]
    hidden = (gate * jax.nn.sigmoid(gate) * up).astype(BF)
    hid_parts = [permute_y(hidden, -d, n_y) for d in range(1, n_y)]
    gate, up, _ = lax.optimization_barrier((gate, up, hidden))
    sig = jax.nn.sigmoid(gate)
    factor = jnp.concatenate([up * sig * (1.0 + gate * (1.0 - sig)), gate * sig], axis=1)

    grad_slab, _ = lax.optimization_barrier((grad_slab, hidden))
    grad_part = permute_core(relative(grad_slab, 1 - core, y, n_y), n_y)
    grad_own = relative(grad_slab, core, y, n_y)
    near, got = reduce_rows(dot_t, grad_own, grad_part, out_own, out_part, n_y)
    gate_up_grad = gate_grad(near, got, factor)

    hid = jnp.concatenate([hidden] + hid_parts, axis=0)
    out_other = permute_core(absolute(dot(hid, out_part).astype(BF), y, n_y), n_y)
    out_mine = absolute(dot(hid, out_own).astype(BF), y, n_y)
    expert_out = both_halves(out_mine, out_other, core)
    out_back = exchange(expert_out)

    gug = gather_rows(gate_up_grad, core, n_y)
    grad_other = permute_core(absolute(dot_t(gug, in_part).astype(BF), y, n_y), n_y)
    grad_mine = absolute(dot_t(gug, in_own).astype(BF), y, n_y)
    choice_grad = both_halves(grad_mine, grad_other, core)
    grad_back = exchange(choice_grad)

    tok_part, tok_own, _ = lax.optimization_barrier((tok_part, tok_own, choice_grad))
    w_out_other = permute_core(gather_dot(hid, grad_part), n_y)
    w_out_grad = (gather_dot(hid, grad_own) + w_out_other).astype(BF)
    w_in_other = permute_core(gather_dot(tok_part, gug), n_y)
    w_in_grad = (gather_dot(tok_own, gug) + w_in_other).astype(BF)

    high = lax.reduce_precision(weight_place, 8, 7)
    low = (weight_place - high).astype(BF)
    high = high.astype(BF)
    layer_out = (gather_dot(high, out_back) + gather_dot(low, out_back)).astype(BF)
    slot_dot = jnp.sum(grad_rows.astype(F32) * out_back.astype(F32), axis=1)
    slot_dot = slot_dot.reshape(n_data, capacity)
    bit = 1
    while bit < 2 * n_y:
        slot_dot = slot_dot + permute_xor(slot_dot, bit, n_y)
        bit = 2 * bit
    dot_of = jnp.sum(jnp.where(placed, slot_dot[:, :, None], 0.0), axis=1)
    choice_dot = jnp.sum(jnp.where(named, dot_of[None, :, :], 0.0), axis=1)
    scores_grad = (
        ROUTE_SCALE * choice_dot - jnp.sum(choice_dot * weights_t, axis=0, keepdims=True)
    ) / score_total
    tokens_grad = gather_dot(place, grad_back).astype(BF)
    return layer_out, tokens_grad, scores_grad.T, w_in_grad[None], w_out_grad[None]


def solution(mesh):
    return jax.shard_map(
        body,
        mesh=mesh,
        in_specs=(
            P("dp", "expert"),
            P("dp", None),
            P("dp", None),
            P("dp", "expert", None),
            P("dp", None, "expert"),
            P("dp", "expert"),
        ),
        out_specs=(
            P("dp", "expert"),
            P("dp", "expert"),
            P("dp", None),
            P("dp", "expert", None),
            P("dp", None, "expert"),
        ),
        check_vma=False,
    )
```

profile of v0, /device:TPU:33, one launch (start us, length us, event | category | flops | bytes accessed | tf_op | source)
XLA Modules:
  0.0 253.3 jit_solution(4779116248976834096)
XLA Ops:
  1.9 2.5 convolution_convert_fusion
  4.4 10.8 %all-to-all-start = ((bf16[32,40,512]{2,1,0:T(8,128)(2,1)}), bf16[32,40,512]{2,1,0:T(8,128)(2,1)S(1)}, u32[]{:S(2)}, u32[]{:S(2)}) async-start(bf16[32,40,512]{2,1,0:T(8,128)(2,1)} %bitcast.71), calls=%async_computation | async-start | bytes 2621440 | tf_op jit(solution)/shard_map/all_to_all | solution.py:146
  15.2 1.3 collective-permute-start.1
  16.5 1.2 reduce_sum.73
  19.7 0.9 select_reduce_fusion
  20.6 1.4 mul.135
  22.0 26.3 %all-to-all-done = bf16[32,40,512]{2,1,0:T(8,128)(2,1)S(1)} async-done(((bf16[32,40,512]{2,1,0:T(8,128)(2,1)}), bf16[32,40,512]{2,1,0:T(8,128)(2,1)S(1)}, u32[]{:S(2)}, u32[]{:S(2)}) %all-to-all-start) | async-done | bytes 1310752 | tf_op jit(solution)/shard_map/all_to_all | solution.py:146
  48.3 0.9 constant_dynamic-slice_fusion.30
  50.1 2.0 collective-permute-start
  52.1 2.0 fusion.64
  54.1 4.8 %all-to-all-start.2 = ((bf16[32,40,512]{2,1,0:T(8,128)(2,1)}), bf16[32,40,512]{2,1,0:T(8,128)(2,1)S(1)}, u32[]{:S(2)}, u32[]{:S(2)}) async-start(bf16[32,40,512]{2,1,0:T(8,128)(2,1)} %bitcast.74), calls=%async_computation.2 | async-start | bytes 2621440 | tf_op jit(solution)/shard_map/all_to_all | solution.py:146
  59.0 2.3 fusion.25
  61.2 3.0 %convolution_add_fusion = f32[480,2048]{1,0:T(8,128)S(1)} fusion(f32[480,2048]{1,0:T(8,128)S(1)} %fusion.25, bf16[512,2048]{1,0:T(8,128)(2,1)} %collective-permute-done.1, bf16[640,512]{1,0:T(8,128)(2,1)} %collective-permute-done), kind=kOutput, calls=%fused_computation.1 | convolution fusion | flops 1007616000 | bytes 10452992 | tf_op jit(solution)/shard_map/dot_general | solution.py:26
  64.3 1.9 copy-done.2
  66.1 0.9 slice.78
  67.1 2.7 %collective-permute-start.2 = (bf16[160,2048]{1,0:T(8,128)(2,1)}, bf16[160,2048]{1,0:T(8,128)(2,1)}, u32[]{:S(2)}, u32[]{:S(2)}) collective-permute-start(bf16[160,2048]{1,0:T(8,128)(2,1)} %slice.78), channel_id=1, source_target_pairs={{0,2},{1,7},{2,4},{3,1},{4,6},{5,3},{6,0},{7,5},{8,10},{9,15},{10,... | collective-permute-start | bytes 1966088 | tf_op jit(solution)/shard_map/ppermute | solution.py:81
  69.8 7.8 %collective-permute-done.2 = bf16[160,2048]{1,0:T(8,128)(2,1)} collective-permute-done((bf16[160,2048]{1,0:T(8,128)(2,1)}, bf16[160,2048]{1,0:T(8,128)(2,1)}, u32[]{:S(2)}, u32[]{:S(2)}) %collective-permute-start.2) | collective-permute-done | bytes 655392 | tf_op jit(solution)/shard_map/ppermute | solution.py:81
  77.6 2.2 fusion.6
  80.7 2.6 %collective-permute-start.4 = (bf16[160,2048]{1,0:T(8,128)(2,1)S(1)}, bf16[160,2048]{1,0:T(8,128)(2,1)S(1)}, u32[]{:S(2)}, u32[]{:S(2)}) collective-permute-start(bf16[160,2048]{1,0:T(8,128)(2,1)S(1)} %get-tuple-element.22), channel_id=1, source_target_pairs={{0,6},{1,7},{2,0},{3,1},{4,2},{5,3},{6,4},{7,5},{8,14},{9,15},{10,... | collective-permute-start | bytes 1966088 | tf_op jit(solution)/shard_map/ppermute | solution.py:14
  83.4 2.0 collective-permute-start.8
  85.9 10.7 %collective-permute-done.3 = bf16[160,2048]{1,0:T(8,128)(2,1)S(1)} collective-permute-done((bf16[160,2048]{1,0:T(8,128)(2,1)S(1)}, bf16[160,2048]{1,0:T(8,128)(2,1)S(1)}, u32[]{:S(2)}, u32[]{:S(2)}) %collective-permute-start.3) | collective-permute-done | bytes 655392 | tf_op jit(solution)/shard_map/ppermute | solution.py:14
  96.6 2.4 fusion.3
  99.0 1.2 fusion.65
  100.2 0.9 constant_dynamic-slice_fusion.10
  101.2 0.9 pad_maximum_fusion.5
  102.0 2.4 collective-permute-start.10
  104.4 0.9 pad_maximum_fusion.7
  106.2 3.1 %collective-permute-start.6 = (bf16[160,1024]{1,0:T(8,128)(2,1)}, bf16[160,1024]{1,0:T(8,128)(2,1)}, u32[]{:S(2)}, u32[]{:S(2)}) collective-permute-start(bf16[160,1024]{1,0:T(8,128)(2,1)} %get-tuple-element.26), channel_id=1, source_target_pairs={{0,4},{1,5},{2,6},{3,7},{4,0},{5,1},{6,2},{7,3},{8,12},{9,13},{10,... | collective-permute-start | bytes 983048 | tf_op jit(solution)/shard_map/ppermute | solution.py:14
  110.0 1.9 fusion.31
  112.0 2.2 add_convert_fusion.2
  115.1 1.7 fusion.53
  117.2 1.8 collective-permute-start.12
  119.0 11.5 %collective-permute-done.13.third = bf16[160,1024]{1,0:T(8,128)(2,1)S(1)} collective-permute-done((bf16[160,1024]{1,0:T(8,128)(2,1)S(1)}, bf16[160,1024]{1,0:T(8,128)(2,1)S(1)}, u32[]{:S(2)}, u32[]{:S(2)}) %collective-permute-start.13) | collective-permute-done | bytes 327712 | tf_op jit(solution)/shard_map/ppermute | solution.py:14
  130.5 1.6 collective-permute-start.11
  132.1 1.2 pad_maximum_fusion.2.factor
  133.3 2.6 %convolution_add_fusion.2.near = f32[160,1024]{1,0:T(8,128)} fusion(f32[160,1024]{1,0:T(8,128)S(1)} %fusion.53, bf16[1024,512]{1,0:T(8,128)(2,1)} %collective-permute-done.8, bf16[640,512]{1,0:T(8,128)(2,1)S(1)} %collective-permute-done.10), kind=kOutput, calls=%fused_computation.29 | convolution fusion | flops 167936000 | bytes 2523136 | tf_op jit(solution)/shard_map/rd,fd->rf/dot_general | solution.py:30
  135.9 5.5 %collective-permute-done.11.first = bf16[160,1024]{1,0:T(8,128)(2,1)} collective-permute-done((bf16[160,1024]{1,0:T(8,128)(2,1)S(1)}, bf16[160,1024]{1,0:T(8,128)(2,1)}, u32[]{:S(2)}, u32[]{:S(2)}) %collective-permute-start.11) | collective-permute-done | bytes 327712 | tf_op jit(solution)/shard_map/ppermute | solution.py:14
  141.4 2.7 %shard_map.101 = bf16[160,2048]{1,0:T(8,128)(2,1)} custom-call(f32[160,1024]{1,0:T(8,128)} %convolution_add_fusion.2.near, bf16[160,1024]{1,0:T(8,128)(2,1)} %collective-permute-done.11.first, bf16[160,1024]{1,0:T(8,128)(2,1)} %copy-done.32, bf16[160,1024]{1,0:T(8,128)(2,1)} %copy-done.31, f32[160,2048]{1,0:T(8,128)} %pad_maximum_fusion.2.factor), custom_call_target="tpu_custom_call" | custom-call | tf_op jit(solution)/shard_map/pallas_call | solution.py:71
  144.1 2.7 %collective-permute-start.14 = (bf16[160,2048]{1,0:T(8,128)(2,1)}, bf16[160,2048]{1,0:T(8,128)(2,1)S(1)}, u32[]{:S(2)}, u32[]{:S(2)}) collective-permute-start(bf16[160,2048]{1,0:T(8,128)(2,1)} %shard_map.101), channel_id=1, source_target_pairs={{0,6},{1,7},{2,0},{3,1},{4,2},{5,3},{6,4},{7,5},{8,14},{9,15},{10,... | collective-permute-start | bytes 1966088 | tf_op jit(solution)/shard_map/ppermute | solution.py:14
  146.8 2.5 convolution_convert_fusion.3
  149.4 2.5 collective-permute-start.9
  151.9 2.5 convolution_convert_fusion.4
  154.4 5.7 %collective-permute-done.15 = bf16[160,2048]{1,0:T(8,128)(2,1)S(1)} collective-permute-done((bf16[160,2048]{1,0:T(8,128)(2,1)}, bf16[160,2048]{1,0:T(8,128)(2,1)S(1)}, u32[]{:S(2)}, u32[]{:S(2)}) %collective-permute-start.15) | collective-permute-done | bytes 655392 | tf_op jit(solution)/shard_map/ppermute | solution.py:14
  160.0 1.0 broadcast_select_fusion
  161.0 2.4 collective-permute-start.16
  163.6 1.3 maximum_select_fusion
  164.9 9.2 %all-to-all-start.1 = ((bf16[32,40,512]{2,1,0:T(8,128)(2,1)}), bf16[32,40,512]{2,1,0:T(8,128)(2,1)S(1)}, u32[]{:S(2)}, u32[]{:S(2)}) async-start(bf16[32,40,512]{2,1,0:T(8,128)(2,1)} %bitcast.75), calls=%async_computation.1 | async-start | bytes 2621440 | tf_op jit(solution)/shard_map/all_to_all | solution.py:146
  174.1 4.0 %fusion.62 = f32[1024,512]{1,0:T(8,128)} fusion(bf16[640,512]{1,0:T(8,128)(2,1)} %copy-done.16, bf16[160,1024]{1,0:T(8,128)(2,1)} %collective-permute-done.7, bf16[160,1024]{1,0:T(8,128)(2,1)} %collective-permute-done.6, bf16[160,1024]{1,0:T(8,128)(2,1)} %collective-permute-done.5, bf16[160,1024]{1,0:T(8,128)(2,1)} %get-tuple-element.26), kind=kOutput, calls=%fused_computation.142 | convolution fusion | flops 676331520 | bytes 4063232 | tf_op jit(solution)/shard_map/rd,rf->df/dot_general | solution.py:34
  178.1 1.2 collective-permute-start.22
  179.3 5.1 %fusion.63 = f32[512,2048]{1,0:T(8,128)} fusion(bf16[640,512]{1,0:T(8,128)(2,1)} %collective-permute-done, bf16[160,2048]{1,0:T(8,128)(2,1)S(1)} %copy-done.27, bf16[160,2048]{1,0:T(8,128)(2,1)} %collective-permute-done.16, bf16[160,2048]{1,0:T(8,128)(2,1)S(1)} %copy-done.30, bf16[160,2048]{1,0:T(8,128)(2,1)S(1)} %copy-done.17), kind=kOutput, calls=%fused_computation.143 | convolution fusion | flops 1352663040 | bytes 7471104 | tf_op jit(solution)/shard_map/rd,rf->df/dot_general | solution.py:34
  184.4 3.4 %convolution_convert_fusion.1 = bf16[640,512]{1,0:T(8,128)(2,1)S(1)} fusion(bf16[512,2048]{1,0:T(8,128)(2,1)} %collective-permute-done.1, bf16[160,2048]{1,0:T(8,128)(2,1)S(1)} %copy-done.27, bf16[160,2048]{1,0:T(8,128)(2,1)} %collective-permute-done.16, bf16[160,2048]{1,0:T(8,128)(2,1)S(1)} %copy-done.30, bf16[160,2048]{1,0:T(8,128)(2,1)S(1)} %copy-done.17), kind=kOutput, calls=%fused_computation.16 | convolution fusion | flops 1352990720 | bytes 5373952 | tf_op jit(solution)/shard_map/rd,fd->rf/dot_general | solution.py:30
  188.4 2.6 %convolution_convert_fusion.2 = bf16[640,512]{1,0:T(8,128)(2,1)S(1)} fusion(bf16[1,512,2048]{2,1,0:T(8,128)(2,1)S(1)} %copy-done.3, bf16[160,2048]{1,0:T(8,128)(2,1)S(1)} %copy-done.27, bf16[160,2048]{1,0:T(8,128)(2,1)} %collective-permute-done.16, bf16[160,2048]{1,0:T(8,128)(2,1)S(1)} %copy-done.30, bf16[160,2048]{1,0:T(8,128)(2,1)S(1)} %copy-done.17), kind=kOutput, calls=%fused_computation.17 | convolution fusion | flops 1352990720 | bytes 5373952 | tf_op jit(solution)/shard_map/rd,fd->rf/dot_general | solution.py:30
  191.2 1.5 collective-permute-done.17
  192.7 1.2 maximum_select_fusion.1
  193.9 13.5 %all-to-all-done.1 = bf16[32,40,512]{2,1,0:T(8,128)(2,1)S(1)} async-done(((bf16[32,40,512]{2,1,0:T(8,128)(2,1)}), bf16[32,40,512]{2,1,0:T(8,128)(2,1)S(1)}, u32[]{:S(2)}, u32[]{:S(2)}) %all-to-all-start.1) | async-done | bytes 1310752 | tf_op jit(solution)/shard_map/all_to_all | solution.py:146
  207.4 5.7 %all-to-all-start.3 = ((bf16[32,40,512]{2,1,0:T(8,128)(2,1)}), bf16[32,40,512]{2,1,0:T(8,128)(2,1)}, u32[]{:S(2)}, u32[]{:S(2)}) async-start(bf16[32,40,512]{2,1,0:T(8,128)(2,1)} %bitcast.73), calls=%async_computation.3 | async-start | bytes 2621440 | tf_op jit(solution)/shard_map/all_to_all | solution.py:146
  213.7 1.8 collective-permute-start.18
  215.5 4.0 %fusion.4 = bf16[1,1024,512]{2,1,0:T(8,128)(2,1)} fusion(f32[1024,512]{1,0:T(8,128)} %collective-permute-done.22, bf16[160,512]{1,0:T(8,128)(2,1)S(1)} %copy-done.22, bf16[160,512]{1,0:T(8,128)(2,1)S(1)} %copy-done.24, bf16[160,512]{1,0:T(8,128)(2,1)S(1)} %copy-done.20, bf16[160,512]{1,0:T(8,128)(2,1)S(1)} %copy-done.15, ...), kind=kOutput, calls=%fused_computation.15 | convolution fusion | flops 680001536 | bytes 5111808 | tf_op jit(solution)/shard_map/rd,rf->df/dot_general | solution.py:34
  220.1 2.6 %collective-permute-done.19 = f32[32,40]{1,0:T(8,128)S(1)} collective-permute-done((f32[32,40]{1,0:T(8,128)S(1)}, f32[32,40]{1,0:T(8,128)S(1)}, u32[]{:S(2)}, u32[]{:S(2)}) %collective-permute-start.19) | collective-permute-done | bytes 5152 | tf_op jit(solution)/shard_map/ppermute | solution.py:38
  222.8 1.0 fusion.11
  223.8 3.4 %collective-permute-done.20 = f32[32,40]{1,0:T(8,128)S(1)} collective-permute-done((f32[32,40]{1,0:T(8,128)S(1)}, f32[32,40]{1,0:T(8,128)S(1)}, u32[]{:S(2)}, u32[]{:S(2)}) %collective-permute-start.20) | collective-permute-done | bytes 5152 | tf_op jit(solution)/shard_map/ppermute | solution.py:38
  228.2 16.9 %all-to-all-done.3 = bf16[32,40,512]{2,1,0:T(8,128)(2,1)} async-done(((bf16[32,40,512]{2,1,0:T(8,128)(2,1)}), bf16[32,40,512]{2,1,0:T(8,128)(2,1)}, u32[]{:S(2)}, u32[]{:S(2)}) %all-to-all-start.3) | async-done | bytes 1310752 | tf_op jit(solution)/shard_map/all_to_all | solution.py:146
  245.1 2.4 fusion.10
  247.5 5.8 %fusion = bf16[1,512,2048]{2,1,0:T(8,128)(2,1)} fusion(f32[512,2048]{1,0:T(8,128)} %collective-permute-done.21, bf16[640,512]{1,0:T(8,128)(2,1)S(1)} %copy-done.25, bf16[160,2048]{1,0:T(8,128)(2,1)S(1)} %copy-done.28, bf16[160,2048]{1,0:T(8,128)(2,1)} %collective-permute-done.16, bf16[160,2048]{1,0:T(8,128)(2,1)} %copy-done.29, ...), kind=kOutput, calls=%fused_computation.3 | convolution fusion | flops 1354760192 | bytes 9568256 | tf_op jit(solution)/shard_map/rd,rf->df/dot_general | solution.py:34
  (131 shorter events, 11.4 us)
Async XLA Ops:
  0.6 51.5 %copy-start = (bf16[128,512]{1,0:T(8,128)(2,1)S(1)}, bf16[128,512]{1,0:T(8,128)(2,1)}, u32[]{:S(2)}) copy-start(bf16[128,512]{1,0:T(8,128)(2,1)} %param.11) | copy-start | bytes 393220
  1.9 2.5 copy-start.12
  4.4 10.8 %copy-start.3 = (bf16[1,512,2048]{2,1,0:T(8,128)(2,1)S(1)}, bf16[1,512,2048]{2,1,0:T(8,128)(2,1)}, u32[]{:S(2)}) copy-start(bf16[1,512,2048]{2,1,0:T(8,128)(2,1)} %param.9) | copy-start | bytes 6291460
  4.4 43.9 %all-to-all-start = ((bf16[32,40,512]{2,1,0:T(8,128)(2,1)}), bf16[32,40,512]{2,1,0:T(8,128)(2,1)S(1)}, u32[]{:S(2)}, u32[]{:S(2)}) async-start(bf16[32,40,512]{2,1,0:T(8,128)(2,1)} %bitcast.71), calls=%async_computation | async-start | bytes 2621440 | tf_op jit(solution)/shard_map/all_to_all | solution.py:146
  15.2 46.0 %collective-permute-start.1 = (bf16[512,2048]{1,0:T(8,128)(2,1)S(1)}, bf16[512,2048]{1,0:T(8,128)(2,1)}, u32[]{:S(2)}, u32[]{:S(2)}) collective-permute-start(bf16[512,2048]{1,0:T(8,128)(2,1)S(1)} %bitcast.69), channel_id=1, source_target_pairs={{0,1},{1,0},{2,3},{3,2},{4,5},{5,4},{6,7},{7,6},{8,9},{9,8},{10,11... | collective-permute-start | bytes 6291464 | tf_op jit(solution)/shard_map/ppermute | solution.py:20
  49.2 2.9 %copy-start.13 = (pred[1280,128]{1,0:T(32,128)(4,1)S(1)}, pred[1280,128]{1,0:T(32,128)(4,1)}, u32[]{:S(2)}) copy-start(pred[1280,128]{1,0:T(32,128)(4,1)} %copy-done.12) | copy-start | bytes 491524
  49.2 2.9 %copy-start.37 = (f32[1280]{0:T(1024)S(1)}, f32[1280]{0:T(1024)}, u32[]{:S(2)}) copy-start(f32[1280]{0:T(1024)} %mul.135) | copy-start | bytes 15364
  50.1 11.1 %collective-permute-start = (bf16[640,512]{1,0:T(8,128)(2,1)}, bf16[640,512]{1,0:T(8,128)(2,1)}, u32[]{:S(2)}, u32[]{:S(2)}) collective-permute-start(bf16[640,512]{1,0:T(8,128)(2,1)} %pad_maximum_fusion.3), channel_id=1, source_target_pairs={{0,1},{1,0},{2,3},{3,2},{4,5},{5,4},{6,7},{7,6},{8,9},{9,8},{10,11... | collective-permute-start | bytes 1966088 | tf_op jit(solution)/shard_map/ppermute | solution.py:20
  54.1 46.1 %all-to-all-start.2 = ((bf16[32,40,512]{2,1,0:T(8,128)(2,1)}), bf16[32,40,512]{2,1,0:T(8,128)(2,1)S(1)}, u32[]{:S(2)}, u32[]{:S(2)}) async-start(bf16[32,40,512]{2,1,0:T(8,128)(2,1)} %bitcast.74), calls=%async_computation.2 | async-start | bytes 2621440 | tf_op jit(solution)/shard_map/all_to_all | solution.py:146
  64.2 1.9 copy-start.2
  67.1 10.6 %collective-permute-start.2 = (bf16[160,2048]{1,0:T(8,128)(2,1)}, bf16[160,2048]{1,0:T(8,128)(2,1)}, u32[]{:S(2)}, u32[]{:S(2)}) collective-permute-start(bf16[160,2048]{1,0:T(8,128)(2,1)} %slice.78), channel_id=1, source_target_pairs={{0,2},{1,7},{2,4},{3,1},{4,6},{5,3},{6,0},{7,5},{8,10},{9,15},{10,... | collective-permute-start | bytes 1966088 | tf_op jit(solution)/shard_map/ppermute | solution.py:81
  69.8 15.5 %copy-start.7 = (bf16[160,512]{1,0:T(8,128)(2,1)S(1)}, bf16[160,512]{1,0:T(8,128)(2,1)}, u32[]{:S(2)}) copy-start(bf16[160,512]{1,0:T(8,128)(2,1)} %get-tuple-element.43) | copy-start | bytes 491524
  79.9 16.7 %collective-permute-start.3 = (bf16[160,2048]{1,0:T(8,128)(2,1)S(1)}, bf16[160,2048]{1,0:T(8,128)(2,1)S(1)}, u32[]{:S(2)}, u32[]{:S(2)}) collective-permute-start(bf16[160,2048]{1,0:T(8,128)(2,1)S(1)} %get-tuple-element.21), channel_id=1, source_target_pairs={{0,2},{1,3},{2,4},{3,5},{4,6},{5,7},{6,0},{7,1},{8,10},{9,11},{10,... | collective-permute-start | bytes 1966088 | tf_op jit(solution)/shard_map/ppermute | solution.py:14
  80.7 15.9 %collective-permute-start.4 = (bf16[160,2048]{1,0:T(8,128)(2,1)S(1)}, bf16[160,2048]{1,0:T(8,128)(2,1)S(1)}, u32[]{:S(2)}, u32[]{:S(2)}) collective-permute-start(bf16[160,2048]{1,0:T(8,128)(2,1)S(1)} %get-tuple-element.22), channel_id=1, source_target_pairs={{0,6},{1,7},{2,0},{3,1},{4,2},{5,3},{6,4},{7,5},{8,14},{9,15},{10,... | collective-permute-start | bytes 1966088 | tf_op jit(solution)/shard_map/ppermute | solution.py:14
  83.4 28.6 %collective-permute-start.8 = (bf16[1024,512]{1,0:T(8,128)(2,1)}, bf16[1024,512]{1,0:T(8,128)(2,1)}, u32[]{:S(2)}, u32[]{:S(2)}) collective-permute-start(bf16[1024,512]{1,0:T(8,128)(2,1)} %bitcast.6), channel_id=1, source_target_pairs={{0,1},{1,0},{2,3},{3,2},{4,5},{5,4},{6,7},{7,6},{8,9},{9,8},{10,11... | collective-permute-start | bytes 3145736 | tf_op jit(solution)/shard_map/ppermute | solution.py:20
  101.1 3.3 %copy-start.8 = (bf16[160,512]{1,0:T(8,128)(2,1)S(1)}, bf16[160,512]{1,0:T(8,128)(2,1)}, u32[]{:S(2)}) copy-start(bf16[160,512]{1,0:T(8,128)(2,1)} %get-tuple-element.43) | copy-start | bytes 491524
  101.1 3.3 %copy-start.9 = (bf16[160,512]{1,0:T(8,128)(2,1)S(1)}, bf16[160,512]{1,0:T(8,128)(2,1)}, u32[]{:S(2)}) copy-start(bf16[160,512]{1,0:T(8,128)(2,1)} %get-tuple-element.37) | copy-start | bytes 491524
  101.1 3.3 %copy-start.10 = (bf16[160,512]{1,0:T(8,128)(2,1)S(1)}, bf16[160,512]{1,0:T(8,128)(2,1)}, u32[]{:S(2)}) copy-start(bf16[160,512]{1,0:T(8,128)(2,1)} %get-tuple-element.38) | copy-start | bytes 491524
  101.1 3.3 %copy-start.11 = (bf16[160,512]{1,0:T(8,128)(2,1)S(1)}, bf16[160,512]{1,0:T(8,128)(2,1)}, u32[]{:S(2)}) copy-start(bf16[160,512]{1,0:T(8,128)(2,1)} %get-tuple-element.39) | copy-start | bytes 491524
  102.0 10.0 %collective-permute-start.10 = (bf16[640,512]{1,0:T(8,128)(2,1)}, bf16[640,512]{1,0:T(8,128)(2,1)S(1)}, u32[]{:S(2)}, u32[]{:S(2)}) collective-permute-start(bf16[640,512]{1,0:T(8,128)(2,1)} %pad_maximum_fusion.5), channel_id=1, source_target_pairs={{0,1},{1,0},{2,3},{3,2},{4,5},{5,4},{6,7},{7,6},{8,9},{9,8},{10,11... | collective-permute-start | bytes 1966088 | tf_op jit(solution)/shard_map/ppermute | solution.py:20
  104.4 5.6 %copy-start.19 = (bf16[160,512]{1,0:T(8,128)(2,1)S(1)}, bf16[160,512]{1,0:T(8,128)(2,1)}, u32[]{:S(2)}) copy-start(bf16[160,512]{1,0:T(8,128)(2,1)} %get-tuple-element.28) | copy-start | bytes 491524
  104.4 5.6 %copy-start.21 = (bf16[160,512]{1,0:T(8,128)(2,1)S(1)}, bf16[160,512]{1,0:T(8,128)(2,1)}, u32[]{:S(2)}) copy-start(bf16[160,512]{1,0:T(8,128)(2,1)} %get-tuple-element.29) | copy-start | bytes 491524
  104.4 5.6 %copy-start.23 = (bf16[160,512]{1,0:T(8,128)(2,1)S(1)}, bf16[160,512]{1,0:T(8,128)(2,1)}, u32[]{:S(2)}) copy-start(bf16[160,512]{1,0:T(8,128)(2,1)} %get-tuple-element.30) | copy-start | bytes 491524
  105.3 41.5 %collective-permute-start.7 = (bf16[160,1024]{1,0:T(8,128)(2,1)}, bf16[160,1024]{1,0:T(8,128)(2,1)}, u32[]{:S(2)}, u32[]{:S(2)}) collective-permute-start(bf16[160,1024]{1,0:T(8,128)(2,1)} %get-tuple-element.26), channel_id=1, source_target_pairs={{0,2},{1,3},{2,4},{3,5},{4,6},{5,7},{6,0},{7,1},{8,10},{9,11},{10,... | collective-permute-start | bytes 983048 | tf_op jit(solution)/shard_map/ppermute | solution.py:14
  106.2 40.6 %collective-permute-start.6 = (bf16[160,1024]{1,0:T(8,128)(2,1)}, bf16[160,1024]{1,0:T(8,128)(2,1)}, u32[]{:S(2)}, u32[]{:S(2)}) collective-permute-start(bf16[160,1024]{1,0:T(8,128)(2,1)} %get-tuple-element.26), channel_id=1, source_target_pairs={{0,4},{1,5},{2,6},{3,7},{4,0},{5,1},{6,2},{7,3},{8,12},{9,13},{10,... | collective-permute-start | bytes 983048 | tf_op jit(solution)/shard_map/ppermute | solution.py:14
  109.3 37.6 %collective-permute-start.5 = (bf16[160,1024]{1,0:T(8,128)(2,1)}, bf16[160,1024]{1,0:T(8,128)(2,1)}, u32[]{:S(2)}, u32[]{:S(2)}) collective-permute-start(bf16[160,1024]{1,0:T(8,128)(2,1)} %get-tuple-element.26), channel_id=1, source_target_pairs={{0,6},{1,7},{2,0},{3,1},{4,2},{5,3},{6,4},{7,5},{8,14},{9,15},{10,... | collective-permute-start | bytes 983048 | tf_op jit(solution)/shard_map/ppermute | solution.py:14
  112.0 21.3 %copy-start.16 = (bf16[640,512]{1,0:T(8,128)(2,1)}, bf16[640,512]{1,0:T(8,128)(2,1)S(1)}, u32[]{:S(2)}) copy-start(bf16[640,512]{1,0:T(8,128)(2,1)S(1)} %collective-permute-done.10) | copy-start | bytes 1966084
  114.3 2.5 %copy-start.5 = (f32[160,1024]{1,0:T(8,128)S(1)}, f32[160,1024]{1,0:T(8,128)}, u32[]{:S(2)}) copy-start(f32[160,1024]{1,0:T(8,128)} %get-tuple-element.16) | copy-start | bytes 1966084
  114.3 2.5 %copy-start.6 = (f32[160,1024]{1,0:T(8,128)S(1)}, f32[160,1024]{1,0:T(8,128)}, u32[]{:S(2)}) copy-start(f32[160,1024]{1,0:T(8,128)} %get-tuple-element.17) | copy-start | bytes 1966084
  114.3 16.2 %collective-permute-start.13 = (bf16[160,1024]{1,0:T(8,128)(2,1)S(1)}, bf16[160,1024]{1,0:T(8,128)(2,1)S(1)}, u32[]{:S(2)}, u32[]{:S(2)}) collective-permute-start(bf16[160,1024]{1,0:T(8,128)(2,1)S(1)} %get-tuple-element.44), channel_id=1, source_target_pairs={{0,6},{1,7},{2,0},{3,1},{4,2},{5,3},{6,4},{7,5},{8,14},{9,15},{10,... | collective-permute-start | bytes 983048 | tf_op jit(solution)/shard_map/ppermute | solution.py:14
  117.2 18.7 %collective-permute-start.12 = (bf16[160,1024]{1,0:T(8,128)(2,1)S(1)}, bf16[160,1024]{1,0:T(8,128)(2,1)S(1)}, u32[]{:S(2)}, u32[]{:S(2)}) collective-permute-start(bf16[160,1024]{1,0:T(8,128)(2,1)S(1)} %get-tuple-element.45), channel_id=1, source_target_pairs={{0,4},{1,5},{2,6},{3,7},{4,0},{5,1},{6,2},{7,3},{8,12},{9,13},{10,... | collective-permute-start | bytes 983048 | tf_op jit(solution)/shard_map/ppermute | solution.py:14
  130.5 2.7 %copy-start.31 = (bf16[160,1024]{1,0:T(8,128)(2,1)}, bf16[160,1024]{1,0:T(8,128)(2,1)S(1)}, u32[]{:S(2)}) copy-start(bf16[160,1024]{1,0:T(8,128)(2,1)S(1)} %collective-permute-done.13.third) | copy-start | bytes 983044
  130.5 10.9 %collective-permute-start.11 = (bf16[160,1024]{1,0:T(8,128)(2,1)S(1)}, bf16[160,1024]{1,0:T(8,128)(2,1)}, u32[]{:S(2)}, u32[]{:S(2)}) collective-permute-start(bf16[160,1024]{1,0:T(8,128)(2,1)S(1)} %get-tuple-element.46), channel_id=1, source_target_pairs={{0,2},{1,3},{2,4},{3,5},{4,6},{5,7},{6,0},{7,1},{8,10},{9,11},{10,... | collective-permute-start | bytes 983048 | tf_op jit(solution)/shard_map/ppermute | solution.py:14
  135.8 5.5 %copy-start.32 = (bf16[160,1024]{1,0:T(8,128)(2,1)}, bf16[160,1024]{1,0:T(8,128)(2,1)S(1)}, u32[]{:S(2)}) copy-start(bf16[160,1024]{1,0:T(8,128)(2,1)S(1)} %collective-permute-done.12.second) | copy-start | bytes 983044
  144.1 15.9 %collective-permute-start.15 = (bf16[160,2048]{1,0:T(8,128)(2,1)}, bf16[160,2048]{1,0:T(8,128)(2,1)S(1)}, u32[]{:S(2)}, u32[]{:S(2)}) collective-permute-start(bf16[160,2048]{1,0:T(8,128)(2,1)} %shard_map.101), channel_id=1, source_target_pairs={{0,2},{1,3},{2,4},{3,5},{4,6},{5,7},{6,0},{7,1},{8,10},{9,11},{10,... | collective-permute-start | bytes 1966088 | tf_op jit(solution)/shard_map/ppermute | solution.py:14
  144.1 15.9 %collective-permute-start.14 = (bf16[160,2048]{1,0:T(8,128)(2,1)}, bf16[160,2048]{1,0:T(8,128)(2,1)S(1)}, u32[]{:S(2)}, u32[]{:S(2)}) collective-permute-start(bf16[160,2048]{1,0:T(8,128)(2,1)} %shard_map.101), channel_id=1, source_target_pairs={{0,6},{1,7},{2,0},{3,1},{4,2},{5,3},{6,4},{7,5},{8,14},{9,15},{10,... | collective-permute-start | bytes 1966088 | tf_op jit(solution)/shard_map/ppermute | solution.py:14
  149.4 14.1 %collective-permute-start.9 = (bf16[640,512]{1,0:T(8,128)(2,1)S(1)}, bf16[640,512]{1,0:T(8,128)(2,1)S(1)}, u32[]{:S(2)}, u32[]{:S(2)}) collective-permute-start(bf16[640,512]{1,0:T(8,128)(2,1)S(1)} %pad_maximum_fusion.4), channel_id=1, source_target_pairs={{0,1},{1,0},{2,3},{3,2},{4,5},{5,4},{6,7},{7,6},{8,9},{9,8},{10,11... | collective-permute-start | bytes 1966088 | tf_op jit(solution)/shard_map/ppermute | solution.py:20
  160.0 3.4 %copy-start.26 = (bf16[160,2048]{1,0:T(8,128)(2,1)}, bf16[160,2048]{1,0:T(8,128)(2,1)S(1)}, u32[]{:S(2)}) copy-start(bf16[160,2048]{1,0:T(8,128)(2,1)S(1)} %collective-permute-done.15) | copy-start | bytes 1966084
  160.0 3.4 %copy-start.29 = (bf16[160,2048]{1,0:T(8,128)(2,1)}, bf16[160,2048]{1,0:T(8,128)(2,1)S(1)}, u32[]{:S(2)}) copy-start(bf16[160,2048]{1,0:T(8,128)(2,1)S(1)} %collective-permute-done.14) | copy-start | bytes 1966084
  161.0 18.2 %collective-permute-start.16 = (bf16[160,2048]{1,0:T(8,128)(2,1)}, bf16[160,2048]{1,0:T(8,128)(2,1)}, u32[]{:S(2)}, u32[]{:S(2)}) collective-permute-start(bf16[160,2048]{1,0:T(8,128)(2,1)} %broadcast_select_fusion), channel_id=1, source_target_pairs={{0,2},{1,7},{2,4},{3,1},{4,6},{5,3},{6,0},{7,5},{8,10},{9,15},{10,... | collective-permute-start | bytes 1966088 | tf_op jit(solution)/shard_map/ppermute | solution.py:81
  164.9 42.5 %all-to-all-start.1 = ((bf16[32,40,512]{2,1,0:T(8,128)(2,1)}), bf16[32,40,512]{2,1,0:T(8,128)(2,1)S(1)}, u32[]{:S(2)}, u32[]{:S(2)}) async-start(bf16[32,40,512]{2,1,0:T(8,128)(2,1)} %bitcast.75), calls=%async_computation.1 | async-start | bytes 2621440 | tf_op jit(solution)/shard_map/all_to_all | solution.py:146
  174.1 5.2 %copy-start.17 = (bf16[160,2048]{1,0:T(8,128)(2,1)S(1)}, bf16[160,2048]{1,0:T(8,128)(2,1)}, u32[]{:S(2)}) copy-start(bf16[160,2048]{1,0:T(8,128)(2,1)} %shard_map.101) | copy-start | bytes 1966084
  174.1 5.1 %copy-start.27 = (bf16[160,2048]{1,0:T(8,128)(2,1)S(1)}, bf16[160,2048]{1,0:T(8,128)(2,1)}, u32[]{:S(2)}) copy-start(bf16[160,2048]{1,0:T(8,128)(2,1)} %copy-done.26) | copy-start | bytes 1966084
  174.1 5.1 %copy-start.30 = (bf16[160,2048]{1,0:T(8,128)(2,1)S(1)}, bf16[160,2048]{1,0:T(8,128)(2,1)}, u32[]{:S(2)}) copy-start(bf16[160,2048]{1,0:T(8,128)(2,1)} %copy-done.29) | copy-start | bytes 1966084
  178.1 37.4 %collective-permute-start.22 = (f32[1024,512]{1,0:T(8,128)}, f32[1024,512]{1,0:T(8,128)}, u32[]{:S(2)}, u32[]{:S(2)}) collective-permute-start(f32[1024,512]{1,0:T(8,128)} %fusion.62), channel_id=1, source_target_pairs={{0,1},{1,0},{2,3},{3,2},{4,5},{5,4},{6,7},{7,6},{8,9},{9,8},{10,11... | collective-permute-start | bytes 6291464 | tf_op jit(solution)/shard_map/ppermute | solution.py:20
  184.4 63.1 %collective-permute-start.21 = (f32[512,2048]{1,0:T(8,128)}, f32[512,2048]{1,0:T(8,128)}, u32[]{:S(2)}, u32[]{:S(2)}) collective-permute-start(f32[512,2048]{1,0:T(8,128)} %fusion.63), channel_id=1, source_target_pairs={{0,1},{1,0},{2,3},{3,2},{4,5},{5,4},{6,7},{7,6},{8,9},{9,8},{10,11... | collective-permute-start | bytes 12582920 | tf_op jit(solution)/shard_map/ppermute | solution.py:20
  187.9 4.8 %collective-permute-start.17 = (bf16[640,512]{1,0:T(8,128)(2,1)S(1)}, bf16[640,512]{1,0:T(8,128)(2,1)S(1)}, u32[]{:S(2)}, u32[]{:S(2)}) collective-permute-start(bf16[640,512]{1,0:T(8,128)(2,1)S(1)} %pad_maximum_fusion.6), channel_id=1, source_target_pairs={{0,1},{1,0},{2,3},{3,2},{4,5},{5,4},{6,7},{7,6},{8,9},{9,8},{10,11... | collective-permute-start | bytes 1966088 | tf_op jit(solution)/shard_map/ppermute | solution.py:20
  207.4 5.7 %copy-start.4 = (bf16[1280,512]{1,0:T(8,128)(2,1)S(1)}, bf16[1280,512]{1,0:T(8,128)(2,1)}, u32[]{:S(2)}) copy-start(bf16[1280,512]{1,0:T(8,128)(2,1)} %get-tuple-element.18) | copy-start | bytes 3932164
  207.4 37.7 %all-to-all-start.3 = ((bf16[32,40,512]{2,1,0:T(8,128)(2,1)}), bf16[32,40,512]{2,1,0:T(8,128)(2,1)}, u32[]{:S(2)}, u32[]{:S(2)}) async-start(bf16[32,40,512]{2,1,0:T(8,128)(2,1)} %bitcast.73), calls=%async_computation.3 | async-start | bytes 2621440 | tf_op jit(solution)/shard_map/all_to_all | solution.py:146
  213.1 2.4 copy-start.15
  213.1 2.4 copy-start.20
  213.1 2.4 copy-start.22
  213.2 2.4 copy-start.24
  213.7 6.0 %copy-start.34 = (f32[32,128]{1,0:T(8,128)S(1)}, f32[32,128]{1,0:T(8,128)}, u32[]{:S(2)}) copy-start(f32[32,128]{1,0:T(8,128)} %copy-done.33) | copy-start | bytes 49156
  213.7 5.9 %collective-permute-start.18 = (f32[32,40]{1,0:T(8,128)S(1)}, f32[32,40]{1,0:T(8,128)S(1)}, u32[]{:S(2)}, u32[]{:S(2)}) collective-permute-start(f32[32,40]{1,0:T(8,128)S(1)} %reshape.77), channel_id=1, source_target_pairs={{0,1},{1,0},{2,3},{3,2},{4,5},{5,4},{6,7},{7,6},{8,9},{9,8},{10,11... | collective-permute-start | bytes 15368 | tf_op jit(solution)/shard_map/ppermute | solution.py:38
  219.6 3.1 %collective-permute-start.19 = (f32[32,40]{1,0:T(8,128)S(1)}, f32[32,40]{1,0:T(8,128)S(1)}, u32[]{:S(2)}, u32[]{:S(2)}) collective-permute-start(f32[32,40]{1,0:T(8,128)S(1)} %add.249), channel_id=1, source_target_pairs={{0,2},{1,3},{2,0},{3,1},{4,6},{5,7},{6,4},{7,5},{8,10},{9,11},{10,... | collective-permute-start | bytes 15368 | tf_op jit(solution)/shard_map/ppermute | solution.py:38
  220.0 7.5 %copy-start.36 = (s32[128,8]{0,1:T(8,128)S(1)}, s32[128,8]{0,1:T(8,128)}, u32[]{:S(2)}) copy-start(s32[128,8]{0,1:T(8,128)} %param.7) | copy-start | bytes 12292
  220.1 7.5 %copy-start.35 = (f32[128,8]{0,1:T(8,128)S(1)}, f32[128,8]{0,1:T(8,128)}, u32[]{:S(2)}) copy-start(f32[128,8]{0,1:T(8,128)} %param.8) | copy-start | bytes 12292
  220.1 7.5 %copy-start.38 = (f32[128]{0:T(128)S(1)}, f32[128]{0:T(128)}, u32[]{:S(2)}) copy-start(f32[128]{0:T(128)} %reduce_sum.73) | copy-start | bytes 1540
  222.6 24.9 %copy-start.18 = (bf16[160,2048]{1,0:T(8,128)(2,1)S(1)}, bf16[160,2048]{1,0:T(8,128)(2,1)}, u32[]{:S(2)}) copy-start(bf16[160,2048]{1,0:T(8,128)(2,1)} %shard_map.101) | copy-start | bytes 1966084
  222.6 24.9 %copy-start.25 = (bf16[640,512]{1,0:T(8,128)(2,1)S(1)}, bf16[640,512]{1,0:T(8,128)(2,1)}, u32[]{:S(2)}) copy-start(bf16[640,512]{1,0:T(8,128)(2,1)} %pad_maximum_fusion.7) | copy-start | bytes 1966084
  222.6 24.9 %copy-start.28 = (bf16[160,2048]{1,0:T(8,128)(2,1)S(1)}, bf16[160,2048]{1,0:T(8,128)(2,1)}, u32[]{:S(2)}) copy-start(bf16[160,2048]{1,0:T(8,128)(2,1)} %copy-done.26) | copy-start | bytes 1966084
  222.7 4.6 %collective-permute-start.20 = (f32[32,40]{1,0:T(8,128)S(1)}, f32[32,40]{1,0:T(8,128)S(1)}, u32[]{:S(2)}, u32[]{:S(2)}) collective-permute-start(f32[32,40]{1,0:T(8,128)S(1)} %add.250), channel_id=1, source_target_pairs={{0,4},{1,5},{2,6},{3,7},{4,0},{5,1},{6,2},{7,3},{8,12},{9,13},{10,... | collective-permute-start | bytes 15368 | tf_op jit(solution)/shard_map/ppermute | solution.py:38
  247.5 5.8 %copy-start.1 = (bf16[128,512]{1,0:T(8,128)(2,1)S(1)}, bf16[128,512]{1,0:T(8,128)(2,1)}, u32[]{:S(2)}) copy-start(bf16[128,512]{1,0:T(8,128)(2,1)} %param.11) | copy-start | bytes 393220
  (2 other events, 1.5 us)
where the time goes:
time: 257 us; the launch traced here: 253 us
  waiting for transfers between devices  106 us (41%)
  starting transfers between devices  63.9 us (25%)
  matrix products  54.7 us (21%)
  other arithmetic  17.1 us (7%)
  local copies, waits for them, and re-layouts  7.95 us (3%)
  Pallas kernels  2.74 us (1%)
    all_to_all x4, waiting for transfers between devices, exchange(): lax.all_to_all(v, 'dp', split_axis=0, concat_axis=0, tiled=True)  56.7 us
    ppermute x10, waiting for transfers between devices, permute_y(): lax.ppermute(v, 'expert', [(2 * y + c, 2 * ((y + step) % n_y) + c) for y...  33.5 us
    all_to_all x4, starting transfers between devices, exchange(): lax.all_to_all(v, 'dp', split_axis=0, concat_axis=0, tiled=True)  30.5 us
    dot_general x7, matrix products, gather_dot(): return jnp.einsum('rd,rf->df', a, b, preferred_element_type=F32)  22.6 us
    dot_general x9, matrix products, dot(): return jnp.dot(a, b, preferred_element_type=F32)  17.7 us
    dot_general x6, matrix products, dot_t(): return jnp.einsum('rd,fd->rf', a, b, preferred_element_type=F32)  14.4 us
    ppermute x10, starting transfers between devices, permute_y(): lax.ppermute(v, 'expert', [(2 * y + c, 2 * ((y + step) % n_y) + c) for y...  14.3 us
    ppermute x8, starting transfers between devices, permute_core(): lax.ppermute(v, 'expert', [(2 * y + c, 2 * y + 1 - c) for y in range(n_y)...  11.9 us
  transfers between devices with their start and end apart: 27, of which 11 were waited for; matrix products, arithmetic and copies ran while one was open for 26% of the time, Pallas kernels for 1%

commit v1 on v0

--- a/solution.py
+++ b/solution.py
@@ -1,7 +1,10 @@
+import functools
+
 import jax
 import jax.numpy as jnp
 from jax import lax
 from jax.experimental import pallas as pl
+from jax.experimental.pallas import tpu as pltpu
 from jax.sharding import PartitionSpec as P
 
 
@@ -38,32 +41,97 @@
     return lax.ppermute(v, "expert", [(e, e ^ bit) for e in range(2 * n_y)])
 
 
-def reduce_rows(product, own, part, w_own, w_part, n_y):
-    rows = own.shape[0] // n_y
-    far = (product(own[rows:], w_own) + product(part[rows:], w_part)).astype(BF)
-    got = [permute_y(far[(d - 1) * rows : d * rows], d, n_y) for d in range(1, n_y)]
-    return product(own[:rows], w_own) + product(part[:rows], w_part), got
-
-
-def reduce_rows_relayed(product, own, part, w_own, w_part, core, n_y):
-    rows = own.shape[0] // n_y
-    far = product(own[rows:], w_own) + product(part[rows:], w_part)
-    b1, b2, b3 = far[:rows], far[rows : 2 * rows], far[2 * rows :]
-    relay = permute_by_core(b2.astype(BF), n_y).astype(F32)
-    up = (b1 + jnp.where(core == 0, relay, 0.0)).astype(BF)
-    dn = (b3 + jnp.where(core == 0, 0.0, relay)).astype(BF)
-    got = [permute_y(up, 1, n_y), permute_y(dn, -1, n_y)]
-    return product(own[:rows], w_own) + product(part[:rows], w_part), got
-
-
-def gate_grad_kernel(near, first, second, third, factor, out):
+def partial_kernel(order, own, part, w_own, w_part, near, far1, far2, far3, *, dims, chunk):
+    step = pl.program_id(0)
+    width = near.shape[1]
+
+    def columns(j, carry):
+        cols = pl.ds(pl.multiple_of(j * chunk, chunk), chunk)
+        if dims[1] == 0:
+            a, b = w_own[:, cols], w_part[:, cols]
+        else:
+            a, b = w_own[cols, :], w_part[cols, :]
+        contract = (((1,), (dims[1],)), ((), ()))
+        total = lax.dot_general(own[...], a, contract, preferred_element_type=F32)
+        total = total + lax.dot_general(part[...], b, contract, preferred_element_type=F32)
+        for k, out in enumerate((far1, far2, far3)):
+
+            @pl.when(step == k)
+            def _(out=out):
+                out[:, cols] = total.astype(BF)
+
+        @pl.when(step == 3)
+        def _():
+            near[:, cols] = total
+
+        return carry
+
+    lax.fori_loop(0, width // chunk, columns, 0)
+
+
+def partial_products(slab, part, w_own, w_part, order, turned):
+    n_y = order.shape[0]
+    rows = part.shape[0] // n_y
+    k = slab.shape[1]
+    width = w_own.shape[0] if turned else w_own.shape[1]
+    whole = pl.BlockSpec(w_own.shape, lambda i, order: (0, 0))
+    out = pl.BlockSpec((rows, width), lambda i, order: (0, 0))
+    return pl.pallas_call(
+        functools.partial(partial_kernel, dims=(1, 1 if turned else 0), chunk=512),
+        grid_spec=pltpu.PrefetchScalarGridSpec(
+            num_scalar_prefetch=1,
+            grid=(n_y,),
+            in_specs=[
+                pl.BlockSpec((rows, k), lambda i, order: (order[i], 0)),
+                pl.BlockSpec((rows, k), lambda i, order: ((i + 1) % 4, 0)),
+                whole,
+                whole,
+            ],
+            out_specs=[out, out, out, out],
+        ),
+        out_shape=[jax.ShapeDtypeStruct((rows, width), F32)]
+        + [jax.ShapeDtypeStruct((rows, width), BF)] * 3,
+    )(order, slab, part, w_own, w_part)
+
+
+def send_far(far, n_y):
+    return [permute_y(piece, d + 1, n_y) for d, piece in enumerate(far)]
+
+
+def hidden_kernel(near, first, second, third, gate_up, hidden):
+    width = hidden.shape[1]
+    total = near[...] + first[...].astype(F32) + second[...].astype(F32) + third[...].astype(F32)
+    gate_up[...] = total
+    gate, up = total[:, :width], total[:, width:]
+    hidden[...] = (gate * jax.nn.sigmoid(gate) * up).astype(BF)
+
+
+def hidden_rows(near, got):
+    rows, width = near.shape
+    tile = rows // 2
+    wide = pl.BlockSpec((tile, width), lambda i: (i, 0))
+    return pl.pallas_call(
+        hidden_kernel,
+        grid=(2,),
+        in_specs=[wide, wide, wide, wide],
+        out_specs=[wide, pl.BlockSpec((tile, width // 2), lambda i: (i, 0))],
+        out_shape=[
+            jax.ShapeDtypeStruct((rows, width), F32),
+            jax.ShapeDtypeStruct((rows, width // 2), BF),
+        ],
+    )(near, *got)
+
+
+def gate_grad_kernel(near, first, second, third, gate_up, out):
     width = near.shape[1]
     grad = near[...] + first[...].astype(F32) + second[...].astype(F32) + third[...].astype(F32)
-    out[:, :width] = (grad * factor[:, :width]).astype(BF)
-    out[:, width:] = (grad * factor[:, width:]).astype(BF)
-
-
-def gate_grad(near, got, factor):
+    gate, up = gate_up[:, :width], gate_up[:, width:]
+    sig = jax.nn.sigmoid(gate)
+    out[:, :width] = (grad * up * sig * (1.0 + gate * (1.0 - sig))).astype(BF)
+    out[:, width:] = (grad * gate * sig).astype(BF)
+
+
+def gate_grad(near, got, gate_up):
     rows, width = near.shape
     tile = rows // 2
     narrow = pl.BlockSpec((tile, width), lambda i: (i, 0))
@@ -74,7 +142,7 @@
         in_specs=[narrow, narrow, narrow, narrow, wide],
         out_specs=wide,
         out_shape=jax.ShapeDtypeStruct((rows, 2 * width), BF),
-    )(near, *got, factor)
+    )(near, *got, gate_up)
 
 
 def permute_by_core(v, n_y):
@@ -123,7 +191,6 @@
     y, core = lax.div(here, 2), lax.rem(here, 2)
     tok_count, width = tokens.shape
     top_count = expert_ids.shape[1]
-    hidden_units = weight_out.shape[1]
     capacity = min(tok_count, 5 * tok_count * top_count // (4 * n_data))
     slots = n_data * capacity
 
@@ -161,25 +228,25 @@
     grad_send, grad_rows = lax.optimization_barrier((grad_send, grad_rows.astype(BF)))
     grad_slab = exchange(grad_send)
 
+    token_slab, _ = lax.optimization_barrier((token_slab, grad_send[:8]))
+    order = core * n_y + lax.rem(y + jnp.array([1, 2, 3, 4], jnp.int32), n_y)
     tok_part = permute_core(relative(token_slab, 1 - core, y, n_y), n_y)
-    tok_own = relative(token_slab, core, y, n_y)
-    near, got = reduce_rows_relayed(dot, tok_own, tok_part, in_own, in_part, core, n_y)
-    gate_up = near
-    for piece in got:
-        gate_up = gate_up + piece.astype(F32)
-    gate, up = gate_up[:, :hidden_units], gate_up[:, hidden_units:]
-    hidden = (gate * jax.nn.sigmoid(gate) * up).astype(BF)
+    near, *far = partial_products(token_slab, tok_part, in_own, in_part, order, False)
+    got = send_far(far, n_y)
+    gate_up, hidden = hidden_rows(near, got)
     hid_parts = [permute_y(hidden, -d, n_y) for d in range(1, n_y)]
-    gate, up, _ = lax.optimization_barrier((gate, up, hidden))
-    sig = jax.nn.sigmoid(gate)
-    factor = jnp.concatenate([up * sig * (1.0 + gate * (1.0 - sig)), gate * sig], axis=1)
 
     grad_slab, _ = lax.optimization_barrier((grad_slab, hidden))
     grad_part = permute_core(relative(grad_slab, 1 - core, y, n_y), n_y)
+    near, *far = partial_products(grad_slab, grad_part, out_own, out_part, order, True)
+    got = send_far(far, n_y)
+    gate_up_grad = gate_grad(near, got, gate_up)
+    grad_slab, _ = lax.optimization_barrier((grad_slab, gate_up_grad))
     grad_own = relative(grad_slab, core, y, n_y)
-    near, got = reduce_rows(dot_t, grad_own, grad_part, out_own, out_part, n_y)
-    gate_up_grad = gate_grad(near, got, factor)
-
+    token_slab, _ = lax.optimization_barrier((token_slab, gate_up_grad))
+    tok_own = relative(token_slab, core, y, n_y)
+
+    hid_parts, _ = lax.optimization_barrier((hid_parts, far[0]))
     hid = jnp.concatenate([hidden] + hid_parts, axis=0)
     out_other = permute_core(absolute(dot(hid, out_part).astype(BF), y, n_y), n_y)
     out_mine = absolute(dot(hid, out_own).astype(BF), y, n_y)

time: 257 us -> 265 us (1.031)
  Pallas kernels: 2.74 us -> 24.5 us
  matrix products: 54.7 us -> 35.6 us
  waiting for transfers between devices: 106 us -> 116 us
  other arithmetic: 17.1 us -> 9.63 us
  local copies, waits for them, and re-layouts: 7.95 us -> 11.5 us
    pallas_call x0 -> x3, Pallas kernels: none -> 21.7 us  [the longest x2 18.7 us: partial_products(): pl.pallas_call(functools.partial(partial_kernel, dims=(1, 1 if turned els...]
    ppermute x10 -> x11, waiting for transfers between devices: 33.5 us -> 46.7 us  [permute_y(): lax.ppermute(v, 'expert', [(2 * y + c, 2 * ((y + step) % n_y) + c) for y...]
    dot_general x9 -> x5, matrix products: 17.7 us -> 7.53 us  [dot(): return jnp.dot(a, b, preferred_element_type=F32)]
    dot_general x6 -> x2, matrix products: 14.4 us -> 6 us  [dot_t(): return jnp.einsum('rd,fd->rf', a, b, preferred_element_type=F32)]
    ppermute x2 -> x1, waiting for transfers between devices: 7.85 us -> 0.01 us  [permute_by_core(): lax.ppermute(v, 'expert', [(2 * y + c, 2 * ((y + 1 - 2 * c) % n_y) + c) f...]
    unnamed x78 -> x77, local copies, waits for them, and re-layouts: 3.36 us -> 9.28 us
    all_to_all x4, waiting for transfers between devices: 56.7 us -> 61.3 us  [exchange(): lax.all_to_all(v, 'dp', split_axis=0, concat_axis=0, tiled=True)]
    ppermute x8, starting transfers between devices: 11.9 us -> 8.59 us  [permute_core(): lax.ppermute(v, 'expert', [(2 * y + c, 2 * y + 1 - c) for y in range(n_y)...]
  transfers between devices with their start and end apart: 27 -> 27, of which waited for: 11 -> 14; matrix products, arithmetic and copies ran while one was open for 26% -> 16% of each run, Pallas kernels for 1% -> 8%
where the time goes in v1:
time: 265 us; the launch traced here: 261 us
  waiting for transfers between devices  116 us (44%)
  starting transfers between devices  62.6 us (24%)
  matrix products  35.6 us (13%)
  Pallas kernels  24.5 us (9%)
  local copies, waits for them, and re-layouts  11.5 us (4%)
  other arithmetic  9.63 us (4%)
    all_to_all x4, waiting for transfers between devices, exchange(): lax.all_to_all(v, 'dp', split_axis=0, concat_axis=0, tiled=True)  61.3 us
    ppermute x11, waiting for transfers between devices, permute_y(): lax.ppermute(v, 'expert', [(2 * y + c, 2 * ((y + step) % n_y) + c) for y...  46.7 us
    all_to_all x4, starting transfers between devices, exchange(): lax.all_to_all(v, 'dp', split_axis=0, concat_axis=0, tiled=True)  31.5 us
    dot_general x7, matrix products, gather_dot(): return jnp.einsum('rd,rf->df', a, b, preferred_element_type=F32)  22.1 us
    pallas_call x2, Pallas kernels, partial_products(): pl.pallas_call(functools.partial(partial_kernel, dims=(1, 1 if turned els...  18.7 us
    ppermute x11, starting transfers between devices, permute_y(): lax.ppermute(v, 'expert', [(2 * y + c, 2 * ((y + step) % n_y) + c) for y...  17 us
    unnamed x77, local copies, waits for them, and re-layouts  9.28 us
    ppermute x8, starting transfers between devices, permute_core(): lax.ppermute(v, 'expert', [(2 * y + c, 2 * y + 1 - c) for y in range(n_y)...  8.59 us
  transfers between devices with their start and end apart: 27, of which 14 were waited for; matrix products, arithmetic and copies ran while one was open for 16% of the time, Pallas kernels for 8%

profile of v1, /device:TPU:33, one launch (start us, length us, event | category | flops | bytes accessed | tf_op | source)
XLA Modules:
  0.0 261.1 jit_solution(12433736322269955715)
XLA Ops:
  1.9 2.5 convolution_convert_fusion
  4.3 10.8 %all-to-all-start = ((bf16[32,40,512]{2,1,0:T(8,128)(2,1)}), bf16[32,40,512]{2,1,0:T(8,128)(2,1)S(1)}, u32[]{:S(2)}, u32[]{:S(2)}) async-start(bf16[32,40,512]{2,1,0:T(8,128)(2,1)} %bitcast.3), calls=%async_computation | async-start | bytes 2621440 | tf_op jit(solution)/shard_map/all_to_all | solution.py:213
  15.1 1.3 collective-permute-start.1
  17.4 1.9 fusion.34
  19.4 28.9 %all-to-all-done = bf16[32,40,512]{2,1,0:T(8,128)(2,1)S(1)} async-done(((bf16[32,40,512]{2,1,0:T(8,128)(2,1)}), bf16[32,40,512]{2,1,0:T(8,128)(2,1)S(1)}, u32[]{:S(2)}, u32[]{:S(2)}) %all-to-all-start) | async-done | bytes 1310752 | tf_op jit(solution)/shard_map/all_to_all | solution.py:213
  48.2 5.7 %all-to-all-start.1 = ((bf16[32,40,512]{2,1,0:T(8,128)(2,1)}), bf16[32,40,512]{2,1,0:T(8,128)(2,1)S(1)}, u32[]{:S(2)}, u32[]{:S(2)}) async-start(bf16[32,40,512]{2,1,0:T(8,128)(2,1)} %bitcast.65), calls=%async_computation.1 | async-start | bytes 2621440 | tf_op jit(solution)/shard_map/all_to_all | solution.py:213
  54.1 0.9 pad_maximum_fusion.1
  55.0 1.7 collective-permute-start
  57.3 1.4 collective-permute-done.part
  58.7 0.8 copy-done.11
  59.5 10.9 %shard_map.110 = (f32[160,2048]{1,0:T(8,128)}, bf16[160,2048]{1,0:T(8,128)(2,1)}, bf16[160,2048]{1,0:T(8,128)(2,1)}, bf16[160,2048]{1,0:T(8,128)(2,1)}) custom-call(s32[4]{0:T(128)} %fusion.27.order, bf16[1280,512]{1,0:T(8,128)(2,1)} %bitcast.63, bf16[640,512]{1,0:T(8,128)(2,1)} %copy-done.11, bf16[512,2048]{1,0:T(8,128)(2,1)} %bitcast.68, ...), custom_call_target="tpu_custom_call" | custom-call | tf_op jit(solution)/shard_map/pallas_call | solution.py:79
  70.4 1.3 collective-permute-start.2
  71.7 2.6 %collective-permute-start.3 = (bf16[160,2048]{1,0:T(8,128)(2,1)}, bf16[160,2048]{1,0:T(8,128)(2,1)}, u32[]{:S(2)}, u32[]{:S(2)}) collective-permute-start(bf16[160,2048]{1,0:T(8,128)(2,1)} %get-tuple-element.29), channel_id=1, source_target_pairs={{0,4},{1,5},{2,6},{3,7},{4,0},{5,1},{6,2},{7,3},{8,12},{9,13},{10,... | collective-permute-start | bytes 1966088 | tf_op jit(solution)/shard_map/ppermute | solution.py:17
  74.3 1.1 collective-permute-start.4
  75.4 1.2 collective-permute-start.9
  76.6 11.4 %collective-permute-done.2.first = bf16[160,2048]{1,0:T(8,128)(2,1)} collective-permute-done((bf16[160,2048]{1,0:T(8,128)(2,1)}, bf16[160,2048]{1,0:T(8,128)(2,1)}, u32[]{:S(2)}, u32[]{:S(2)}) %collective-permute-start.2) | collective-permute-done | bytes 655392 | tf_op jit(solution)/shard_map/ppermute | solution.py:17
  88.0 15.2 %collective-permute-done.3.second = bf16[160,2048]{1,0:T(8,128)(2,1)} collective-permute-done((bf16[160,2048]{1,0:T(8,128)(2,1)}, bf16[160,2048]{1,0:T(8,128)(2,1)}, u32[]{:S(2)}, u32[]{:S(2)}) %collective-permute-start.3) | collective-permute-done | bytes 655392 | tf_op jit(solution)/shard_map/ppermute | solution.py:17
  103.2 2.9 %shard_map.111 = (f32[160,2048]{1,0:T(8,128)}, bf16[160,1024]{1,0:T(8,128)(2,1)}) custom-call(f32[160,2048]{1,0:T(8,128)} %get-tuple-element.27.near, bf16[160,2048]{1,0:T(8,128)(2,1)} %collective-permute-done.2.first, bf16[160,2048]{1,0:T(8,128)(2,1)} %collective-permute-done.3.second, bf16[160,2048]{1,0:T(8,128)(2,1)} %collective-permute-done.4.third), custom_call_target="tpu_custom_call" | custom-call | tf_op jit(solution)/shard_map/pallas_call | solution.py:113
  106.2 1.0 pad_maximum_fusion.2
  107.4 1.2 collective-permute-start.8
  108.6 0.9 collective-permute-start.7
  109.5 2.1 collective-permute-start.6
  111.6 1.4 collective-permute-start.5
  113.0 1.8 constant_dynamic-update-slice_fusion.3
  114.7 1.0 copy-done.9
  115.7 7.8 %shard_map.112 = (f32[160,1024]{1,0:T(8,128)}, bf16[160,1024]{1,0:T(8,128)(2,1)}, bf16[160,1024]{1,0:T(8,128)(2,1)}, bf16[160,1024]{1,0:T(8,128)(2,1)}) custom-call(s32[4]{0:T(128)} %fusion.27.order, bf16[1280,512]{1,0:T(8,128)(2,1)} %bitcast.60, bf16[640,512]{1,0:T(8,128)(2,1)} %collective-permute-done.8.part, bf16[1024,512]{1,0:T(8,128)(2,1)} %bitcast.69, ...), custom_call_target="tpu_custom_call" | custom-call | tf_op jit(solution)/shard_map/pallas_call | solution.py:79
  123.6 3.0 %collective-permute-done.6 = bf16[160,1024]{1,0:T(8,128)(2,1)S(1)} collective-permute-done((bf16[160,1024]{1,0:T(8,128)(2,1)}, bf16[160,1024]{1,0:T(8,128)(2,1)S(1)}, u32[]{:S(2)}, u32[]{:S(2)}) %collective-permute-start.6) | collective-permute-done | bytes 327712 | tf_op jit(solution)/shard_map/ppermute | solution.py:17
  127.4 2.3 collective-permute-start.12
  129.7 2.0 collective-permute-start.13
  131.6 1.7 constant_dynamic-update-slice_fusion.2
  133.4 0.8 constant_dynamic-update-slice_fusion.1
  134.9 2.2 convolution_convert_fusion.3
  137.1 3.6 %collective-permute-done.12.second = bf16[160,1024]{1,0:T(8,128)(2,1)S(1)} collective-permute-done((bf16[160,1024]{1,0:T(8,128)(2,1)}, bf16[160,1024]{1,0:T(8,128)(2,1)S(1)}, u32[]{:S(2)}, u32[]{:S(2)}) %collective-permute-start.12) | collective-permute-done | bytes 327712 | tf_op jit(solution)/shard_map/ppermute | solution.py:17
  140.7 4.8 %collective-permute-done.13.third = bf16[160,1024]{1,0:T(8,128)(2,1)S(1)} collective-permute-done((bf16[160,1024]{1,0:T(8,128)(2,1)}, bf16[160,1024]{1,0:T(8,128)(2,1)S(1)}, u32[]{:S(2)}, u32[]{:S(2)}) %collective-permute-start.13) | collective-permute-done | bytes 327712 | tf_op jit(solution)/shard_map/ppermute | solution.py:17
  146.4 2.8 %shard_map.113 = bf16[160,2048]{1,0:T(8,128)(2,1)} custom-call(f32[160,1024]{1,0:T(8,128)} %get-tuple-element.38.near, bf16[160,1024]{1,0:T(8,128)(2,1)} %copy-done.19, bf16[160,1024]{1,0:T(8,128)(2,1)} %copy-done.20, bf16[160,1024]{1,0:T(8,128)(2,1)} %copy-done.21, f32[160,2048]{1,0:T(8,128)} %get-tuple-element.41.gate_up), custom_call_target="tpu_custom_call" | custom-call | tf_op jit(solution)/shard_map/pallas_call | solution.py:139
  149.2 2.1 collective-permute-start.15
  151.3 1.2 collective-permute-start.14
  152.6 1.4 collective-permute-start.10
  153.9 3.4 %fusion.35 = f32[1024,512]{1,0:T(8,128)} fusion(bf16[640,1024]{1,0:T(8,128)(2,1)S(1)} %copy-done.29, bf16[640,512]{1,0:T(8,128)(2,1)} %collective-permute-done.8.part), kind=kOutput, calls=%fused_computation.109 | convolution fusion | flops 671088640 | bytes 4063232 | tf_op jit(solution)/shard_map/rd,rf->df/dot_general | solution.py:37
  157.5 0.8 convolution_convert_fusion.4
  158.3 8.3 %collective-permute-done.15 = bf16[160,2048]{1,0:T(8,128)(2,1)S(1)} collective-permute-done((bf16[160,2048]{1,0:T(8,128)(2,1)}, bf16[160,2048]{1,0:T(8,128)(2,1)S(1)}, u32[]{:S(2)}, u32[]{:S(2)}) %collective-permute-start.15) | collective-permute-done | bytes 655392 | tf_op jit(solution)/shard_map/ppermute | solution.py:17
  167.0 1.0 broadcast_select_fusion
  168.0 2.2 collective-permute-start.16
  170.4 0.9 pad_maximum_fusion.5
  171.3 1.3 maximum_select_fusion
  172.5 9.4 %all-to-all-start.2 = ((bf16[32,40,512]{2,1,0:T(8,128)(2,1)}), bf16[32,40,512]{2,1,0:T(8,128)(2,1)S(1)}, u32[]{:S(2)}, u32[]{:S(2)}) async-start(bf16[32,40,512]{2,1,0:T(8,128)(2,1)} %bitcast.11), calls=%async_computation.2 | async-start | bytes 2621440 | tf_op jit(solution)/shard_map/all_to_all | solution.py:213
  181.9 5.2 %fusion.33 = f32[512,2048]{1,0:T(8,128)} fusion(bf16[640,512]{1,0:T(8,128)(2,1)S(1)} %copy-done.12, bf16[160,2048]{1,0:T(8,128)(2,1)S(1)} %collective-permute-done.15, bf16[160,2048]{1,0:T(8,128)(2,1)} %collective-permute-done.16, bf16[160,2048]{1,0:T(8,128)(2,1)} %copy-done.16, bf16[160,2048]{1,0:T(8,128)(2,1)S(1)} %copy-done.13), kind=kOutput, calls=%fused_computation.107 | convolution fusion | flops 1352663040 | bytes 7471104 | tf_op jit(solution)/shard_map/rd,rf->df/dot_general | solution.py:37
  187.1 1.2 collective-permute-start.21
  188.3 3.4 %convolution_convert_fusion.1 = bf16[640,512]{1,0:T(8,128)(2,1)S(1)} fusion(bf16[512,2048]{1,0:T(8,128)(2,1)} %collective-permute-done.1.w_part, bf16[160,2048]{1,0:T(8,128)(2,1)S(1)} %collective-permute-done.15, bf16[160,2048]{1,0:T(8,128)(2,1)} %collective-permute-done.16, bf16[160,2048]{1,0:T(8,128)(2,1)S(1)} %copy-done.17, ...), kind=kOutput, calls=%fused_computation.9 | convolution fusion | flops 1352990720 | bytes 5373952 | tf_op jit(solution)/shard_map/rd,fd->rf/dot_general | solution.py:33
  191.7 2.6 %convolution_convert_fusion.2 = bf16[640,512]{1,0:T(8,128)(2,1)S(1)} fusion(bf16[1,512,2048]{2,1,0:T(8,128)(2,1)S(1)} %copy-done.6, bf16[160,2048]{1,0:T(8,128)(2,1)S(1)} %collective-permute-done.15, bf16[160,2048]{1,0:T(8,128)(2,1)} %collective-permute-done.16, bf16[160,2048]{1,0:T(8,128)(2,1)S(1)} %copy-done.17, bf16[160,2048]{1,0:T(8,128)(2,1)S(1)} %copy-done.13), kind=kOutput, calls=%fused_computation.10 | convolution fusion | flops 1352990720 | bytes 5373952 | tf_op jit(solution)/shard_map/rd,fd->rf/dot_general | solution.py:33
  195.0 1.9 collective-permute-done.17
  196.9 1.2 maximum_select_fusion.1
  198.2 17.0 %all-to-all-done.2 = bf16[32,40,512]{2,1,0:T(8,128)(2,1)S(1)} async-done(((bf16[32,40,512]{2,1,0:T(8,128)(2,1)}), bf16[32,40,512]{2,1,0:T(8,128)(2,1)S(1)}, u32[]{:S(2)}, u32[]{:S(2)}) %all-to-all-start.2) | async-done | bytes 1310752 | tf_op jit(solution)/shard_map/all_to_all | solution.py:213
  215.2 5.7 %all-to-all-start.3 = ((bf16[32,40,512]{2,1,0:T(8,128)(2,1)}), bf16[32,40,512]{2,1,0:T(8,128)(2,1)}, u32[]{:S(2)}, u32[]{:S(2)}) async-start(bf16[32,40,512]{2,1,0:T(8,128)(2,1)} %bitcast.66), calls=%async_computation.3 | async-start | bytes 2621440 | tf_op jit(solution)/shard_map/all_to_all | solution.py:213
  220.9 0.8 constant_dynamic-slice_fusion.3
  223.0 1.8 collective-permute-start.18
  224.9 4.0 %fusion.2 = bf16[1,1024,512]{2,1,0:T(8,128)(2,1)} fusion(f32[1024,512]{1,0:T(8,128)} %collective-permute-done.22, bf16[640,1024]{1,0:T(8,128)(2,1)} %constant_dynamic-update-slice_fusion, bf16[160,512]{1,0:T(8,128)(2,1)S(1)} %copy-done.24, bf16[160,512]{1,0:T(8,128)(2,1)S(1)} %copy-done.25, bf16[160,512]{1,0:T(8,128)(2,1)S(1)} %copy-done.26, ...), kind=kOutput, calls=%fused_computation.8 | convolution fusion | flops 674758656 | bytes 5111808 | tf_op jit(solution)/shard_map/rd,rf->df/dot_general | solution.py:37
  229.4 2.6 collective-permute-done.19
  232.0 1.4 collective-permute-start.20
  233.4 1.0 fusion.5
  234.4 2.1 collective-permute-done.20
  237.5 15.4 %all-to-all-done.3 = bf16[32,40,512]{2,1,0:T(8,128)(2,1)} async-done(((bf16[32,40,512]{2,1,0:T(8,128)(2,1)}), bf16[32,40,512]{2,1,0:T(8,128)(2,1)}, u32[]{:S(2)}, u32[]{:S(2)}) %all-to-all-start.3) | async-done | bytes 1310752 | tf_op jit(solution)/shard_map/all_to_all | solution.py:213
  252.9 2.4 fusion.4
  255.3 5.8 %fusion = bf16[1,512,2048]{2,1,0:T(8,128)(2,1)} fusion(f32[512,2048]{1,0:T(8,128)} %collective-permute-done.21, bf16[640,512]{1,0:T(8,128)(2,1)} %pad_maximum_fusion.5, bf16[160,2048]{1,0:T(8,128)(2,1)S(1)} %copy-done.15, bf16[160,2048]{1,0:T(8,128)(2,1)} %collective-permute-done.16, bf16[160,2048]{1,0:T(8,128)(2,1)S(1)} %copy-done.18, ...), kind=kOutput, calls=%fused_computation.2 | convolution fusion | flops 1354760192 | bytes 9568256 | tf_op jit(solution)/shard_map/rd,rf->df/dot_general | solution.py:37
  (122 shorter events, 9.6 us)
Async XLA Ops:
  0.6 16.8 %copy-start = (bf16[128,512]{1,0:T(8,128)(2,1)S(1)}, bf16[128,512]{1,0:T(8,128)(2,1)}, u32[]{:S(2)}) copy-start(bf16[128,512]{1,0:T(8,128)(2,1)} %param.12) | copy-start | bytes 393220
  4.3 12.1 %copy-start.30 = (f32[128,8]{0,1:T(8,128)S(1)}, f32[128,8]{0,1:T(8,128)}, u32[]{:S(2)}) copy-start(f32[128,8]{0,1:T(8,128)} %param.9) | copy-start | bytes 12292
  4.3 12.7 %copy-start.32 = (s32[128,8]{0,1:T(8,128)S(1)}, s32[128,8]{0,1:T(8,128)}, u32[]{:S(2)}) copy-start(s32[128,8]{0,1:T(8,128)} %param.8) | copy-start | bytes 12292
  4.3 43.9 %all-to-all-start = ((bf16[32,40,512]{2,1,0:T(8,128)(2,1)}), bf16[32,40,512]{2,1,0:T(8,128)(2,1)S(1)}, u32[]{:S(2)}, u32[]{:S(2)}) async-start(bf16[32,40,512]{2,1,0:T(8,128)(2,1)} %bitcast.3), calls=%async_computation | async-start | bytes 2621440 | tf_op jit(solution)/shard_map/all_to_all | solution.py:213
  15.1 42.2 %collective-permute-start.1 = (bf16[512,2048]{1,0:T(8,128)(2,1)}, bf16[512,2048]{1,0:T(8,128)(2,1)}, u32[]{:S(2)}, u32[]{:S(2)}) collective-permute-start(bf16[512,2048]{1,0:T(8,128)(2,1)} %bitcast.67), channel_id=1, source_target_pairs={{0,1},{1,0},{2,3},{3,2},{4,5},{5,4},{6,7},{7,6},{8,9},{9,8},{10,11... | collective-permute-start | bytes 6291464 | tf_op jit(solution)/shard_map/ppermute | solution.py:23
  16.4 0.6 copy-start.34
  17.0 2.3 copy-start.27
  48.2 5.8 %copy-start.3 = (bf16[32,40,512]{2,1,0:T(8,128)(2,1)}, bf16[32,40,512]{2,1,0:T(8,128)(2,1)S(1)}, u32[]{:S(2)}) copy-start(bf16[32,40,512]{2,1,0:T(8,128)(2,1)S(1)} %all-to-all-done) | copy-start | bytes 3932164
  48.2 57.8 %all-to-all-start.1 = ((bf16[32,40,512]{2,1,0:T(8,128)(2,1)}), bf16[32,40,512]{2,1,0:T(8,128)(2,1)S(1)}, u32[]{:S(2)}, u32[]{:S(2)}) async-start(bf16[32,40,512]{2,1,0:T(8,128)(2,1)} %bitcast.65), calls=%async_computation.1 | async-start | bytes 2621440 | tf_op jit(solution)/shard_map/all_to_all | solution.py:213
  54.1 2.7 %copy-start.36 = (s32[4]{0:T(128)S(1)}, s32[4]{0:T(128)}, u32[]{:S(2)}) copy-start(s32[4]{0:T(128)} %constant.121.clone) | copy-start | bytes 52
  55.0 3.6 %collective-permute-start = (bf16[640,512]{1,0:T(8,128)(2,1)}, bf16[640,512]{1,0:T(8,128)(2,1)S(1)}, u32[]{:S(2)}, u32[]{:S(2)}) collective-permute-start(bf16[640,512]{1,0:T(8,128)(2,1)} %pad_maximum_fusion.1), channel_id=1, source_target_pairs={{0,1},{1,0},{2,3},{3,2},{4,5},{5,4},{6,7},{7,6},{8,9},{9,8},{10,11... | collective-permute-start | bytes 1966088 | tf_op jit(solution)/shard_map/ppermute | solution.py:23
  57.3 18.1 %copy-start.7 = (bf16[1,1024,512]{2,1,0:T(8,128)(2,1)S(1)}, bf16[1,1024,512]{2,1,0:T(8,128)(2,1)}, u32[]{:S(2)}) copy-start(bf16[1,1024,512]{2,1,0:T(8,128)(2,1)} %param.11) | copy-start | bytes 3145732
  58.7 0.9 copy-start.11
  70.4 17.6 %collective-permute-start.2 = (bf16[160,2048]{1,0:T(8,128)(2,1)}, bf16[160,2048]{1,0:T(8,128)(2,1)}, u32[]{:S(2)}, u32[]{:S(2)}) collective-permute-start(bf16[160,2048]{1,0:T(8,128)(2,1)} %get-tuple-element.28), channel_id=1, source_target_pairs={{0,2},{1,3},{2,4},{3,5},{4,6},{5,7},{6,0},{7,1},{8,10},{9,11},{10,... | collective-permute-start | bytes 1966088 | tf_op jit(solution)/shard_map/ppermute | solution.py:17
  71.7 31.4 %collective-permute-start.3 = (bf16[160,2048]{1,0:T(8,128)(2,1)}, bf16[160,2048]{1,0:T(8,128)(2,1)}, u32[]{:S(2)}, u32[]{:S(2)}) collective-permute-start(bf16[160,2048]{1,0:T(8,128)(2,1)} %get-tuple-element.29), channel_id=1, source_target_pairs={{0,4},{1,5},{2,6},{3,7},{4,0},{5,1},{6,2},{7,3},{8,12},{9,13},{10,... | collective-permute-start | bytes 1966088 | tf_op jit(solution)/shard_map/ppermute | solution.py:17
  74.3 28.8 %collective-permute-start.4 = (bf16[160,2048]{1,0:T(8,128)(2,1)}, bf16[160,2048]{1,0:T(8,128)(2,1)}, u32[]{:S(2)}, u32[]{:S(2)}) collective-permute-start(bf16[160,2048]{1,0:T(8,128)(2,1)} %get-tuple-element.30), channel_id=1, source_target_pairs={{0,6},{1,7},{2,0},{3,1},{4,2},{5,3},{6,4},{7,5},{8,14},{9,15},{10,... | collective-permute-start | bytes 1966088 | tf_op jit(solution)/shard_map/ppermute | solution.py:17
  75.4 39.3 %collective-permute-start.9 = (bf16[1024,512]{1,0:T(8,128)(2,1)S(1)}, bf16[1024,512]{1,0:T(8,128)(2,1)S(1)}, u32[]{:S(2)}, u32[]{:S(2)}) collective-permute-start(bf16[1024,512]{1,0:T(8,128)(2,1)S(1)} %bitcast.70), channel_id=1, source_target_pairs={{0,1},{1,0},{2,3},{3,2},{4,5},{5,4},{6,7},{7,6},{8,9},{9,8},{10,11... | collective-permute-start | bytes 3145736 | tf_op jit(solution)/shard_map/ppermute | solution.py:23
  106.1 1.3 copy-start.1
  107.4 7.4 %collective-permute-start.8 = (bf16[640,512]{1,0:T(8,128)(2,1)}, bf16[640,512]{1,0:T(8,128)(2,1)}, u32[]{:S(2)}, u32[]{:S(2)}) collective-permute-start(bf16[640,512]{1,0:T(8,128)(2,1)} %pad_maximum_fusion.2), channel_id=1, source_target_pairs={{0,1},{1,0},{2,3},{3,2},{4,5},{5,4},{6,7},{7,6},{8,9},{9,8},{10,11... | collective-permute-start | bytes 1966088 | tf_op jit(solution)/shard_map/ppermute | solution.py:23
  108.6 15.0 %collective-permute-start.7 = (bf16[160,1024]{1,0:T(8,128)(2,1)}, bf16[160,1024]{1,0:T(8,128)(2,1)S(1)}, u32[]{:S(2)}, u32[]{:S(2)}) collective-permute-start(bf16[160,1024]{1,0:T(8,128)(2,1)} %get-tuple-element.31), channel_id=1, source_target_pairs={{0,2},{1,3},{2,4},{3,5},{4,6},{5,7},{6,0},{7,1},{8,10},{9,11},{10,... | collective-permute-start | bytes 983048 | tf_op jit(solution)/shard_map/ppermute | solution.py:17
  109.5 17.1 %collective-permute-start.6 = (bf16[160,1024]{1,0:T(8,128)(2,1)}, bf16[160,1024]{1,0:T(8,128)(2,1)S(1)}, u32[]{:S(2)}, u32[]{:S(2)}) collective-permute-start(bf16[160,1024]{1,0:T(8,128)(2,1)} %get-tuple-element.31), channel_id=1, source_target_pairs={{0,4},{1,5},{2,6},{3,7},{4,0},{5,1},{6,2},{7,3},{8,12},{9,13},{10,... | collective-permute-start | bytes 983048 | tf_op jit(solution)/shard_map/ppermute | solution.py:17
  111.6 15.1 %collective-permute-start.5 = (bf16[160,1024]{1,0:T(8,128)(2,1)}, bf16[160,1024]{1,0:T(8,128)(2,1)S(1)}, u32[]{:S(2)}, u32[]{:S(2)}) collective-permute-start(bf16[160,1024]{1,0:T(8,128)(2,1)} %get-tuple-element.31), channel_id=1, source_target_pairs={{0,6},{1,7},{2,0},{3,1},{4,2},{5,3},{6,4},{7,5},{8,14},{9,15},{10,... | collective-permute-start | bytes 983048 | tf_op jit(solution)/shard_map/ppermute | solution.py:17
  114.7 1.0 copy-start.9
  123.5 11.4 %copy-start.10 = (bf16[1024,512]{1,0:T(8,128)(2,1)S(1)}, bf16[1024,512]{1,0:T(8,128)(2,1)}, u32[]{:S(2)}) copy-start(bf16[1024,512]{1,0:T(8,128)(2,1)} %copy-done.9) | copy-start | bytes 3145732
  123.5 22.0 %collective-permute-start.11 = (bf16[160,1024]{1,0:T(8,128)(2,1)}, bf16[160,1024]{1,0:T(8,128)(2,1)S(1)}, u32[]{:S(2)}, u32[]{:S(2)}) collective-permute-start(bf16[160,1024]{1,0:T(8,128)(2,1)} %get-tuple-element.34), channel_id=1, source_target_pairs={{0,2},{1,3},{2,4},{3,5},{4,6},{5,7},{6,0},{7,1},{8,10},{9,11},{10,... | collective-permute-start | bytes 983048 | tf_op jit(solution)/shard_map/ppermute | solution.py:17
  126.7 0.7 copy-start.22
  127.4 13.3 %collective-permute-start.12 = (bf16[160,1024]{1,0:T(8,128)(2,1)}, bf16[160,1024]{1,0:T(8,128)(2,1)S(1)}, u32[]{:S(2)}, u32[]{:S(2)}) collective-permute-start(bf16[160,1024]{1,0:T(8,128)(2,1)} %get-tuple-element.39), channel_id=1, source_target_pairs={{0,4},{1,5},{2,6},{3,7},{4,0},{5,1},{6,2},{7,3},{8,12},{9,13},{10,... | collective-permute-start | bytes 983048 | tf_op jit(solution)/shard_map/ppermute | solution.py:17
  129.7 15.9 %collective-permute-start.13 = (bf16[160,1024]{1,0:T(8,128)(2,1)}, bf16[160,1024]{1,0:T(8,128)(2,1)S(1)}, u32[]{:S(2)}, u32[]{:S(2)}) collective-permute-start(bf16[160,1024]{1,0:T(8,128)(2,1)} %get-tuple-element.40), channel_id=1, source_target_pairs={{0,6},{1,7},{2,0},{3,1},{4,2},{5,3},{6,4},{7,5},{8,14},{9,15},{10,... | collective-permute-start | bytes 983048 | tf_op jit(solution)/shard_map/ppermute | solution.py:17
  140.7 4.9 %copy-start.20 = (bf16[160,1024]{1,0:T(8,128)(2,1)}, bf16[160,1024]{1,0:T(8,128)(2,1)S(1)}, u32[]{:S(2)}) copy-start(bf16[160,1024]{1,0:T(8,128)(2,1)S(1)} %collective-permute-done.12.second) | copy-start | bytes 983044
  145.5 0.7 copy-start.21
  145.6 0.9 copy-start.19
  149.2 4.7 %copy-start.29 = (bf16[640,1024]{1,0:T(8,128)(2,1)S(1)}, bf16[640,1024]{1,0:T(8,128)(2,1)}, u32[]{:S(2)}) copy-start(bf16[640,1024]{1,0:T(8,128)(2,1)} %constant_dynamic-update-slice_fusion) | copy-start | bytes 3932164
  149.2 17.4 %collective-permute-start.15 = (bf16[160,2048]{1,0:T(8,128)(2,1)}, bf16[160,2048]{1,0:T(8,128)(2,1)S(1)}, u32[]{:S(2)}, u32[]{:S(2)}) collective-permute-start(bf16[160,2048]{1,0:T(8,128)(2,1)} %shard_map.113), channel_id=1, source_target_pairs={{0,2},{1,3},{2,4},{3,5},{4,6},{5,7},{6,0},{7,1},{8,10},{9,11},{10,... | collective-permute-start | bytes 1966088 | tf_op jit(solution)/shard_map/ppermute | solution.py:17
  151.3 15.7 %collective-permute-start.14 = (bf16[160,2048]{1,0:T(8,128)(2,1)}, bf16[160,2048]{1,0:T(8,128)(2,1)S(1)}, u32[]{:S(2)}, u32[]{:S(2)}) collective-permute-start(bf16[160,2048]{1,0:T(8,128)(2,1)} %shard_map.113), channel_id=1, source_target_pairs={{0,6},{1,7},{2,0},{3,1},{4,2},{5,3},{6,4},{7,5},{8,14},{9,15},{10,... | collective-permute-start | bytes 1966088 | tf_op jit(solution)/shard_map/ppermute | solution.py:17
  152.5 4.9 %copy-start.8 = (bf16[1,1024,512]{2,1,0:T(8,128)(2,1)S(1)}, bf16[1,1024,512]{2,1,0:T(8,128)(2,1)}, u32[]{:S(2)}) copy-start(bf16[1,1024,512]{2,1,0:T(8,128)(2,1)} %param.11) | copy-start | bytes 3145732
  152.6 18.7 %collective-permute-start.10 = (bf16[640,512]{1,0:T(8,128)(2,1)S(1)}, bf16[640,512]{1,0:T(8,128)(2,1)S(1)}, u32[]{:S(2)}, u32[]{:S(2)}) collective-permute-start(bf16[640,512]{1,0:T(8,128)(2,1)S(1)} %pad_maximum_fusion.3), channel_id=1, source_target_pairs={{0,1},{1,0},{2,3},{3,2},{4,5},{5,4},{6,7},{7,6},{8,9},{9,8},{10,11... | collective-permute-start | bytes 1966088 | tf_op jit(solution)/shard_map/ppermute | solution.py:23
  157.4 67.5 %collective-permute-start.22 = (f32[1024,512]{1,0:T(8,128)}, f32[1024,512]{1,0:T(8,128)}, u32[]{:S(2)}, u32[]{:S(2)}) collective-permute-start(f32[1024,512]{1,0:T(8,128)} %fusion.35), channel_id=1, source_target_pairs={{0,1},{1,0},{2,3},{3,2},{4,5},{5,4},{6,7},{7,6},{8,9},{9,8},{10,11... | collective-permute-start | bytes 6291464 | tf_op jit(solution)/shard_map/ppermute | solution.py:23
  166.6 25.0 %copy-start.14 = (bf16[160,2048]{1,0:T(8,128)(2,1)}, bf16[160,2048]{1,0:T(8,128)(2,1)S(1)}, u32[]{:S(2)}) copy-start(bf16[160,2048]{1,0:T(8,128)(2,1)S(1)} %collective-permute-done.15) | copy-start | bytes 1966084
  167.0 3.2 %copy-start.16 = (bf16[160,2048]{1,0:T(8,128)(2,1)}, bf16[160,2048]{1,0:T(8,128)(2,1)S(1)}, u32[]{:S(2)}) copy-start(bf16[160,2048]{1,0:T(8,128)(2,1)S(1)} %collective-permute-done.14) | copy-start | bytes 1966084
  168.0 2.3 copy-start.4
  168.0 13.9 %collective-permute-start.16 = (bf16[160,2048]{1,0:T(8,128)(2,1)}, bf16[160,2048]{1,0:T(8,128)(2,1)}, u32[]{:S(2)}, u32[]{:S(2)}) collective-permute-start(bf16[160,2048]{1,0:T(8,128)(2,1)} %broadcast_select_fusion), channel_id=1, source_target_pairs={{0,2},{1,7},{2,4},{3,1},{4,6},{5,3},{6,0},{7,5},{8,10},{9,15},{10,... | collective-permute-start | bytes 1966088 | tf_op jit(solution)/shard_map/ppermute | solution.py:149
  172.5 9.4 %copy-start.12 = (bf16[640,512]{1,0:T(8,128)(2,1)S(1)}, bf16[640,512]{1,0:T(8,128)(2,1)}, u32[]{:S(2)}) copy-start(bf16[640,512]{1,0:T(8,128)(2,1)} %copy-done.11) | copy-start | bytes 1966084
  172.5 9.4 %copy-start.13 = (bf16[160,2048]{1,0:T(8,128)(2,1)S(1)}, bf16[160,2048]{1,0:T(8,128)(2,1)}, u32[]{:S(2)}) copy-start(bf16[160,2048]{1,0:T(8,128)(2,1)} %shard_map.113) | copy-start | bytes 1966084
  172.5 42.6 %all-to-all-start.2 = ((bf16[32,40,512]{2,1,0:T(8,128)(2,1)}), bf16[32,40,512]{2,1,0:T(8,128)(2,1)S(1)}, u32[]{:S(2)}, u32[]{:S(2)}) async-start(bf16[32,40,512]{2,1,0:T(8,128)(2,1)} %bitcast.11), calls=%async_computation.2 | async-start | bytes 2621440 | tf_op jit(solution)/shard_map/all_to_all | solution.py:213
  181.9 6.4 %copy-start.17 = (bf16[160,2048]{1,0:T(8,128)(2,1)S(1)}, bf16[160,2048]{1,0:T(8,128)(2,1)}, u32[]{:S(2)}) copy-start(bf16[160,2048]{1,0:T(8,128)(2,1)} %copy-done.16) | copy-start | bytes 1966084
  187.1 4.6 %copy-start.6 = (bf16[1,512,2048]{2,1,0:T(8,128)(2,1)S(1)}, bf16[1,512,2048]{2,1,0:T(8,128)(2,1)}, u32[]{:S(2)}) copy-start(bf16[1,512,2048]{2,1,0:T(8,128)(2,1)} %param.10) | copy-start | bytes 6291460
  187.1 68.2 %collective-permute-start.21 = (f32[512,2048]{1,0:T(8,128)}, f32[512,2048]{1,0:T(8,128)}, u32[]{:S(2)}, u32[]{:S(2)}) collective-permute-start(f32[512,2048]{1,0:T(8,128)} %fusion.33), channel_id=1, source_target_pairs={{0,1},{1,0},{2,3},{3,2},{4,5},{5,4},{6,7},{7,6},{8,9},{9,8},{10,11... | collective-permute-start | bytes 12582920 | tf_op jit(solution)/shard_map/ppermute | solution.py:23
  194.5 2.4 collective-permute-start.17
  215.2 5.7 %copy-start.2 = (bf16[32,40,512]{2,1,0:T(8,128)(2,1)S(1)}, bf16[32,40,512]{2,1,0:T(8,128)(2,1)}, u32[]{:S(2)}) copy-start(bf16[32,40,512]{2,1,0:T(8,128)(2,1)} %copy-done.1) | copy-start | bytes 3932164
  215.2 37.8 %all-to-all-start.3 = ((bf16[32,40,512]{2,1,0:T(8,128)(2,1)}), bf16[32,40,512]{2,1,0:T(8,128)(2,1)}, u32[]{:S(2)}, u32[]{:S(2)}) async-start(bf16[32,40,512]{2,1,0:T(8,128)(2,1)} %bitcast.66), calls=%async_computation.3 | async-start | bytes 2621440 | tf_op jit(solution)/shard_map/all_to_all | solution.py:213
  220.9 1.6 copy-start.5
  222.5 2.4 copy-start.23
  222.5 2.4 copy-start.24
  222.5 2.4 copy-start.25
  222.5 2.4 copy-start.26
  223.0 5.9 %collective-permute-start.18 = (f32[32,40]{1,0:T(8,128)S(1)}, f32[32,40]{1,0:T(8,128)S(1)}, u32[]{:S(2)}, u32[]{:S(2)}) collective-permute-start(f32[32,40]{1,0:T(8,128)S(1)} %reshape.77), channel_id=1, source_target_pairs={{0,1},{1,0},{2,3},{3,2},{4,5},{5,4},{6,7},{7,6},{8,9},{9,8},{10,11... | collective-permute-start | bytes 15368 | tf_op jit(solution)/shard_map/ppermute | solution.py:41
  224.9 4.1 %copy-start.28 = (f32[32,128]{1,0:T(8,128)S(1)}, f32[32,128]{1,0:T(8,128)}, u32[]{:S(2)}) copy-start(f32[32,128]{1,0:T(8,128)} %copy-done.27) | copy-start | bytes 49156
  228.9 3.1 %collective-permute-start.19 = (f32[32,40]{1,0:T(8,128)S(1)}, f32[32,40]{1,0:T(8,128)S(1)}, u32[]{:S(2)}, u32[]{:S(2)}) collective-permute-start(f32[32,40]{1,0:T(8,128)S(1)} %add.213), channel_id=1, source_target_pairs={{0,2},{1,3},{2,0},{3,1},{4,6},{5,7},{6,4},{7,5},{8,10},{9,11},{10,... | collective-permute-start | bytes 15368 | tf_op jit(solution)/shard_map/ppermute | solution.py:41
  229.4 7.4 %copy-start.33 = (s32[128,8]{0,1:T(8,128)S(1)}, s32[128,8]{0,1:T(8,128)}, u32[]{:S(2)}) copy-start(s32[128,8]{0,1:T(8,128)} %param.8) | copy-start | bytes 12292
  229.4 7.5 %copy-start.31 = (f32[128,8]{0,1:T(8,128)S(1)}, f32[128,8]{0,1:T(8,128)}, u32[]{:S(2)}) copy-start(f32[128,8]{0,1:T(8,128)} %param.9) | copy-start | bytes 12292
  229.4 7.5 %copy-start.35 = (f32[128]{0:T(128)S(1)}, f32[128]{0:T(128)}, u32[]{:S(2)}) copy-start(f32[128]{0:T(128)} %copy-done.34) | copy-start | bytes 1540
  232.0 23.3 %copy-start.15 = (bf16[160,2048]{1,0:T(8,128)(2,1)S(1)}, bf16[160,2048]{1,0:T(8,128)(2,1)}, u32[]{:S(2)}) copy-start(bf16[160,2048]{1,0:T(8,128)(2,1)} %copy-done.14) | copy-start | bytes 1966084
  232.0 23.3 %copy-start.18 = (bf16[160,2048]{1,0:T(8,128)(2,1)S(1)}, bf16[160,2048]{1,0:T(8,128)(2,1)}, u32[]{:S(2)}) copy-start(bf16[160,2048]{1,0:T(8,128)(2,1)} %copy-done.16) | copy-start | bytes 1966084
  232.0 4.6 %collective-permute-start.20 = (f32[32,40]{1,0:T(8,128)S(1)}, f32[32,40]{1,0:T(8,128)S(1)}, u32[]{:S(2)}, u32[]{:S(2)}) collective-permute-start(f32[32,40]{1,0:T(8,128)S(1)} %add.214), channel_id=1, source_target_pairs={{0,4},{1,5},{2,6},{3,7},{4,0},{5,1},{6,2},{7,3},{8,12},{9,13},{10,... | collective-permute-start | bytes 15368 | tf_op jit(solution)/shard_map/ppermute | solution.py:41

commit v2 on v1

--- a/solution.py
+++ b/solution.py
@@ -29,10 +29,6 @@
     return jnp.dot(a, b, preferred_element_type=F32)
 
 
-def dot_t(a, b):
-    return jnp.einsum("rd,fd->rf", a, b, preferred_element_type=F32)
-
-
 def gather_dot(a, b):
     return jnp.einsum("rd,rf->df", a, b, preferred_element_type=F32)
 
@@ -41,32 +37,15 @@
     return lax.ppermute(v, "expert", [(e, e ^ bit) for e in range(2 * n_y)])
 
 
-def partial_kernel(order, own, part, w_own, w_part, near, far1, far2, far3, *, dims, chunk):
-    step = pl.program_id(0)
-    width = near.shape[1]
-
-    def columns(j, carry):
-        cols = pl.ds(pl.multiple_of(j * chunk, chunk), chunk)
-        if dims[1] == 0:
-            a, b = w_own[:, cols], w_part[:, cols]
-        else:
-            a, b = w_own[cols, :], w_part[cols, :]
-        contract = (((1,), (dims[1],)), ((), ()))
-        total = lax.dot_general(own[...], a, contract, preferred_element_type=F32)
-        total = total + lax.dot_general(part[...], b, contract, preferred_element_type=F32)
-        for k, out in enumerate((far1, far2, far3)):
-
-            @pl.when(step == k)
-            def _(out=out):
-                out[:, cols] = total.astype(BF)
-
-        @pl.when(step == 3)
-        def _():
-            near[:, cols] = total
-
-        return carry
-
-    lax.fori_loop(0, width // chunk, columns, 0)
+def partial_kernel(order, own0, own1, own2, own3, part, w_own, w_part, near, *far, turned):
+    rows = near.shape[0]
+    contract = (((1,), (1 if turned else 0,)), ((), ()))
+    own = jnp.concatenate([own0[...], own1[...], own2[...], own3[...]], axis=0)
+    total = lax.dot_general(own, w_own[...], contract, preferred_element_type=F32)
+    total = total + lax.dot_general(part[...], w_part[...], contract, preferred_element_type=F32)
+    near[...] = total[:rows]
+    for k, out in enumerate(far):
+        out[...] = total[(k + 1) * rows : (k + 2) * rows].astype(BF)
 
 
 def partial_products(slab, part, w_own, w_part, order, turned):
@@ -74,24 +53,65 @@
     rows = part.shape[0] // n_y
     k = slab.shape[1]
     width = w_own.shape[0] if turned else w_own.shape[1]
-    whole = pl.BlockSpec(w_own.shape, lambda i, order: (0, 0))
-    out = pl.BlockSpec((rows, width), lambda i, order: (0, 0))
+    chunk = width // 4
+
+    def rows_of(d):
+        return pl.BlockSpec((rows, k), lambda j, order: (order[d], 0))
+
+    if turned:
+        weight = pl.BlockSpec((chunk, k), lambda j, order: (j, 0))
+    else:
+        weight = pl.BlockSpec((k, chunk), lambda j, order: (0, j))
+    out = pl.BlockSpec((rows, chunk), lambda j, order: (0, j))
     return pl.pallas_call(
-        functools.partial(partial_kernel, dims=(1, 1 if turned else 0), chunk=512),
+        functools.partial(partial_kernel, turned=turned),
         grid_spec=pltpu.PrefetchScalarGridSpec(
             num_scalar_prefetch=1,
-            grid=(n_y,),
-            in_specs=[
-                pl.BlockSpec((rows, k), lambda i, order: (order[i], 0)),
-                pl.BlockSpec((rows, k), lambda i, order: ((i + 1) % 4, 0)),
-                whole,
-                whole,
-            ],
+            grid=(width // chunk,),
+            in_specs=[rows_of(d) for d in range(4)]
+            + [pl.BlockSpec(part.shape, lambda j, order: (0, 0)), weight, weight],
             out_specs=[out, out, out, out],
         ),
         out_shape=[jax.ShapeDtypeStruct((rows, width), F32)]
         + [jax.ShapeDtypeStruct((rows, width), BF)] * 3,
-    )(order, slab, part, w_own, w_part)
+    )(order, slab, slab, slab, slab, part, w_own, w_part)
+
+
+def spread_kernel(places, p0, p1, p2, p3, weight, out, held, *, turned):
+    rows = p0.shape[0]
+
+    @pl.when(pl.program_id(0) == 0)
+    def _():
+        for d, piece in enumerate((p0, p1, p2, p3)):
+            held[d * rows : (d + 1) * rows, :] = piece[...]
+
+    contract = (((1,), (1 if turned else 0,)), ((), ()))
+    total = lax.dot_general(held[...], weight[...], contract, preferred_element_type=F32).astype(BF)
+    for d in range(4):
+        start = pl.multiple_of(places[d] * rows, rows)
+        out[pl.ds(start, rows), :] = total[d * rows : (d + 1) * rows]
+
+
+def spread_product(pieces, weight, places, turned):
+    rows, k = pieces[0].shape
+    width = weight.shape[0] if turned else weight.shape[1]
+    chunk = width // 2
+    piece = pl.BlockSpec((rows, k), lambda j, places: (0, 0))
+    if turned:
+        w_spec = pl.BlockSpec((chunk, k), lambda j, places: (j, 0))
+    else:
+        w_spec = pl.BlockSpec((k, chunk), lambda j, places: (0, j))
+    return pl.pallas_call(
+        functools.partial(spread_kernel, turned=turned),
+        grid_spec=pltpu.PrefetchScalarGridSpec(
+            num_scalar_prefetch=1,
+            grid=(2,),
+            in_specs=[piece, piece, piece, piece, w_spec],
+            out_specs=pl.BlockSpec((4 * rows, chunk), lambda j, places: (0, j)),
+            scratch_shapes=[pltpu.VMEM((4 * rows, k), BF)],
+        ),
+        out_shape=jax.ShapeDtypeStruct((4 * rows, width), BF),
+    )(places, *pieces, weight)
 
 
 def send_far(far, n_y):
@@ -157,7 +177,7 @@
     dn = permute_y(v, 1, n_y)
     up = permute_y(v, -1, n_y)
     far = permute_by_core(jnp.where(core == 0, dn, up), n_y)
-    return jnp.concatenate([v, up, far, dn], axis=0)
+    return [v, up, far, dn]
 
 
 def relative(slab, half, y, n_y):
@@ -167,14 +187,6 @@
             lax.dynamic_slice_in_dim(slab, (half * n_y + (y + d) % n_y) * rows, rows, 0)
             for d in range(n_y)
         ],
-        axis=0,
-    )
-
-
-def absolute(part, y, n_y):
-    rows = part.shape[0] // n_y
-    return jnp.concatenate(
-        [lax.dynamic_slice_in_dim(part, ((yy - y) % n_y) * rows, rows, 0) for yy in range(n_y)],
         axis=0,
     )
 
@@ -217,7 +229,9 @@
     in_part = permute_core(in_own, n_y)
     out_part = permute_core(out_own, n_y)
 
-    scores_t, _ = lax.optimization_barrier((scores_t, token_send))
+    places = lax.rem(y + jnp.arange(n_y, dtype=jnp.int32), n_y)
+    order = core * n_y + places
+    scores_t, places, order, _ = lax.optimization_barrier((scores_t, places, order, token_send))
     score_total = jnp.sum(scores_t, axis=0, keepdims=True)
     weights_t = ROUTE_SCALE * scores_t / score_total
     weight_of = jnp.sum(jnp.where(named, weights_t[:, None, :], 0.0), axis=0)
@@ -229,7 +243,6 @@
     grad_slab = exchange(grad_send)
 
     token_slab, _ = lax.optimization_barrier((token_slab, grad_send[:8]))
-    order = core * n_y + lax.rem(y + jnp.array([1, 2, 3, 4], jnp.int32), n_y)
     tok_part = permute_core(relative(token_slab, 1 - core, y, n_y), n_y)
     near, *far = partial_products(token_slab, tok_part, in_own, in_part, order, False)
     got = send_far(far, n_y)
@@ -246,17 +259,19 @@
     token_slab, _ = lax.optimization_barrier((token_slab, gate_up_grad))
     tok_own = relative(token_slab, core, y, n_y)
 
-    hid_parts, _ = lax.optimization_barrier((hid_parts, far[0]))
-    hid = jnp.concatenate([hidden] + hid_parts, axis=0)
-    out_other = permute_core(absolute(dot(hid, out_part).astype(BF), y, n_y), n_y)
-    out_mine = absolute(dot(hid, out_own).astype(BF), y, n_y)
+    out_other = permute_core(spread_product([hidden] + hid_parts, out_part, places, False), n_y)
+    out_mine = spread_product([hidden] + hid_parts, out_own, places, False)
     expert_out = both_halves(out_mine, out_other, core)
     out_back = exchange(expert_out)
 
-    gug = gather_rows(gate_up_grad, core, n_y)
-    grad_other = permute_core(absolute(dot_t(gug, in_part).astype(BF), y, n_y), n_y)
-    grad_mine = absolute(dot_t(gug, in_own).astype(BF), y, n_y)
+    gug_parts = gather_rows(gate_up_grad, core, n_y)
+    grad_other = permute_core(spread_product(gug_parts, in_part, places, True), n_y)
+    grad_mine = spread_product(gug_parts, in_own, places, True)
+    hidden, hid_parts, _ = lax.optimization_barrier((hidden, hid_parts, gate_up_grad))
+    hid = jnp.concatenate([hidden] + hid_parts, axis=0)
     choice_grad = both_halves(grad_mine, grad_other, core)
+    gug_parts, _ = lax.optimization_barrier((gug_parts, choice_grad))
+    gug = jnp.concatenate(gug_parts, axis=0)
     grad_back = exchange(choice_grad)
 
     tok_part, tok_own, _ = lax.optimization_barrier((tok_part, tok_own, choice_grad))

time: 265 us -> 278 us (1.049)
  Pallas kernels: 24.5 us -> 37.5 us
  waiting for transfers between devices: 116 us -> 128 us
  matrix products: 35.6 us -> 24.7 us
    ppermute x11, waiting for transfers between devices: 46.7 us -> 63.1 us  [permute_y(): lax.ppermute(v, 'expert', [(2 * y + c, 2 * ((y + step) % n_y) + c) for y...]
    pallas_call x2 -> x6, Pallas kernels: 18.7 us -> 31.7 us  [the longest x4 18.7 us: spread_product(): pl.pallas_call(functools.partial(spread_kernel, turned=turned), grid_spec...]
    dot_general x2 -> x0, matrix products: 6 us -> none  [dot_t(): return jnp.einsum('rd,fd->rf', a, b, preferred_element_type=F32)]
    all_to_all x4, waiting for transfers between devices: 61.3 us -> 57.2 us  [exchange(): lax.all_to_all(v, 'dp', split_axis=0, concat_axis=0, tiled=True)]
    dot_general x5 -> x3, matrix products: 7.53 us -> 4.57 us  [dot(): return jnp.dot(a, b, preferred_element_type=F32)]
    unnamed x77 -> x88, local copies, waits for them, and re-layouts: 9.28 us -> 11.1 us
  transfers between devices with their start and end apart: 27 -> 27, of which waited for: 14 -> 15; matrix products, arithmetic and copies ran while one was open for 16% -> 9% of each run, Pallas kernels for 8% -> 11%
where the time goes in v2:
time: 278 us; the launch traced here: 274 us
  waiting for transfers between devices  128 us (46%)
  starting transfers between devices  61.9 us (22%)
  Pallas kernels  37.5 us (13%)
  matrix products  24.7 us (9%)
  local copies, waits for them, and re-layouts  12.5 us (4%)
  other arithmetic  8.72 us (3%)
    ppermute x11, waiting for transfers between devices, permute_y(): lax.ppermute(v, 'expert', [(2 * y + c, 2 * ((y + step) % n_y) + c) for y...  63.1 us
    all_to_all x4, waiting for transfers between devices, exchange(): lax.all_to_all(v, 'dp', split_axis=0, concat_axis=0, tiled=True)  57.2 us
    all_to_all x4, starting transfers between devices, exchange(): lax.all_to_all(v, 'dp', split_axis=0, concat_axis=0, tiled=True)  31.4 us
    dot_general x7, matrix products, gather_dot(): return jnp.einsum('rd,rf->df', a, b, preferred_element_type=F32)  20.1 us
    pallas_call x4, Pallas kernels, spread_product(): pl.pallas_call(functools.partial(spread_kernel, turned=turned), grid_spec...  18.7 us
    ppermute x11, starting transfers between devices, permute_y(): lax.ppermute(v, 'expert', [(2 * y + c, 2 * ((y + step) % n_y) + c) for y...  15.9 us
    pallas_call x2, Pallas kernels, partial_products(): pl.pallas_call(functools.partial(partial_kernel, turned=turned), grid_spe...  13 us
    unnamed x88, local copies, waits for them, and re-layouts  11.1 us
  transfers between devices with their start and end apart: 27, of which 15 were waited for; matrix products, arithmetic and copies ran while one was open for 9% of the time, Pallas kernels for 11%

profile of v2, /device:TPU:33, one launch (start us, length us, event | category | flops | bytes accessed | tf_op | source)
XLA Modules:
  0.0 274.0 jit_solution(13130499836436730357)
XLA Ops:
  1.9 2.5 convolution_convert_fusion
  4.3 10.8 %all-to-all-start = ((bf16[32,40,512]{2,1,0:T(8,128)(2,1)}), bf16[32,40,512]{2,1,0:T(8,128)(2,1)S(1)}, u32[]{:S(2)}, u32[]{:S(2)}) async-start(bf16[32,40,512]{2,1,0:T(8,128)(2,1)} %bitcast.3), calls=%async_computation | async-start | bytes 2621440 | tf_op jit(solution)/shard_map/all_to_all | solution.py:225
  15.1 1.3 collective-permute-start.1
  17.4 2.0 fusion.30
  19.4 28.9 %all-to-all-done = bf16[32,40,512]{2,1,0:T(8,128)(2,1)S(1)} async-done(((bf16[32,40,512]{2,1,0:T(8,128)(2,1)}), bf16[32,40,512]{2,1,0:T(8,128)(2,1)S(1)}, u32[]{:S(2)}, u32[]{:S(2)}) %all-to-all-start) | async-done | bytes 1310752 | tf_op jit(solution)/shard_map/all_to_all | solution.py:225
  48.2 5.7 %all-to-all-start.2 = ((bf16[32,40,512]{2,1,0:T(8,128)(2,1)}), bf16[32,40,512]{2,1,0:T(8,128)(2,1)S(1)}, u32[]{:S(2)}, u32[]{:S(2)}) async-start(bf16[32,40,512]{2,1,0:T(8,128)(2,1)} %bitcast.67), calls=%async_computation.2 | async-start | bytes 2621440 | tf_op jit(solution)/shard_map/all_to_all | solution.py:225
  54.2 1.8 collective-permute-start
  56.0 1.7 collective-permute-done.part
  57.7 0.8 copy-done.23
  58.6 7.3 %shard_map.101 = (f32[160,2048]{1,0:T(8,128)}, bf16[160,2048]{1,0:T(8,128)(2,1)}, bf16[160,2048]{1,0:T(8,128)(2,1)}, bf16[160,2048]{1,0:T(8,128)(2,1)}) custom-call(s32[4]{0:T(128)} %get-tuple-element.35.order, bf16[1280,512]{1,0:T(8,128)(2,1)} %bitcast.59, bf16[1280,512]{1,0:T(8,128)(2,1)} %bitcast.60, bf16[1280,512]{1,0:T(8,128)(2,1)} %bitcast.61, ...), custom_call_target="tpu_custom_call" | custom-call | tf_op jit(solution)/shard_map/pallas_call | solution.py:66
  65.8 1.3 collective-permute-start.2
  67.1 2.6 collective-permute-start.3
  69.7 1.1 collective-permute-start.4
  70.8 1.2 collective-permute-start.8
  72.0 11.3 %collective-permute-done.2.first = bf16[160,2048]{1,0:T(8,128)(2,1)S(1)} collective-permute-done((bf16[160,2048]{1,0:T(8,128)(2,1)}, bf16[160,2048]{1,0:T(8,128)(2,1)S(1)}, u32[]{:S(2)}, u32[]{:S(2)}) %collective-permute-start.2) | collective-permute-done | bytes 655392 | tf_op jit(solution)/shard_map/ppermute | solution.py:17
  83.3 15.3 %collective-permute-done.3.second = bf16[160,2048]{1,0:T(8,128)(2,1)} collective-permute-done((bf16[160,2048]{1,0:T(8,128)(2,1)}, bf16[160,2048]{1,0:T(8,128)(2,1)}, u32[]{:S(2)}, u32[]{:S(2)}) %collective-permute-start.3) | collective-permute-done | bytes 655392 | tf_op jit(solution)/shard_map/ppermute | solution.py:17
  98.6 2.9 %shard_map.102 = (f32[160,2048]{1,0:T(8,128)}, bf16[160,1024]{1,0:T(8,128)(2,1)}) custom-call(f32[160,2048]{1,0:T(8,128)} %get-tuple-element.36.near, bf16[160,2048]{1,0:T(8,128)(2,1)} %copy-done.28, bf16[160,2048]{1,0:T(8,128)(2,1)} %collective-permute-done.3.second, bf16[160,2048]{1,0:T(8,128)(2,1)} %collective-permute-done.4.third), custom_call_target="tpu_custom_call" | custom-call | tf_op jit(solution)/shard_map/pallas_call | solution.py:133
  101.6 1.0 copy-done.1
  102.6 1.2 collective-permute-start.10
  103.8 1.7 collective-permute-done.10.part
  105.5 0.8 copy-done.26
  106.4 5.7 %shard_map.105 = (f32[160,1024]{1,0:T(8,128)}, bf16[160,1024]{1,0:T(8,128)(2,1)}, bf16[160,1024]{1,0:T(8,128)(2,1)}, bf16[160,1024]{1,0:T(8,128)(2,1)}) custom-call(s32[4]{0:T(128)} %get-tuple-element.35.order, bf16[1280,512]{1,0:T(8,128)(2,1)} %bitcast.53, bf16[1280,512]{1,0:T(8,128)(2,1)} %bitcast.54, bf16[1280,512]{1,0:T(8,128)(2,1)} %bitcast.55, ...), custom_call_target="tpu_custom_call" | custom-call | tf_op jit(solution)/shard_map/pallas_call | solution.py:66
  112.1 1.0 collective-permute-start.11
  113.1 2.1 collective-permute-start.12
  115.2 1.3 collective-permute-start.13
  116.5 6.0 %collective-permute-done.11.first = bf16[160,1024]{1,0:T(8,128)(2,1)S(1)} collective-permute-done((bf16[160,1024]{1,0:T(8,128)(2,1)}, bf16[160,1024]{1,0:T(8,128)(2,1)S(1)}, u32[]{:S(2)}, u32[]{:S(2)}) %collective-permute-start.11) | collective-permute-done | bytes 327712 | tf_op jit(solution)/shard_map/ppermute | solution.py:17
  122.5 7.4 %collective-permute-done.12.second = bf16[160,1024]{1,0:T(8,128)(2,1)S(1)} collective-permute-done((bf16[160,1024]{1,0:T(8,128)(2,1)}, bf16[160,1024]{1,0:T(8,128)(2,1)S(1)}, u32[]{:S(2)}, u32[]{:S(2)}) %collective-permute-start.12) | collective-permute-done | bytes 327712 | tf_op jit(solution)/shard_map/ppermute | solution.py:17
  130.7 2.9 %shard_map.106.p0 = bf16[160,2048]{1,0:T(8,128)(2,1)} custom-call(f32[160,1024]{1,0:T(8,128)} %get-tuple-element.43.near, bf16[160,1024]{1,0:T(8,128)(2,1)} %copy-done.29, bf16[160,1024]{1,0:T(8,128)(2,1)} %copy-done.30, bf16[160,1024]{1,0:T(8,128)(2,1)} %copy-done.31, f32[160,2048]{1,0:T(8,128)} %get-tuple-element.47.gate_up), custom_call_target="tpu_custom_call" | custom-call | tf_op jit(solution)/shard_map/pallas_call | solution.py:159
  133.6 2.1 collective-permute-start.15
  135.6 1.1 collective-permute-start.14
  137.1 2.3 collective-permute-start.6
  140.1 11.0 %collective-permute-done.15.p3 = bf16[160,2048]{1,0:T(8,128)(2,1)S(1)} collective-permute-done((bf16[160,2048]{1,0:T(8,128)(2,1)}, bf16[160,2048]{1,0:T(8,128)(2,1)S(1)}, u32[]{:S(2)}, u32[]{:S(2)}) %collective-permute-start.15) | collective-permute-done | bytes 655392 | tf_op jit(solution)/shard_map/ppermute | solution.py:17
  151.2 1.1 broadcast_select_fusion
  152.2 2.2 collective-permute-start.16
  154.4 3.6 %collective-permute-done.7.p3 = bf16[160,1024]{1,0:T(8,128)(2,1)S(1)} collective-permute-done((bf16[160,1024]{1,0:T(8,128)(2,1)S(1)}, bf16[160,1024]{1,0:T(8,128)(2,1)S(1)}, u32[]{:S(2)}, u32[]{:S(2)}) %collective-permute-start.7) | collective-permute-done | bytes 327712 | tf_op jit(solution)/shard_map/ppermute | solution.py:17
  158.0 8.5 %collective-permute-done.6.p2 = bf16[160,1024]{1,0:T(8,128)(2,1)S(1)} collective-permute-done((bf16[160,1024]{1,0:T(8,128)(2,1)S(1)}, bf16[160,1024]{1,0:T(8,128)(2,1)S(1)}, u32[]{:S(2)}, u32[]{:S(2)}) %collective-permute-start.6) | collective-permute-done | bytes 327712 | tf_op jit(solution)/shard_map/ppermute | solution.py:17
  168.0 4.0 %shard_map.104 = bf16[640,512]{1,0:T(8,128)(2,1)} custom-call(s32[4]{0:T(128)} %get-tuple-element.34.places, bf16[160,1024]{1,0:T(8,128)(2,1)} %get-tuple-element.56.p0, bf16[160,1024]{1,0:T(8,128)(2,1)} %copy-done.21, bf16[160,1024]{1,0:T(8,128)(2,1)} %copy-done.19, bf16[160,1024]{1,0:T(8,128)(2,1)} %copy-done.17, ...), custom_call_target="tpu_custom_call" | custom-call | tf_op jit(solution)/shard_map/pallas_call | solution.py:104
  172.0 1.5 collective-permute-start.9
  173.5 4.0 %shard_map.103 = bf16[640,512]{1,0:T(8,128)(2,1)} custom-call(s32[4]{0:T(128)} %get-tuple-element.34.places, bf16[160,1024]{1,0:T(8,128)(2,1)} %get-tuple-element.56.p0, bf16[160,1024]{1,0:T(8,128)(2,1)} %copy-done.21, bf16[160,1024]{1,0:T(8,128)(2,1)} %copy-done.19, bf16[160,1024]{1,0:T(8,128)(2,1)} %copy-done.17, bf16[1024,512]{1,0:T(8,128)(2,1)} %bitcast.70), custom_call_target="tpu_custom_call" | custom-call | tf_op jit(solution)/shard_map/pallas_call | solution.py:104
  177.5 0.8 copy-done.10
  178.4 5.4 %shard_map.108 = bf16[640,512]{1,0:T(8,128)(2,1)} custom-call(s32[4]{0:T(128)} %get-tuple-element.34.places, bf16[160,2048]{1,0:T(8,128)(2,1)} %shard_map.106.p0, bf16[160,2048]{1,0:T(8,128)(2,1)} %copy-done.8, bf16[160,2048]{1,0:T(8,128)(2,1)} %copy-done.10, bf16[160,2048]{1,0:T(8,128)(2,1)} %copy-done.6, bf16[512,2048]{1,0:T(8,128)(2,1)} %collective-permute-done.1.w_part.weight), custom_call_target="tpu_custom_call" | custom-call | tf_op jit(solution)/shard_map/pallas_call | solution.py:104
  183.8 1.3 maximum_select_fusion
  185.1 9.3 %all-to-all-start.1 = ((bf16[32,40,512]{2,1,0:T(8,128)(2,1)}), bf16[32,40,512]{2,1,0:T(8,128)(2,1)S(1)}, u32[]{:S(2)}, u32[]{:S(2)}) async-start(bf16[32,40,512]{2,1,0:T(8,128)(2,1)} %bitcast.9), calls=%async_computation.1 | async-start | bytes 2621440 | tf_op jit(solution)/shard_map/all_to_all | solution.py:225
  194.6 1.2 copy-done.4
  195.9 1.0 copy-done.36
  196.9 5.4 %shard_map.107 = bf16[640,512]{1,0:T(8,128)(2,1)} custom-call(s32[4]{0:T(128)} %get-tuple-element.34.places, bf16[160,2048]{1,0:T(8,128)(2,1)} %shard_map.106.p0, bf16[160,2048]{1,0:T(8,128)(2,1)} %copy-done.8, bf16[160,2048]{1,0:T(8,128)(2,1)} %copy-done.10, bf16[160,2048]{1,0:T(8,128)(2,1)} %copy-done.6, bf16[512,2048]{1,0:T(8,128)(2,1)} %bitcast.66), custom_call_target="tpu_custom_call" | custom-call | tf_op jit(solution)/shard_map/pallas_call | solution.py:104
  202.3 3.0 %maximum_select_fusion.1 = bf16[2,640,512]{2,1,0:T(8,128)(2,1)} fusion(bf16[1,640,512]{2,1,0:T(8,128)(2,1)} %bitcast.15, bf16[1,640,512]{2,1,0:T(8,128)(2,1)} %bitcast.73, pred[]{:T(512)S(6)} %eq.74), kind=kLoop, calls=%fused_computation.9 | loop fusion | flops 1966080 | bytes 2621441 | tf_op jit(solution)/shard_map/jit(_where)/select_n | solution.py:195
  205.4 1.0 copy-done.9
  206.7 0.9 copy-done.7
  207.8 3.9 %fusion.31 = f32[512,2048]{1,0:T(8,128)} fusion(bf16[640,512]{1,0:T(8,128)(2,1)S(1)} %copy-done.24, bf16[640,2048]{1,0:T(8,128)(2,1)S(1)} %constant_dynamic-update-slice_fusion), kind=kOutput, calls=%fused_computation.85 | convolution fusion | flops 1342177280 | bytes 7471104 | tf_op jit(solution)/shard_map/rd,rf->df/dot_general | solution.py:33
  211.7 1.0 collective-permute-start.21
  212.7 2.4 fusion.32
  215.1 12.8 %all-to-all-done.1 = bf16[32,40,512]{2,1,0:T(8,128)(2,1)S(1)} async-done(((bf16[32,40,512]{2,1,0:T(8,128)(2,1)}), bf16[32,40,512]{2,1,0:T(8,128)(2,1)S(1)}, u32[]{:S(2)}, u32[]{:S(2)}) %all-to-all-start.1) | async-done | bytes 1310752 | tf_op jit(solution)/shard_map/all_to_all | solution.py:225
  227.9 5.6 %all-to-all-start.3 = ((bf16[32,40,512]{2,1,0:T(8,128)(2,1)}), bf16[32,40,512]{2,1,0:T(8,128)(2,1)}, u32[]{:S(2)}, u32[]{:S(2)}) async-start(bf16[32,40,512]{2,1,0:T(8,128)(2,1)} %bitcast.68), calls=%async_computation.3 | async-start | bytes 2621440 | tf_op jit(solution)/shard_map/all_to_all | solution.py:225
  233.5 0.9 constant_dynamic-slice_fusion.3
  235.6 1.8 collective-permute-start.18
  237.5 4.0 %fusion.2 = bf16[1,1024,512]{2,1,0:T(8,128)(2,1)} fusion(f32[1024,512]{1,0:T(8,128)} %collective-permute-done.22, bf16[640,1024]{1,0:T(8,128)(2,1)} %copy-done.38, bf16[160,512]{1,0:T(8,128)(2,1)S(1)} %copy-done.33, bf16[160,512]{1,0:T(8,128)(2,1)S(1)} %copy-done.34, bf16[160,512]{1,0:T(8,128)(2,1)S(1)} %copy-done.35, bf16[160,512]{1,0:T(8,128)(2,1)S(1)} %copy-done.32), kind=kOutput, calls=%fused_computation.7 | convolution fusion | flops 674758656 | bytes 5111808 | tf_op jit(solution)/shard_map/rd,rf->df/dot_general | solution.py:33
  242.3 2.3 collective-permute-done.19
  244.6 2.0 collective-permute-start.20
  246.5 1.0 fusion.5
  247.6 1.5 collective-permute-done.20
  250.0 15.6 %all-to-all-done.3 = bf16[32,40,512]{2,1,0:T(8,128)(2,1)} async-done(((bf16[32,40,512]{2,1,0:T(8,128)(2,1)}), bf16[32,40,512]{2,1,0:T(8,128)(2,1)}, u32[]{:S(2)}, u32[]{:S(2)}) %all-to-all-start.3) | async-done | bytes 1310752 | tf_op jit(solution)/shard_map/all_to_all | solution.py:225
  265.5 2.4 fusion.4
  267.9 6.1 %fusion = bf16[1,512,2048]{2,1,0:T(8,128)(2,1)} fusion(f32[512,2048]{1,0:T(8,128)} %collective-permute-done.21, bf16[640,512]{1,0:T(8,128)(2,1)S(1)} %pad_maximum_fusion.2, bf16[640,2048]{1,0:T(8,128)(2,1)} %copy-done.14), kind=kOutput, calls=%fused_computation.2 | convolution fusion | flops 1344274432 | bytes 9568256 | tf_op jit(solution)/shard_map/rd,rf->df/dot_general | solution.py:33
  (127 shorter events, 9.5 us)
Async XLA Ops:
  0.6 16.8 %copy-start = (bf16[128,512]{1,0:T(8,128)(2,1)S(1)}, bf16[128,512]{1,0:T(8,128)(2,1)}, u32[]{:S(2)}) copy-start(bf16[128,512]{1,0:T(8,128)(2,1)} %param.11) | copy-start | bytes 393220
  4.3 12.6 %copy-start.39 = (f32[128,8]{0,1:T(8,128)S(1)}, f32[128,8]{0,1:T(8,128)}, u32[]{:S(2)}) copy-start(f32[128,8]{0,1:T(8,128)} %param.8) | copy-start | bytes 12292
  4.3 12.6 %copy-start.40 = (s32[128,8]{0,1:T(8,128)S(1)}, s32[128,8]{0,1:T(8,128)}, u32[]{:S(2)}) copy-start(s32[128,8]{0,1:T(8,128)} %param.7) | copy-start | bytes 12292
  4.3 43.9 %all-to-all-start = ((bf16[32,40,512]{2,1,0:T(8,128)(2,1)}), bf16[32,40,512]{2,1,0:T(8,128)(2,1)S(1)}, u32[]{:S(2)}, u32[]{:S(2)}) async-start(bf16[32,40,512]{2,1,0:T(8,128)(2,1)} %bitcast.3), calls=%async_computation | async-start | bytes 2621440 | tf_op jit(solution)/shard_map/all_to_all | solution.py:225
  15.1 40.9 %collective-permute-start.1 = (bf16[512,2048]{1,0:T(8,128)(2,1)}, bf16[512,2048]{1,0:T(8,128)(2,1)}, u32[]{:S(2)}, u32[]{:S(2)}) collective-permute-start(bf16[512,2048]{1,0:T(8,128)(2,1)} %bitcast.64), channel_id=1, source_target_pairs={{0,1},{1,0},{2,3},{3,2},{4,5},{5,4},{6,7},{7,6},{8,9},{9,8},{10,11... | collective-permute-start | bytes 6291464 | tf_op jit(solution)/shard_map/ppermute | solution.py:23
  48.2 5.8 %copy-start.3 = (bf16[32,40,512]{2,1,0:T(8,128)(2,1)}, bf16[32,40,512]{2,1,0:T(8,128)(2,1)S(1)}, u32[]{:S(2)}) copy-start(bf16[32,40,512]{2,1,0:T(8,128)(2,1)S(1)} %all-to-all-done) | copy-start | bytes 3932164
  48.2 53.2 %all-to-all-start.2 = ((bf16[32,40,512]{2,1,0:T(8,128)(2,1)}), bf16[32,40,512]{2,1,0:T(8,128)(2,1)S(1)}, u32[]{:S(2)}, u32[]{:S(2)}) async-start(bf16[32,40,512]{2,1,0:T(8,128)(2,1)} %bitcast.67), calls=%async_computation.2 | async-start | bytes 2621440 | tf_op jit(solution)/shard_map/all_to_all | solution.py:225
  54.2 16.6 %copy-start.13 = (bf16[1,1024,512]{2,1,0:T(8,128)(2,1)S(1)}, bf16[1,1024,512]{2,1,0:T(8,128)(2,1)}, u32[]{:S(2)}) copy-start(bf16[1,1024,512]{2,1,0:T(8,128)(2,1)} %param.10) | copy-start | bytes 3145732
  54.2 3.5 %collective-permute-start = (bf16[640,512]{1,0:T(8,128)(2,1)S(1)}, bf16[640,512]{1,0:T(8,128)(2,1)S(1)}, u32[]{:S(2)}, u32[]{:S(2)}) collective-permute-start(bf16[640,512]{1,0:T(8,128)(2,1)S(1)} %pad_maximum_fusion), channel_id=1, source_target_pairs={{0,1},{1,0},{2,3},{3,2},{4,5},{5,4},{6,7},{7,6},{8,9},{9,8},{10,11... | collective-permute-start | bytes 1966088 | tf_op jit(solution)/shard_map/ppermute | solution.py:23
  57.7 0.8 copy-start.23
  65.8 17.5 %collective-permute-start.2 = (bf16[160,2048]{1,0:T(8,128)(2,1)}, bf16[160,2048]{1,0:T(8,128)(2,1)S(1)}, u32[]{:S(2)}, u32[]{:S(2)}) collective-permute-start(bf16[160,2048]{1,0:T(8,128)(2,1)} %get-tuple-element.37), channel_id=1, source_target_pairs={{0,2},{1,3},{2,4},{3,5},{4,6},{5,7},{6,0},{7,1},{8,10},{9,11},{10,... | collective-permute-start | bytes 1966088 | tf_op jit(solution)/shard_map/ppermute | solution.py:17
  67.1 31.4 %collective-permute-start.3 = (bf16[160,2048]{1,0:T(8,128)(2,1)}, bf16[160,2048]{1,0:T(8,128)(2,1)}, u32[]{:S(2)}, u32[]{:S(2)}) collective-permute-start(bf16[160,2048]{1,0:T(8,128)(2,1)} %get-tuple-element.38), channel_id=1, source_target_pairs={{0,4},{1,5},{2,6},{3,7},{4,0},{5,1},{6,2},{7,3},{8,12},{9,13},{10,... | collective-permute-start | bytes 1966088 | tf_op jit(solution)/shard_map/ppermute | solution.py:17
  69.7 28.8 %collective-permute-start.4 = (bf16[160,2048]{1,0:T(8,128)(2,1)}, bf16[160,2048]{1,0:T(8,128)(2,1)}, u32[]{:S(2)}, u32[]{:S(2)}) collective-permute-start(bf16[160,2048]{1,0:T(8,128)(2,1)} %get-tuple-element.39), channel_id=1, source_target_pairs={{0,6},{1,7},{2,0},{3,1},{4,2},{5,3},{6,4},{7,5},{8,14},{9,15},{10,... | collective-permute-start | bytes 1966088 | tf_op jit(solution)/shard_map/ppermute | solution.py:17
  70.8 33.0 %collective-permute-start.8 = (bf16[1024,512]{1,0:T(8,128)(2,1)S(1)}, bf16[1024,512]{1,0:T(8,128)(2,1)}, u32[]{:S(2)}, u32[]{:S(2)}) collective-permute-start(bf16[1024,512]{1,0:T(8,128)(2,1)S(1)} %bitcast.71), channel_id=1, source_target_pairs={{0,1},{1,0},{2,3},{3,2},{4,5},{5,4},{6,7},{7,6},{8,9},{9,8},{10,11... | collective-permute-start | bytes 3145736 | tf_op jit(solution)/shard_map/ppermute | solution.py:23
  83.3 15.3 %copy-start.28 = (bf16[160,2048]{1,0:T(8,128)(2,1)}, bf16[160,2048]{1,0:T(8,128)(2,1)S(1)}, u32[]{:S(2)}) copy-start(bf16[160,2048]{1,0:T(8,128)(2,1)S(1)} %collective-permute-done.2.first) | copy-start | bytes 1966084
  101.5 1.1 copy-start.1
  102.6 3.0 %collective-permute-start.10 = (bf16[640,512]{1,0:T(8,128)(2,1)S(1)}, bf16[640,512]{1,0:T(8,128)(2,1)S(1)}, u32[]{:S(2)}, u32[]{:S(2)}) collective-permute-start(bf16[640,512]{1,0:T(8,128)(2,1)S(1)} %pad_maximum_fusion.1), channel_id=1, source_target_pairs={{0,1},{1,0},{2,3},{3,2},{4,5},{5,4},{6,7},{7,6},{8,9},{9,8},{10,11... | collective-permute-start | bytes 1966088 | tf_op jit(solution)/shard_map/ppermute | solution.py:23
  105.5 0.8 copy-start.26
  112.1 10.4 %collective-permute-start.11 = (bf16[160,1024]{1,0:T(8,128)(2,1)}, bf16[160,1024]{1,0:T(8,128)(2,1)S(1)}, u32[]{:S(2)}, u32[]{:S(2)}) collective-permute-start(bf16[160,1024]{1,0:T(8,128)(2,1)} %get-tuple-element.44), channel_id=1, source_target_pairs={{0,2},{1,3},{2,4},{3,5},{4,6},{5,7},{6,0},{7,1},{8,10},{9,11},{10,... | collective-permute-start | bytes 983048 | tf_op jit(solution)/shard_map/ppermute | solution.py:17
  113.1 16.8 %collective-permute-start.12 = (bf16[160,1024]{1,0:T(8,128)(2,1)}, bf16[160,1024]{1,0:T(8,128)(2,1)S(1)}, u32[]{:S(2)}, u32[]{:S(2)}) collective-permute-start(bf16[160,1024]{1,0:T(8,128)(2,1)} %get-tuple-element.45), channel_id=1, source_target_pairs={{0,4},{1,5},{2,6},{3,7},{4,0},{5,1},{6,2},{7,3},{8,12},{9,13},{10,... | collective-permute-start | bytes 983048 | tf_op jit(solution)/shard_map/ppermute | solution.py:17
  115.2 14.7 %collective-permute-start.13 = (bf16[160,1024]{1,0:T(8,128)(2,1)}, bf16[160,1024]{1,0:T(8,128)(2,1)S(1)}, u32[]{:S(2)}, u32[]{:S(2)}) collective-permute-start(bf16[160,1024]{1,0:T(8,128)(2,1)} %get-tuple-element.46), channel_id=1, source_target_pairs={{0,6},{1,7},{2,0},{3,1},{4,2},{5,3},{6,4},{7,5},{8,14},{9,15},{10,... | collective-permute-start | bytes 983048 | tf_op jit(solution)/shard_map/ppermute | solution.py:17
  122.5 7.4 %copy-start.29 = (bf16[160,1024]{1,0:T(8,128)(2,1)}, bf16[160,1024]{1,0:T(8,128)(2,1)S(1)}, u32[]{:S(2)}) copy-start(bf16[160,1024]{1,0:T(8,128)(2,1)S(1)} %collective-permute-done.11.first) | copy-start | bytes 983044
  130.7 6.1 %copy-start.15 = (bf16[160,1024]{1,0:T(8,128)(2,1)S(1)}, bf16[160,1024]{1,0:T(8,128)(2,1)}, u32[]{:S(2)}) copy-start(bf16[160,1024]{1,0:T(8,128)(2,1)} %get-tuple-element.56.p0) | copy-start | bytes 983044
  133.6 17.4 %collective-permute-start.15 = (bf16[160,2048]{1,0:T(8,128)(2,1)}, bf16[160,2048]{1,0:T(8,128)(2,1)S(1)}, u32[]{:S(2)}, u32[]{:S(2)}) collective-permute-start(bf16[160,2048]{1,0:T(8,128)(2,1)} %shard_map.106.p0), channel_id=1, source_target_pairs={{0,2},{1,3},{2,4},{3,5},{4,6},{5,7},{6,0},{7,1},{8,10},{9,11},{10,... | collective-permute-start | bytes 1966088 | tf_op jit(solution)/shard_map/ppermute | solution.py:17
  135.6 15.5 %collective-permute-start.14 = (bf16[160,2048]{1,0:T(8,128)(2,1)}, bf16[160,2048]{1,0:T(8,128)(2,1)S(1)}, u32[]{:S(2)}, u32[]{:S(2)}) collective-permute-start(bf16[160,2048]{1,0:T(8,128)(2,1)} %shard_map.106.p0), channel_id=1, source_target_pairs={{0,6},{1,7},{2,0},{3,1},{4,2},{5,3},{6,4},{7,5},{8,14},{9,15},{10,... | collective-permute-start | bytes 1966088 | tf_op jit(solution)/shard_map/ppermute | solution.py:17
  136.8 21.2 %collective-permute-start.7 = (bf16[160,1024]{1,0:T(8,128)(2,1)S(1)}, bf16[160,1024]{1,0:T(8,128)(2,1)S(1)}, u32[]{:S(2)}, u32[]{:S(2)}) collective-permute-start(bf16[160,1024]{1,0:T(8,128)(2,1)S(1)} %copy-done.15), channel_id=1, source_target_pairs={{0,2},{1,3},{2,4},{3,5},{4,6},{5,7},{6,0},{7,1},{8,10},{9,11},{10,... | collective-permute-start | bytes 983048 | tf_op jit(solution)/shard_map/ppermute | solution.py:17
  137.1 29.4 %collective-permute-start.6 = (bf16[160,1024]{1,0:T(8,128)(2,1)S(1)}, bf16[160,1024]{1,0:T(8,128)(2,1)S(1)}, u32[]{:S(2)}, u32[]{:S(2)}) collective-permute-start(bf16[160,1024]{1,0:T(8,128)(2,1)S(1)} %copy-done.15), channel_id=1, source_target_pairs={{0,4},{1,5},{2,6},{3,7},{4,0},{5,1},{6,2},{7,3},{8,12},{9,13},{10,... | collective-permute-start | bytes 983048 | tf_op jit(solution)/shard_map/ppermute | solution.py:17
  139.4 27.1 %collective-permute-start.5 = (bf16[160,1024]{1,0:T(8,128)(2,1)S(1)}, bf16[160,1024]{1,0:T(8,128)(2,1)S(1)}, u32[]{:S(2)}, u32[]{:S(2)}) collective-permute-start(bf16[160,1024]{1,0:T(8,128)(2,1)S(1)} %copy-done.15), channel_id=1, source_target_pairs={{0,6},{1,7},{2,0},{3,1},{4,2},{5,3},{6,4},{7,5},{8,14},{9,15},{10,... | collective-permute-start | bytes 983048 | tf_op jit(solution)/shard_map/ppermute | solution.py:17
  151.0 21.0 %copy-start.6 = (bf16[160,2048]{1,0:T(8,128)(2,1)}, bf16[160,2048]{1,0:T(8,128)(2,1)S(1)}, u32[]{:S(2)}) copy-start(bf16[160,2048]{1,0:T(8,128)(2,1)S(1)} %collective-permute-done.15.p3) | copy-start | bytes 1966084
  151.2 20.8 %copy-start.8 = (bf16[160,2048]{1,0:T(8,128)(2,1)}, bf16[160,2048]{1,0:T(8,128)(2,1)S(1)}, u32[]{:S(2)}) copy-start(bf16[160,2048]{1,0:T(8,128)(2,1)S(1)} %collective-permute-done.14.p1) | copy-start | bytes 1966084
  152.2 25.3 %collective-permute-start.16 = (bf16[160,2048]{1,0:T(8,128)(2,1)}, bf16[160,2048]{1,0:T(8,128)(2,1)S(1)}, u32[]{:S(2)}, u32[]{:S(2)}) collective-permute-start(bf16[160,2048]{1,0:T(8,128)(2,1)} %broadcast_select_fusion), channel_id=1, source_target_pairs={{0,2},{1,7},{2,4},{3,1},{4,6},{5,3},{6,0},{7,5},{8,10},{9,15},{10,... | collective-permute-start | bytes 1966088 | tf_op jit(solution)/shard_map/ppermute | solution.py:169
  158.0 8.5 %copy-start.17 = (bf16[160,1024]{1,0:T(8,128)(2,1)}, bf16[160,1024]{1,0:T(8,128)(2,1)S(1)}, u32[]{:S(2)}) copy-start(bf16[160,1024]{1,0:T(8,128)(2,1)S(1)} %collective-permute-done.7.p3) | copy-start | bytes 983044
  172.0 11.8 %collective-permute-start.9 = (bf16[640,512]{1,0:T(8,128)(2,1)}, bf16[640,512]{1,0:T(8,128)(2,1)S(1)}, u32[]{:S(2)}, u32[]{:S(2)}) collective-permute-start(bf16[640,512]{1,0:T(8,128)(2,1)} %shard_map.104), channel_id=1, source_target_pairs={{0,1},{1,0},{2,3},{3,2},{4,5},{5,4},{6,7},{7,6},{8,9},{9,8},{10,11... | collective-permute-start | bytes 1966088 | tf_op jit(solution)/shard_map/ppermute | solution.py:23
  177.5 6.3 %copy-start.25 = (bf16[640,512]{1,0:T(8,128)(2,1)S(1)}, bf16[640,512]{1,0:T(8,128)(2,1)}, u32[]{:S(2)}) copy-start(bf16[640,512]{1,0:T(8,128)(2,1)} %shard_map.103) | copy-start | bytes 1966084
  177.5 0.8 copy-start.10
  183.8 18.6 %collective-permute-start.17 = (bf16[640,512]{1,0:T(8,128)(2,1)}, bf16[640,512]{1,0:T(8,128)(2,1)}, u32[]{:S(2)}, u32[]{:S(2)}) collective-permute-start(bf16[640,512]{1,0:T(8,128)(2,1)} %shard_map.108), channel_id=1, source_target_pairs={{0,1},{1,0},{2,3},{3,2},{4,5},{5,4},{6,7},{7,6},{8,9},{9,8},{10,11... | collective-permute-start | bytes 1966088 | tf_op jit(solution)/shard_map/ppermute | solution.py:23
  185.1 9.4 %copy-start.16 = (bf16[160,1024]{1,0:T(8,128)(2,1)S(1)}, bf16[160,1024]{1,0:T(8,128)(2,1)}, u32[]{:S(2)}) copy-start(bf16[160,1024]{1,0:T(8,128)(2,1)} %get-tuple-element.56.p0) | copy-start | bytes 983044
  185.1 9.4 %copy-start.22 = (bf16[160,1024]{1,0:T(8,128)(2,1)S(1)}, bf16[160,1024]{1,0:T(8,128)(2,1)}, u32[]{:S(2)}) copy-start(bf16[160,1024]{1,0:T(8,128)(2,1)} %copy-done.21) | copy-start | bytes 983044
  185.1 9.5 %copy-start.20 = (bf16[160,1024]{1,0:T(8,128)(2,1)S(1)}, bf16[160,1024]{1,0:T(8,128)(2,1)}, u32[]{:S(2)}) copy-start(bf16[160,1024]{1,0:T(8,128)(2,1)} %copy-done.19) | copy-start | bytes 983044
  185.1 42.8 %all-to-all-start.1 = ((bf16[32,40,512]{2,1,0:T(8,128)(2,1)}), bf16[32,40,512]{2,1,0:T(8,128)(2,1)S(1)}, u32[]{:S(2)}, u32[]{:S(2)}) async-start(bf16[32,40,512]{2,1,0:T(8,128)(2,1)} %bitcast.9), calls=%async_computation.1 | async-start | bytes 2621440 | tf_op jit(solution)/shard_map/all_to_all | solution.py:225
  194.5 1.3 copy-start.4
  195.8 1.1 copy-start.36
  202.3 3.1 %copy-start.5 = (bf16[160,2048]{1,0:T(8,128)(2,1)S(1)}, bf16[160,2048]{1,0:T(8,128)(2,1)}, u32[]{:S(2)}) copy-start(bf16[160,2048]{1,0:T(8,128)(2,1)} %shard_map.106.p0) | copy-start | bytes 1966084
  205.4 1.1 copy-start.9
  205.4 1.3 copy-start.11
  206.5 1.1 copy-start.7
  206.7 1.1 copy-start.24
  207.8 3.9 %copy-start.14 = (bf16[640,2048]{1,0:T(8,128)(2,1)}, bf16[640,2048]{1,0:T(8,128)(2,1)S(1)}, u32[]{:S(2)}) copy-start(bf16[640,2048]{1,0:T(8,128)(2,1)S(1)} %constant_dynamic-update-slice_fusion) | copy-start | bytes 7864324
  207.8 4.9 %copy-start.18 = (bf16[160,1024]{1,0:T(8,128)(2,1)S(1)}, bf16[160,1024]{1,0:T(8,128)(2,1)}, u32[]{:S(2)}) copy-start(bf16[160,1024]{1,0:T(8,128)(2,1)} %copy-done.17) | copy-start | bytes 983044
  207.8 4.9 %copy-start.37 = (bf16[640,1024]{1,0:T(8,128)(2,1)S(1)}, bf16[640,1024]{1,0:T(8,128)(2,1)}, u32[]{:S(2)}) copy-start(bf16[640,1024]{1,0:T(8,128)(2,1)} %copy-done.36) | copy-start | bytes 3932164
  207.8 4.9 %copy-start.27 = (bf16[640,512]{1,0:T(8,128)(2,1)S(1)}, bf16[640,512]{1,0:T(8,128)(2,1)}, u32[]{:S(2)}) copy-start(bf16[640,512]{1,0:T(8,128)(2,1)} %copy-done.26) | copy-start | bytes 1966084
  211.7 56.2 %collective-permute-start.21 = (f32[512,2048]{1,0:T(8,128)}, f32[512,2048]{1,0:T(8,128)}, u32[]{:S(2)}, u32[]{:S(2)}) collective-permute-start(f32[512,2048]{1,0:T(8,128)} %fusion.31), channel_id=1, source_target_pairs={{0,1},{1,0},{2,3},{3,2},{4,5},{5,4},{6,7},{7,6},{8,9},{9,8},{10,11... | collective-permute-start | bytes 12582920 | tf_op jit(solution)/shard_map/ppermute | solution.py:23
  212.7 2.4 copy-start.38
  215.1 22.4 %collective-permute-start.22 = (f32[1024,512]{1,0:T(8,128)}, f32[1024,512]{1,0:T(8,128)}, u32[]{:S(2)}, u32[]{:S(2)}) collective-permute-start(f32[1024,512]{1,0:T(8,128)} %fusion.32), channel_id=1, source_target_pairs={{0,1},{1,0},{2,3},{3,2},{4,5},{5,4},{6,7},{7,6},{8,9},{9,8},{10,11... | collective-permute-start | bytes 6291464 | tf_op jit(solution)/shard_map/ppermute | solution.py:23
  227.9 5.6 %copy-start.2 = (bf16[32,40,512]{2,1,0:T(8,128)(2,1)S(1)}, bf16[32,40,512]{2,1,0:T(8,128)(2,1)}, u32[]{:S(2)}) copy-start(bf16[32,40,512]{2,1,0:T(8,128)(2,1)} %copy-done.1) | copy-start | bytes 3932164
  227.9 37.6 %all-to-all-start.3 = ((bf16[32,40,512]{2,1,0:T(8,128)(2,1)}), bf16[32,40,512]{2,1,0:T(8,128)(2,1)}, u32[]{:S(2)}, u32[]{:S(2)}) async-start(bf16[32,40,512]{2,1,0:T(8,128)(2,1)} %bitcast.68), calls=%async_computation.3 | async-start | bytes 2621440 | tf_op jit(solution)/shard_map/all_to_all | solution.py:225
  233.5 1.6 copy-start.12
  235.1 2.4 copy-start.32
  235.1 2.4 copy-start.33
  235.1 2.4 copy-start.34
  235.1 2.4 copy-start.35
  235.6 5.8 %collective-permute-start.18 = (f32[32,40]{1,0:T(8,128)S(1)}, f32[32,40]{1,0:T(8,128)S(1)}, u32[]{:S(2)}, u32[]{:S(2)}) collective-permute-start(f32[32,40]{1,0:T(8,128)S(1)} %reshape.81), channel_id=1, source_target_pairs={{0,1},{1,0},{2,3},{3,2},{4,5},{5,4},{6,7},{7,6},{8,9},{9,8},{10,11... | collective-permute-start | bytes 15368 | tf_op jit(solution)/shard_map/ppermute | solution.py:37
  241.5 3.1 %collective-permute-start.19 = (f32[32,40]{1,0:T(8,128)S(1)}, f32[32,40]{1,0:T(8,128)S(1)}, u32[]{:S(2)}, u32[]{:S(2)}) collective-permute-start(f32[32,40]{1,0:T(8,128)S(1)} %add.157), channel_id=1, source_target_pairs={{0,2},{1,3},{2,0},{3,1},{4,6},{5,7},{6,4},{7,5},{8,10},{9,11},{10,... | collective-permute-start | bytes 15368 | tf_op jit(solution)/shard_map/ppermute | solution.py:37
  244.6 4.5 %collective-permute-start.20 = (f32[32,40]{1,0:T(8,128)S(1)}, f32[32,40]{1,0:T(8,128)S(1)}, u32[]{:S(2)}, u32[]{:S(2)}) collective-permute-start(f32[32,40]{1,0:T(8,128)S(1)} %add.158), channel_id=1, source_target_pairs={{0,4},{1,5},{2,6},{3,7},{4,0},{5,1},{6,2},{7,3},{8,12},{9,13},{10,... | collective-permute-start | bytes 15368 | tf_op jit(solution)/shard_map/ppermute | solution.py:37
  (4 other events, 3.0 us)

commit v3 on v2

--- a/solution.py
+++ b/solution.py
@@ -27,6 +27,10 @@
 
 def dot(a, b):
     return jnp.dot(a, b, preferred_element_type=F32)
+
+
+def dot_t(a, b):
+    return jnp.einsum("rd,fd->rf", a, b, preferred_element_type=F32)
 
 
 def gather_dot(a, b):
@@ -191,6 +195,14 @@
     )
 
 
+def absolute(part, y, n_y):
+    rows = part.shape[0] // n_y
+    return jnp.concatenate(
+        [lax.dynamic_slice_in_dim(part, ((yy - y) % n_y) * rows, rows, 0) for yy in range(n_y)],
+        axis=0,
+    )
+
+
 def both_halves(own, other, core):
     flat = jnp.where(core == 0, jnp.stack([own, other]), jnp.stack([other, own]))
     return flat.reshape(2 * own.shape[0], own.shape[1])
@@ -249,7 +261,6 @@
     gate_up, hidden = hidden_rows(near, got)
     hid_parts = [permute_y(hidden, -d, n_y) for d in range(1, n_y)]
 
-    grad_slab, _ = lax.optimization_barrier((grad_slab, hidden))
     grad_part = permute_core(relative(grad_slab, 1 - core, y, n_y), n_y)
     near, *far = partial_products(grad_slab, grad_part, out_own, out_part, order, True)
     got = send_far(far, n_y)
@@ -264,14 +275,12 @@
     expert_out = both_halves(out_mine, out_other, core)
     out_back = exchange(expert_out)
 
-    gug_parts = gather_rows(gate_up_grad, core, n_y)
-    grad_other = permute_core(spread_product(gug_parts, in_part, places, True), n_y)
-    grad_mine = spread_product(gug_parts, in_own, places, True)
+    gug = jnp.concatenate(gather_rows(gate_up_grad, core, n_y), axis=0)
+    grad_other = permute_core(absolute(dot_t(gug, in_part).astype(BF), y, n_y), n_y)
+    grad_mine = absolute(dot_t(gug, in_own).astype(BF), y, n_y)
     hidden, hid_parts, _ = lax.optimization_barrier((hidden, hid_parts, gate_up_grad))
     hid = jnp.concatenate([hidden] + hid_parts, axis=0)
     choice_grad = both_halves(grad_mine, grad_other, core)
-    gug_parts, _ = lax.optimization_barrier((gug_parts, choice_grad))
-    gug = jnp.concatenate(gug_parts, axis=0)
     grad_back = exchange(choice_grad)
 
     tok_part, tok_own, _ = lax.optimization_barrier((tok_part, tok_own, choice_grad))

time: 278 us -> 284 us (1.022); the launches traced: 274 us -> 283 us
  waiting for transfers between devices: 128 us -> 151 us
  starting transfers between devices: 61.9 us -> 50.9 us
  Pallas kernels: 37.5 us -> 26.7 us
  matrix products: 24.7 us -> 33.5 us
    all_to_all x4, waiting for transfers between devices: 57.2 us -> 92.2 us  [exchange(): lax.all_to_all(v, 'dp', split_axis=0, concat_axis=0, tiled=True)]
    pallas_call x4 -> x2, Pallas kernels: 18.7 us -> 7.94 us  [spread_product(): pl.pallas_call(functools.partial(spread_kernel, turned=turned), grid_spec...]
    ppermute x11, waiting for transfers between devices: 63.1 us -> 54.3 us  [permute_y(): lax.ppermute(v, 'expert', [(2 * y + c, 2 * ((y + step) % n_y) + c) for y...]
    dot_general x0 -> x2, matrix products: none -> 6.39 us  [dot_t(): return jnp.einsum('rd,fd->rf', a, b, preferred_element_type=F32)]
    all_to_all x4, starting transfers between devices: 31.4 us -> 26.8 us  [exchange(): lax.all_to_all(v, 'dp', split_axis=0, concat_axis=0, tiled=True)]
    ppermute x8, waiting for transfers between devices: 3.46 us -> 0.02 us  [permute_core(): lax.ppermute(v, 'expert', [(2 * y + c, 2 * y + 1 - c) for y in range(n_y)...]
    unnamed x88 -> x77, local copies, waits for them, and re-layouts: 11.1 us -> 8.47 us
  transfers between devices with their start and end apart: 27 -> 27, of which waited for: 15 -> 12; matrix products, arithmetic and copies ran while one was open for 9% -> 13% of each run, Pallas kernels for 11% -> 8%
where the time goes in v3:
time: 284 us; the launch traced here: 283 us
  waiting for transfers between devices  151 us (53%)
  starting transfers between devices  50.9 us (18%)
  matrix products  33.5 us (12%)
  Pallas kernels  26.7 us (9%)
  other arithmetic  10.1 us (4%)
  local copies, waits for them, and re-layouts  9.83 us (3%)
    all_to_all x4, waiting for transfers between devices, exchange(): lax.all_to_all(v, 'dp', split_axis=0, concat_axis=0, tiled=True)  92.2 us
    ppermute x11, waiting for transfers between devices, permute_y(): lax.ppermute(v, 'expert', [(2 * y + c, 2 * ((y + step) % n_y) + c) for y...  54.3 us
    all_to_all x4, starting transfers between devices, exchange(): lax.all_to_all(v, 'dp', split_axis=0, concat_axis=0, tiled=True)  26.8 us
    dot_general x7, matrix products, gather_dot(): return jnp.einsum('rd,rf->df', a, b, preferred_element_type=F32)  22.6 us
    ppermute x11, starting transfers between devices, permute_y(): lax.ppermute(v, 'expert', [(2 * y + c, 2 * ((y + step) % n_y) + c) for y...  13.1 us
    pallas_call x2, Pallas kernels, partial_products(): pl.pallas_call(functools.partial(partial_kernel, turned=turned), grid_spe...  12.9 us
    unnamed x77, local copies, waits for them, and re-layouts  8.47 us
    pallas_call x2, Pallas kernels, spread_product(): pl.pallas_call(functools.partial(spread_kernel, turned=turned), grid_spec...  7.94 us
  transfers between devices with their start and end apart: 27, of which 12 were waited for; matrix products, arithmetic and copies ran while one was open for 13% of the time, Pallas kernels for 8%

profile of v3, /device:TPU:33, one launch (start us, length us, event | category | flops | bytes accessed | tf_op | source)
XLA Modules:
  0.0 283.3 jit_solution(3493563429029554961)
XLA Ops:
  0.6 0.7 convert_reduce_fusion
  1.9 2.5 convolution_convert_fusion
  4.3 10.8 %all-to-all-start = ((bf16[32,40,512]{2,1,0:T(8,128)(2,1)}), bf16[32,40,512]{2,1,0:T(8,128)(2,1)S(1)}, u32[]{:S(2)}, u32[]{:S(2)}) async-start(bf16[32,40,512]{2,1,0:T(8,128)(2,1)} %bitcast.3), calls=%async_computation | async-start | bytes 2621440 | tf_op jit(solution)/shard_map/all_to_all | solution.py:237
  16.1 2.0 fusion.32
  18.0 30.2 %all-to-all-done = bf16[32,40,512]{2,1,0:T(8,128)(2,1)S(1)} async-done(((bf16[32,40,512]{2,1,0:T(8,128)(2,1)}), bf16[32,40,512]{2,1,0:T(8,128)(2,1)S(1)}, u32[]{:S(2)}, u32[]{:S(2)}) %all-to-all-start) | async-done | bytes 1310752 | tf_op jit(solution)/shard_map/all_to_all | solution.py:237
  48.2 5.7 %all-to-all-start.2 = ((bf16[32,40,512]{2,1,0:T(8,128)(2,1)}), bf16[32,40,512]{2,1,0:T(8,128)(2,1)S(1)}, u32[]{:S(2)}, u32[]{:S(2)}) async-start(bf16[32,40,512]{2,1,0:T(8,128)(2,1)} %bitcast.65), calls=%async_computation.2 | async-start | bytes 2621440 | tf_op jit(solution)/shard_map/all_to_all | solution.py:237
  54.0 1.8 collective-permute-start.1
  55.8 0.9 pad_maximum_fusion.1
  57.2 28.8 %all-to-all-done.2 = bf16[32,40,512]{2,1,0:T(8,128)(2,1)S(1)} async-done(((bf16[32,40,512]{2,1,0:T(8,128)(2,1)}), bf16[32,40,512]{2,1,0:T(8,128)(2,1)S(1)}, u32[]{:S(2)}, u32[]{:S(2)}) %all-to-all-start.2) | async-done | bytes 1310752 | tf_op jit(solution)/shard_map/all_to_all | solution.py:237
  86.0 1.0 pad_maximum_fusion.2
  87.3 3.1 %collective-permute-start.10 = (bf16[640,512]{1,0:T(8,128)(2,1)}, bf16[640,512]{1,0:T(8,128)(2,1)}, u32[]{:S(2)}, u32[]{:S(2)}) collective-permute-start(bf16[640,512]{1,0:T(8,128)(2,1)} %pad_maximum_fusion.2), channel_id=1, source_target_pairs={{0,1},{1,0},{2,3},{3,2},{4,5},{5,4},{6,7},{7,6},{8,9},{9,8},{10,11... | collective-permute-start | bytes 1966088 | tf_op jit(solution)/shard_map/ppermute | solution.py:23
  90.4 0.8 copy-done.17
  91.2 7.3 %shard_map.101 = (f32[160,2048]{1,0:T(8,128)}, bf16[160,2048]{1,0:T(8,128)(2,1)}, bf16[160,2048]{1,0:T(8,128)(2,1)}, bf16[160,2048]{1,0:T(8,128)(2,1)}) custom-call(s32[4]{0:T(128)} %get-tuple-element.30.order, bf16[1280,512]{1,0:T(8,128)(2,1)} %bitcast.54, bf16[1280,512]{1,0:T(8,128)(2,1)} %bitcast.55, bf16[1280,512]{1,0:T(8,128)(2,1)} %bitcast.56, ...), custom_call_target="tpu_custom_call" | custom-call | tf_op jit(solution)/shard_map/pallas_call | solution.py:70
  98.5 1.3 collective-permute-start.2
  99.8 2.6 collective-permute-start.3
  102.4 1.1 collective-permute-start.4
  103.5 1.0 copy-done.6
  104.4 5.7 %shard_map.105 = (f32[160,1024]{1,0:T(8,128)}, bf16[160,1024]{1,0:T(8,128)(2,1)}, bf16[160,1024]{1,0:T(8,128)(2,1)}, bf16[160,1024]{1,0:T(8,128)(2,1)}) custom-call(s32[4]{0:T(128)} %get-tuple-element.30.order, bf16[1280,512]{1,0:T(8,128)(2,1)} %bitcast.60, bf16[1280,512]{1,0:T(8,128)(2,1)} %bitcast.61, bf16[1280,512]{1,0:T(8,128)(2,1)} %bitcast.62, ...), custom_call_target="tpu_custom_call" | custom-call | tf_op jit(solution)/shard_map/pallas_call | solution.py:70
  110.6 0.8 collective-permute-start.12
  111.3 5.0 %collective-permute-done.2.first = bf16[160,2048]{1,0:T(8,128)(2,1)S(1)} collective-permute-done((bf16[160,2048]{1,0:T(8,128)(2,1)}, bf16[160,2048]{1,0:T(8,128)(2,1)S(1)}, u32[]{:S(2)}, u32[]{:S(2)}) %collective-permute-start.2) | collective-permute-done | bytes 655392 | tf_op jit(solution)/shard_map/ppermute | solution.py:17
  116.3 1.4 collective-permute-start.13
  117.7 13.8 %collective-permute-done.3.second = bf16[160,2048]{1,0:T(8,128)(2,1)S(1)} collective-permute-done((bf16[160,2048]{1,0:T(8,128)(2,1)}, bf16[160,2048]{1,0:T(8,128)(2,1)S(1)}, u32[]{:S(2)}, u32[]{:S(2)}) %collective-permute-start.3) | collective-permute-done | bytes 655392 | tf_op jit(solution)/shard_map/ppermute | solution.py:17
  131.5 0.8 copy-done.25
  132.6 2.9 %shard_map.102 = (f32[160,2048]{1,0:T(8,128)}, bf16[160,1024]{1,0:T(8,128)(2,1)}) custom-call(f32[160,2048]{1,0:T(8,128)} %get-tuple-element.31.near, bf16[160,2048]{1,0:T(8,128)(2,1)} %copy-done.24, bf16[160,2048]{1,0:T(8,128)(2,1)} %copy-done.25, bf16[160,2048]{1,0:T(8,128)(2,1)} %copy-done.26), custom_call_target="tpu_custom_call" | custom-call | tf_op jit(solution)/shard_map/pallas_call | solution.py:137
  135.5 1.8 collective-permute-done.11.first
  137.4 8.2 %collective-permute-done.12.second = bf16[160,1024]{1,0:T(8,128)(2,1)S(1)} collective-permute-done((bf16[160,1024]{1,0:T(8,128)(2,1)}, bf16[160,1024]{1,0:T(8,128)(2,1)S(1)}, u32[]{:S(2)}, u32[]{:S(2)}) %collective-permute-start.12) | collective-permute-done | bytes 327712 | tf_op jit(solution)/shard_map/ppermute | solution.py:17
  145.6 0.7 copy-done.29
  146.4 2.9 %shard_map.106 = bf16[160,2048]{1,0:T(8,128)(2,1)} custom-call(f32[160,1024]{1,0:T(8,128)} %get-tuple-element.37.near, bf16[160,1024]{1,0:T(8,128)(2,1)} %copy-done.27, bf16[160,1024]{1,0:T(8,128)(2,1)} %copy-done.28, bf16[160,1024]{1,0:T(8,128)(2,1)} %copy-done.29, f32[160,2048]{1,0:T(8,128)} %get-tuple-element.41.gate_up), custom_call_target="tpu_custom_call" | custom-call | tf_op jit(solution)/shard_map/pallas_call | solution.py:163
  149.8 2.2 collective-permute-start.14
  152.0 2.1 collective-permute-start.6
  154.1 0.7 collective-permute-start.5
  154.8 0.9 pad_maximum_fusion.4
  155.7 17.5 %collective-permute-done.7.p3 = bf16[160,1024]{1,0:T(8,128)(2,1)S(1)} collective-permute-done((bf16[160,1024]{1,0:T(8,128)(2,1)S(1)}, bf16[160,1024]{1,0:T(8,128)(2,1)S(1)}, u32[]{:S(2)}, u32[]{:S(2)}) %collective-permute-start.7) | collective-permute-done | bytes 327712 | tf_op jit(solution)/shard_map/ppermute | solution.py:17
  173.2 8.0 %collective-permute-done.6.p2 = bf16[160,1024]{1,0:T(8,128)(2,1)S(1)} collective-permute-done((bf16[160,1024]{1,0:T(8,128)(2,1)S(1)}, bf16[160,1024]{1,0:T(8,128)(2,1)S(1)}, u32[]{:S(2)}, u32[]{:S(2)}) %collective-permute-start.6) | collective-permute-done | bytes 327712 | tf_op jit(solution)/shard_map/ppermute | solution.py:17
  181.2 0.7 copy-done.11
  181.9 0.7 copy-done.13
  182.7 4.0 %shard_map.104 = bf16[640,512]{1,0:T(8,128)(2,1)} custom-call(s32[4]{0:T(128)} %get-tuple-element.29.places, bf16[160,1024]{1,0:T(8,128)(2,1)} %get-tuple-element.46.p0, bf16[160,1024]{1,0:T(8,128)(2,1)} %copy-done.13, bf16[160,1024]{1,0:T(8,128)(2,1)} %copy-done.11, bf16[160,1024]{1,0:T(8,128)(2,1)} %copy-done.9, bf16[1024,512]{1,0:T(8,128)(2,1)} %copy-done.6), custom_call_target="tpu_custom_call" | custom-call | tf_op jit(solution)/shard_map/pallas_call | solution.py:108
  186.6 1.4 collective-permute-start.9
  188.0 4.0 %shard_map.103 = bf16[640,512]{1,0:T(8,128)(2,1)} custom-call(s32[4]{0:T(128)} %get-tuple-element.29.places, bf16[160,1024]{1,0:T(8,128)(2,1)} %get-tuple-element.46.p0, bf16[160,1024]{1,0:T(8,128)(2,1)} %copy-done.13, bf16[160,1024]{1,0:T(8,128)(2,1)} %copy-done.11, bf16[160,1024]{1,0:T(8,128)(2,1)} %copy-done.9, bf16[1024,512]{1,0:T(8,128)(2,1)} %bitcast.6.weight.w_own), custom_call_target="tpu_custom_call" | custom-call | tf_op jit(solution)/shard_map/pallas_call | solution.py:108
  192.1 1.5 broadcast_select_fusion
  193.6 1.4 collective-permute-start.16
  195.1 1.0 copy-done.34
  196.1 1.3 maximum_select_fusion
  197.4 4.9 %all-to-all-start.1 = ((bf16[32,40,512]{2,1,0:T(8,128)(2,1)}), bf16[32,40,512]{2,1,0:T(8,128)(2,1)S(1)}, u32[]{:S(2)}, u32[]{:S(2)}) async-start(bf16[32,40,512]{2,1,0:T(8,128)(2,1)} %bitcast.9), calls=%async_computation.1 | async-start | bytes 2621440 | tf_op jit(solution)/shard_map/all_to_all | solution.py:237
  202.3 3.9 %fusion.33 = f32[1024,512]{1,0:T(8,128)} fusion(bf16[640,1024]{1,0:T(8,128)(2,1)} %copy-done.34, bf16[640,512]{1,0:T(8,128)(2,1)} %collective-permute-done.10.part), kind=kOutput, calls=%fused_computation.96 | convolution fusion | flops 671088640 | bytes 4063232 | tf_op jit(solution)/shard_map/rd,rf->df/dot_general | solution.py:37
  206.3 5.1 %fusion.31 = f32[512,2048]{1,0:T(8,128)} fusion(bf16[640,512]{1,0:T(8,128)(2,1)S(1)} %copy-done.18, bf16[160,2048]{1,0:T(8,128)(2,1)S(1)} %copy-done.21, bf16[160,2048]{1,0:T(8,128)(2,1)} %collective-permute-done.16, bf16[160,2048]{1,0:T(8,128)(2,1)} %collective-permute-done.14, bf16[160,2048]{1,0:T(8,128)(2,1)S(1)} %copy-done.19), kind=kOutput, calls=%fused_computation.94 | convolution fusion | flops 1352663040 | bytes 7471104 | tf_op jit(solution)/shard_map/rd,rf->df/dot_general | solution.py:37
  212.0 3.6 %convolution_convert_fusion.1 = bf16[640,512]{1,0:T(8,128)(2,1)S(1)} fusion(bf16[512,2048]{1,0:T(8,128)(2,1)} %collective-permute-done.1.w_part, bf16[160,2048]{1,0:T(8,128)(2,1)S(1)} %copy-done.21, bf16[160,2048]{1,0:T(8,128)(2,1)} %collective-permute-done.16, bf16[160,2048]{1,0:T(8,128)(2,1)} %collective-permute-done.14, bf16[160,2048]{1,0:T(8,128)(2,1)S(1)} %copy-done.19), kind=kOutput, calls=%fused_computation.9 | convolution fusion | flops 1352990720 | bytes 5373952 | tf_op jit(solution)/shard_map/rd,fd->rf/dot_general | solution.py:33
  216.0 1.1 copy-done.16
  217.1 2.8 %convolution_convert_fusion.2 = bf16[640,512]{1,0:T(8,128)(2,1)S(1)} fusion(bf16[1,512,2048]{2,1,0:T(8,128)(2,1)S(1)} %copy-done.16, bf16[160,2048]{1,0:T(8,128)(2,1)S(1)} %copy-done.21, bf16[160,2048]{1,0:T(8,128)(2,1)} %collective-permute-done.16, bf16[160,2048]{1,0:T(8,128)(2,1)} %collective-permute-done.14, bf16[160,2048]{1,0:T(8,128)(2,1)S(1)} %copy-done.19), kind=kOutput, calls=%fused_computation.10 | convolution fusion | flops 1352990720 | bytes 5373952 | tf_op jit(solution)/shard_map/rd,fd->rf/dot_general | solution.py:33
  220.1 1.2 maximum_select_fusion.1
  221.3 14.2 %all-to-all-done.1 = bf16[32,40,512]{2,1,0:T(8,128)(2,1)S(1)} async-done(((bf16[32,40,512]{2,1,0:T(8,128)(2,1)}), bf16[32,40,512]{2,1,0:T(8,128)(2,1)S(1)}, u32[]{:S(2)}, u32[]{:S(2)}) %all-to-all-start.1) | async-done | bytes 1310752 | tf_op jit(solution)/shard_map/all_to_all | solution.py:237
  235.5 5.4 %all-to-all-start.3 = ((bf16[32,40,512]{2,1,0:T(8,128)(2,1)}), bf16[32,40,512]{2,1,0:T(8,128)(2,1)}, u32[]{:S(2)}, u32[]{:S(2)}) async-start(bf16[32,40,512]{2,1,0:T(8,128)(2,1)} %bitcast.66), calls=%async_computation.3 | async-start | bytes 2621440 | tf_op jit(solution)/shard_map/all_to_all | solution.py:237
  241.0 0.8 constant_dynamic-slice_fusion.3
  241.8 0.7 copy-done.5
  243.1 1.0 collective-permute-start.18
  244.1 4.0 %fusion.2 = bf16[1,1024,512]{2,1,0:T(8,128)(2,1)} fusion(f32[1024,512]{1,0:T(8,128)} %collective-permute-done.22, bf16[640,1024]{1,0:T(8,128)(2,1)} %copy-done.34, bf16[160,512]{1,0:T(8,128)(2,1)S(1)} %copy-done.31, bf16[160,512]{1,0:T(8,128)(2,1)S(1)} %copy-done.32, bf16[160,512]{1,0:T(8,128)(2,1)S(1)} %copy-done.33, bf16[160,512]{1,0:T(8,128)(2,1)S(1)} %copy-done.30), kind=kOutput, calls=%fused_computation.8 | convolution fusion | flops 674758656 | bytes 5111808 | tf_op jit(solution)/shard_map/rd,rf->df/dot_general | solution.py:37
  248.5 2.6 collective-permute-done.19
  251.2 1.1 collective-permute-start.20
  252.2 1.0 fusion.5
  253.2 2.1 collective-permute-done.20
  255.7 0.6 divide_bitcast_fusion
  256.3 18.9 %all-to-all-done.3 = bf16[32,40,512]{2,1,0:T(8,128)(2,1)} async-done(((bf16[32,40,512]{2,1,0:T(8,128)(2,1)}), bf16[32,40,512]{2,1,0:T(8,128)(2,1)}, u32[]{:S(2)}, u32[]{:S(2)}) %all-to-all-start.3) | async-done | bytes 1310752 | tf_op jit(solution)/shard_map/all_to_all | solution.py:237
  275.2 2.4 fusion.4
  277.6 5.7 %fusion = bf16[1,512,2048]{2,1,0:T(8,128)(2,1)} fusion(f32[512,2048]{1,0:T(8,128)} %collective-permute-done.21, bf16[640,512]{1,0:T(8,128)(2,1)S(1)} %copy-done.23, bf16[160,2048]{1,0:T(8,128)(2,1)S(1)} %copy-done.22, bf16[160,2048]{1,0:T(8,128)(2,1)} %collective-permute-done.16, bf16[160,2048]{1,0:T(8,128)(2,1)} %collective-permute-done.14, ...), kind=kOutput, calls=%fused_computation.2 | convolution fusion | flops 1354760192 | bytes 9568256 | tf_op jit(solution)/shard_map/rd,rf->df/dot_general | solution.py:37
  (119 shorter events, 6.1 us)
Async XLA Ops:
  0.6 15.4 %copy-start = (bf16[128,512]{1,0:T(8,128)(2,1)S(1)}, bf16[128,512]{1,0:T(8,128)(2,1)}, u32[]{:S(2)}) copy-start(bf16[128,512]{1,0:T(8,128)(2,1)} %param.11) | copy-start | bytes 393220
  4.3 11.3 %copy-start.35 = (f32[128,8]{0,1:T(8,128)S(1)}, f32[128,8]{0,1:T(8,128)}, u32[]{:S(2)}) copy-start(f32[128,8]{0,1:T(8,128)} %param.8) | copy-start | bytes 12292
  4.3 11.3 %copy-start.36 = (s32[128,8]{0,1:T(8,128)S(1)}, s32[128,8]{0,1:T(8,128)}, u32[]{:S(2)}) copy-start(s32[128,8]{0,1:T(8,128)} %param.7) | copy-start | bytes 12292
  4.3 43.9 %all-to-all-start = ((bf16[32,40,512]{2,1,0:T(8,128)(2,1)}), bf16[32,40,512]{2,1,0:T(8,128)(2,1)S(1)}, u32[]{:S(2)}, u32[]{:S(2)}) async-start(bf16[32,40,512]{2,1,0:T(8,128)(2,1)} %bitcast.3), calls=%async_computation | async-start | bytes 2621440 | tf_op jit(solution)/shard_map/all_to_all | solution.py:237
  48.2 7.5 %copy-start.1 = (bf16[32,40,512]{2,1,0:T(8,128)(2,1)}, bf16[32,40,512]{2,1,0:T(8,128)(2,1)S(1)}, u32[]{:S(2)}) copy-start(bf16[32,40,512]{2,1,0:T(8,128)(2,1)S(1)} %all-to-all-done) | copy-start | bytes 3932164
  48.2 37.7 %all-to-all-start.2 = ((bf16[32,40,512]{2,1,0:T(8,128)(2,1)}), bf16[32,40,512]{2,1,0:T(8,128)(2,1)S(1)}, u32[]{:S(2)}, u32[]{:S(2)}) async-start(bf16[32,40,512]{2,1,0:T(8,128)(2,1)} %bitcast.65), calls=%async_computation.2 | async-start | bytes 2621440 | tf_op jit(solution)/shard_map/all_to_all | solution.py:237
  54.0 36.4 %collective-permute-start.1 = (bf16[512,2048]{1,0:T(8,128)(2,1)}, bf16[512,2048]{1,0:T(8,128)(2,1)}, u32[]{:S(2)}, u32[]{:S(2)}) collective-permute-start(bf16[512,2048]{1,0:T(8,128)(2,1)} %bitcast.68), channel_id=1, source_target_pairs={{0,1},{1,0},{2,3},{3,2},{4,5},{5,4},{6,7},{7,6},{8,9},{9,8},{10,11... | collective-permute-start | bytes 6291464 | tf_op jit(solution)/shard_map/ppermute | solution.py:23
  56.7 33.7 %collective-permute-start = (bf16[640,512]{1,0:T(8,128)(2,1)}, bf16[640,512]{1,0:T(8,128)(2,1)S(1)}, u32[]{:S(2)}, u32[]{:S(2)}) collective-permute-start(bf16[640,512]{1,0:T(8,128)(2,1)} %pad_maximum_fusion.1), channel_id=1, source_target_pairs={{0,1},{1,0},{2,3},{3,2},{4,5},{5,4},{6,7},{7,6},{8,9},{9,8},{10,11... | collective-permute-start | bytes 1966088 | tf_op jit(solution)/shard_map/ppermute | solution.py:23
  56.8 46.6 %collective-permute-start.8 = (bf16[1024,512]{1,0:T(8,128)(2,1)}, bf16[1024,512]{1,0:T(8,128)(2,1)S(1)}, u32[]{:S(2)}, u32[]{:S(2)}) collective-permute-start(bf16[1024,512]{1,0:T(8,128)(2,1)} %bitcast.6.weight.w_own), channel_id=1, source_target_pairs={{0,1},{1,0},{2,3},{3,2},{4,5},{5,4},{6,7},{7,6},{8,9},{9,8},{10,11... | collective-permute-start | bytes 3145736 | tf_op jit(solution)/shard_map/ppermute | solution.py:23
  86.0 1.3 copy-start.3
  87.3 16.2 %collective-permute-start.10 = (bf16[640,512]{1,0:T(8,128)(2,1)}, bf16[640,512]{1,0:T(8,128)(2,1)}, u32[]{:S(2)}, u32[]{:S(2)}) collective-permute-start(bf16[640,512]{1,0:T(8,128)(2,1)} %pad_maximum_fusion.2), channel_id=1, source_target_pairs={{0,1},{1,0},{2,3},{3,2},{4,5},{5,4},{6,7},{7,6},{8,9},{9,8},{10,11... | collective-permute-start | bytes 1966088 | tf_op jit(solution)/shard_map/ppermute | solution.py:23
  90.4 0.9 copy-start.17
  98.5 17.8 %collective-permute-start.2 = (bf16[160,2048]{1,0:T(8,128)(2,1)}, bf16[160,2048]{1,0:T(8,128)(2,1)S(1)}, u32[]{:S(2)}, u32[]{:S(2)}) collective-permute-start(bf16[160,2048]{1,0:T(8,128)(2,1)} %get-tuple-element.32), channel_id=1, source_target_pairs={{0,2},{1,3},{2,4},{3,5},{4,6},{5,7},{6,0},{7,1},{8,10},{9,11},{10,... | collective-permute-start | bytes 1966088 | tf_op jit(solution)/shard_map/ppermute | solution.py:17
  99.8 31.7 %collective-permute-start.3 = (bf16[160,2048]{1,0:T(8,128)(2,1)}, bf16[160,2048]{1,0:T(8,128)(2,1)S(1)}, u32[]{:S(2)}, u32[]{:S(2)}) collective-permute-start(bf16[160,2048]{1,0:T(8,128)(2,1)} %get-tuple-element.33), channel_id=1, source_target_pairs={{0,4},{1,5},{2,6},{3,7},{4,0},{5,1},{6,2},{7,3},{8,12},{9,13},{10,... | collective-permute-start | bytes 1966088 | tf_op jit(solution)/shard_map/ppermute | solution.py:17
  102.4 29.1 %collective-permute-start.4 = (bf16[160,2048]{1,0:T(8,128)(2,1)}, bf16[160,2048]{1,0:T(8,128)(2,1)S(1)}, u32[]{:S(2)}, u32[]{:S(2)}) collective-permute-start(bf16[160,2048]{1,0:T(8,128)(2,1)} %get-tuple-element.34), channel_id=1, source_target_pairs={{0,6},{1,7},{2,0},{3,1},{4,2},{5,3},{6,4},{7,5},{8,14},{9,15},{10,... | collective-permute-start | bytes 1966088 | tf_op jit(solution)/shard_map/ppermute | solution.py:17
  103.5 1.0 copy-start.6
  110.1 27.3 %collective-permute-start.11 = (bf16[160,1024]{1,0:T(8,128)(2,1)}, bf16[160,1024]{1,0:T(8,128)(2,1)S(1)}, u32[]{:S(2)}, u32[]{:S(2)}) collective-permute-start(bf16[160,1024]{1,0:T(8,128)(2,1)} %get-tuple-element.38), channel_id=1, source_target_pairs={{0,2},{1,3},{2,4},{3,5},{4,6},{5,7},{6,0},{7,1},{8,10},{9,11},{10,... | collective-permute-start | bytes 983048 | tf_op jit(solution)/shard_map/ppermute | solution.py:17
  110.6 35.0 %collective-permute-start.12 = (bf16[160,1024]{1,0:T(8,128)(2,1)}, bf16[160,1024]{1,0:T(8,128)(2,1)S(1)}, u32[]{:S(2)}, u32[]{:S(2)}) collective-permute-start(bf16[160,1024]{1,0:T(8,128)(2,1)} %get-tuple-element.39), channel_id=1, source_target_pairs={{0,4},{1,5},{2,6},{3,7},{4,0},{5,1},{6,2},{7,3},{8,12},{9,13},{10,... | collective-permute-start | bytes 983048 | tf_op jit(solution)/shard_map/ppermute | solution.py:17
  116.3 15.2 %copy-start.24 = (bf16[160,2048]{1,0:T(8,128)(2,1)}, bf16[160,2048]{1,0:T(8,128)(2,1)S(1)}, u32[]{:S(2)}) copy-start(bf16[160,2048]{1,0:T(8,128)(2,1)S(1)} %collective-permute-done.2.first) | copy-start | bytes 1966084
  116.3 29.2 %collective-permute-start.13 = (bf16[160,1024]{1,0:T(8,128)(2,1)}, bf16[160,1024]{1,0:T(8,128)(2,1)S(1)}, u32[]{:S(2)}, u32[]{:S(2)}) collective-permute-start(bf16[160,1024]{1,0:T(8,128)(2,1)} %get-tuple-element.40), channel_id=1, source_target_pairs={{0,6},{1,7},{2,0},{3,1},{4,2},{5,3},{6,4},{7,5},{8,14},{9,15},{10,... | collective-permute-start | bytes 983048 | tf_op jit(solution)/shard_map/ppermute | solution.py:17
  131.5 0.9 copy-start.25
  131.5 1.1 copy-start.26
  137.4 8.9 %copy-start.27 = (bf16[160,1024]{1,0:T(8,128)(2,1)}, bf16[160,1024]{1,0:T(8,128)(2,1)S(1)}, u32[]{:S(2)}) copy-start(bf16[160,1024]{1,0:T(8,128)(2,1)S(1)} %collective-permute-done.11.first) | copy-start | bytes 983044
  145.6 0.9 copy-start.28
  145.6 0.7 copy-start.29
  146.4 5.6 %copy-start.7 = (bf16[160,1024]{1,0:T(8,128)(2,1)S(1)}, bf16[160,1024]{1,0:T(8,128)(2,1)}, u32[]{:S(2)}) copy-start(bf16[160,1024]{1,0:T(8,128)(2,1)} %get-tuple-element.46.p0) | copy-start | bytes 983044
  146.4 8.4 %copy-start.2 = (bf16[32,40,512]{2,1,0:T(8,128)(2,1)S(1)}, bf16[32,40,512]{2,1,0:T(8,128)(2,1)}, u32[]{:S(2)}) copy-start(bf16[32,40,512]{2,1,0:T(8,128)(2,1)} %copy-done.1) | copy-start | bytes 3932164
  149.3 42.7 %collective-permute-start.15 = (bf16[160,2048]{1,0:T(8,128)(2,1)}, bf16[160,2048]{1,0:T(8,128)(2,1)S(1)}, u32[]{:S(2)}, u32[]{:S(2)}) collective-permute-start(bf16[160,2048]{1,0:T(8,128)(2,1)} %shard_map.106), channel_id=1, source_target_pairs={{0,2},{1,3},{2,4},{3,5},{4,6},{5,7},{6,0},{7,1},{8,10},{9,11},{10,... | collective-permute-start | bytes 1966088 | tf_op jit(solution)/shard_map/ppermute | solution.py:17
  149.8 42.3 %collective-permute-start.14 = (bf16[160,2048]{1,0:T(8,128)(2,1)}, bf16[160,2048]{1,0:T(8,128)(2,1)}, u32[]{:S(2)}, u32[]{:S(2)}) collective-permute-start(bf16[160,2048]{1,0:T(8,128)(2,1)} %shard_map.106), channel_id=1, source_target_pairs={{0,6},{1,7},{2,0},{3,1},{4,2},{5,3},{6,4},{7,5},{8,14},{9,15},{10,... | collective-permute-start | bytes 1966088 | tf_op jit(solution)/shard_map/ppermute | solution.py:17
  152.0 21.2 %collective-permute-start.7 = (bf16[160,1024]{1,0:T(8,128)(2,1)S(1)}, bf16[160,1024]{1,0:T(8,128)(2,1)S(1)}, u32[]{:S(2)}, u32[]{:S(2)}) collective-permute-start(bf16[160,1024]{1,0:T(8,128)(2,1)S(1)} %copy-done.7), channel_id=1, source_target_pairs={{0,2},{1,3},{2,4},{3,5},{4,6},{5,7},{6,0},{7,1},{8,10},{9,11},{10,... | collective-permute-start | bytes 983048 | tf_op jit(solution)/shard_map/ppermute | solution.py:17
  152.0 29.2 %collective-permute-start.6 = (bf16[160,1024]{1,0:T(8,128)(2,1)S(1)}, bf16[160,1024]{1,0:T(8,128)(2,1)S(1)}, u32[]{:S(2)}, u32[]{:S(2)}) collective-permute-start(bf16[160,1024]{1,0:T(8,128)(2,1)S(1)} %copy-done.7), channel_id=1, source_target_pairs={{0,4},{1,5},{2,6},{3,7},{4,0},{5,1},{6,2},{7,3},{8,12},{9,13},{10,... | collective-permute-start | bytes 983048 | tf_op jit(solution)/shard_map/ppermute | solution.py:17
  154.1 27.1 %collective-permute-start.5 = (bf16[160,1024]{1,0:T(8,128)(2,1)S(1)}, bf16[160,1024]{1,0:T(8,128)(2,1)S(1)}, u32[]{:S(2)}, u32[]{:S(2)}) collective-permute-start(bf16[160,1024]{1,0:T(8,128)(2,1)S(1)} %copy-done.7), channel_id=1, source_target_pairs={{0,6},{1,7},{2,0},{3,1},{4,2},{5,3},{6,4},{7,5},{8,14},{9,15},{10,... | collective-permute-start | bytes 983048 | tf_op jit(solution)/shard_map/ppermute | solution.py:17
  173.2 8.0 %copy-start.9 = (bf16[160,1024]{1,0:T(8,128)(2,1)}, bf16[160,1024]{1,0:T(8,128)(2,1)S(1)}, u32[]{:S(2)}) copy-start(bf16[160,1024]{1,0:T(8,128)(2,1)S(1)} %collective-permute-done.7.p3) | copy-start | bytes 983044
  181.2 0.7 copy-start.11
  181.9 0.7 copy-start.13
  186.6 5.3 %copy-start.8 = (bf16[160,1024]{1,0:T(8,128)(2,1)S(1)}, bf16[160,1024]{1,0:T(8,128)(2,1)}, u32[]{:S(2)}) copy-start(bf16[160,1024]{1,0:T(8,128)(2,1)} %get-tuple-element.46.p0) | copy-start | bytes 983044
  186.6 5.4 %copy-start.14 = (bf16[160,1024]{1,0:T(8,128)(2,1)S(1)}, bf16[160,1024]{1,0:T(8,128)(2,1)}, u32[]{:S(2)}) copy-start(bf16[160,1024]{1,0:T(8,128)(2,1)} %copy-done.13) | copy-start | bytes 983044
  186.6 8.4 %collective-permute-start.9 = (bf16[640,512]{1,0:T(8,128)(2,1)}, bf16[640,512]{1,0:T(8,128)(2,1)S(1)}, u32[]{:S(2)}, u32[]{:S(2)}) collective-permute-start(bf16[640,512]{1,0:T(8,128)(2,1)} %shard_map.104), channel_id=1, source_target_pairs={{0,1},{1,0},{2,3},{3,2},{4,5},{5,4},{6,7},{7,6},{8,9},{9,8},{10,11... | collective-permute-start | bytes 1966088 | tf_op jit(solution)/shard_map/ppermute | solution.py:23
  192.0 3.0 %copy-start.12 = (bf16[160,1024]{1,0:T(8,128)(2,1)S(1)}, bf16[160,1024]{1,0:T(8,128)(2,1)}, u32[]{:S(2)}) copy-start(bf16[160,1024]{1,0:T(8,128)(2,1)} %copy-done.11) | copy-start | bytes 983044
  192.0 3.0 %copy-start.10 = (bf16[160,1024]{1,0:T(8,128)(2,1)S(1)}, bf16[160,1024]{1,0:T(8,128)(2,1)}, u32[]{:S(2)}) copy-start(bf16[160,1024]{1,0:T(8,128)(2,1)} %copy-done.9) | copy-start | bytes 983044
  192.1 4.1 %copy-start.15 = (bf16[640,512]{1,0:T(8,128)(2,1)S(1)}, bf16[640,512]{1,0:T(8,128)(2,1)}, u32[]{:S(2)}) copy-start(bf16[640,512]{1,0:T(8,128)(2,1)} %shard_map.103) | copy-start | bytes 1966084
  192.1 2.9 %copy-start.20 = (bf16[160,2048]{1,0:T(8,128)(2,1)}, bf16[160,2048]{1,0:T(8,128)(2,1)S(1)}, u32[]{:S(2)}) copy-start(bf16[160,2048]{1,0:T(8,128)(2,1)S(1)} %collective-permute-done.15) | copy-start | bytes 1966084
  193.6 12.7 %collective-permute-start.16 = (bf16[160,2048]{1,0:T(8,128)(2,1)S(1)}, bf16[160,2048]{1,0:T(8,128)(2,1)}, u32[]{:S(2)}, u32[]{:S(2)}) collective-permute-start(bf16[160,2048]{1,0:T(8,128)(2,1)S(1)} %broadcast_select_fusion), channel_id=1, source_target_pairs={{0,2},{1,7},{2,4},{3,1},{4,6},{5,3},{6,0},{7,5},{8,10},{9,15},{10,... | collective-permute-start | bytes 1966088 | tf_op jit(solution)/shard_map/ppermute | solution.py:173
  195.1 1.1 copy-start.34
  197.4 38.1 %all-to-all-start.1 = ((bf16[32,40,512]{2,1,0:T(8,128)(2,1)}), bf16[32,40,512]{2,1,0:T(8,128)(2,1)S(1)}, u32[]{:S(2)}, u32[]{:S(2)}) async-start(bf16[32,40,512]{2,1,0:T(8,128)(2,1)} %bitcast.9), calls=%async_computation.1 | async-start | bytes 2621440 | tf_op jit(solution)/shard_map/all_to_all | solution.py:237
  202.3 4.0 %copy-start.18 = (bf16[640,512]{1,0:T(8,128)(2,1)S(1)}, bf16[640,512]{1,0:T(8,128)(2,1)}, u32[]{:S(2)}) copy-start(bf16[640,512]{1,0:T(8,128)(2,1)} %copy-done.17) | copy-start | bytes 1966084
  202.3 4.0 %copy-start.19 = (bf16[160,2048]{1,0:T(8,128)(2,1)S(1)}, bf16[160,2048]{1,0:T(8,128)(2,1)}, u32[]{:S(2)}) copy-start(bf16[160,2048]{1,0:T(8,128)(2,1)} %shard_map.106) | copy-start | bytes 1966084
  202.3 4.0 %copy-start.21 = (bf16[160,2048]{1,0:T(8,128)(2,1)S(1)}, bf16[160,2048]{1,0:T(8,128)(2,1)}, u32[]{:S(2)}) copy-start(bf16[160,2048]{1,0:T(8,128)(2,1)} %copy-done.20) | copy-start | bytes 1966084
  206.3 37.8 %collective-permute-start.22 = (f32[1024,512]{1,0:T(8,128)}, f32[1024,512]{1,0:T(8,128)}, u32[]{:S(2)}, u32[]{:S(2)}) collective-permute-start(f32[1024,512]{1,0:T(8,128)} %fusion.33), channel_id=1, source_target_pairs={{0,1},{1,0},{2,3},{3,2},{4,5},{5,4},{6,7},{7,6},{8,9},{9,8},{10,11... | collective-permute-start | bytes 6291464 | tf_op jit(solution)/shard_map/ppermute | solution.py:23
  211.5 66.1 %collective-permute-start.21 = (f32[512,2048]{1,0:T(8,128)}, f32[512,2048]{1,0:T(8,128)}, u32[]{:S(2)}, u32[]{:S(2)}) collective-permute-start(f32[512,2048]{1,0:T(8,128)} %fusion.31), channel_id=1, source_target_pairs={{0,1},{1,0},{2,3},{3,2},{4,5},{5,4},{6,7},{7,6},{8,9},{9,8},{10,11... | collective-permute-start | bytes 12582920 | tf_op jit(solution)/shard_map/ppermute | solution.py:23
  215.5 1.6 copy-start.16
  215.6 4.4 %collective-permute-start.17 = (bf16[640,512]{1,0:T(8,128)(2,1)S(1)}, bf16[640,512]{1,0:T(8,128)(2,1)S(1)}, u32[]{:S(2)}, u32[]{:S(2)}) collective-permute-start(bf16[640,512]{1,0:T(8,128)(2,1)S(1)} %pad_maximum_fusion.3), channel_id=1, source_target_pairs={{0,1},{1,0},{2,3},{3,2},{4,5},{5,4},{6,7},{7,6},{8,9},{9,8},{10,11... | collective-permute-start | bytes 1966088 | tf_op jit(solution)/shard_map/ppermute | solution.py:23
  235.5 5.4 %copy-start.4 = (bf16[32,40,512]{2,1,0:T(8,128)(2,1)S(1)}, bf16[32,40,512]{2,1,0:T(8,128)(2,1)}, u32[]{:S(2)}) copy-start(bf16[32,40,512]{2,1,0:T(8,128)(2,1)} %copy-done.3) | copy-start | bytes 3932164
  235.5 39.6 %all-to-all-start.3 = ((bf16[32,40,512]{2,1,0:T(8,128)(2,1)}), bf16[32,40,512]{2,1,0:T(8,128)(2,1)}, u32[]{:S(2)}, u32[]{:S(2)}) async-start(bf16[32,40,512]{2,1,0:T(8,128)(2,1)} %bitcast.66), calls=%async_computation.3 | async-start | bytes 2621440 | tf_op jit(solution)/shard_map/all_to_all | solution.py:237
  241.0 1.6 copy-start.5
  242.5 1.5 copy-start.30
  242.5 1.5 copy-start.31
  242.5 1.5 copy-start.32
  242.5 1.5 copy-start.33
  243.1 5.0 %collective-permute-start.18 = (f32[32,40]{1,0:T(8,128)S(1)}, f32[32,40]{1,0:T(8,128)S(1)}, u32[]{:S(2)}, u32[]{:S(2)}) collective-permute-start(f32[32,40]{1,0:T(8,128)S(1)} %reshape.77), channel_id=1, source_target_pairs={{0,1},{1,0},{2,3},{3,2},{4,5},{5,4},{6,7},{7,6},{8,9},{9,8},{10,11... | collective-permute-start | bytes 15368 | tf_op jit(solution)/shard_map/ppermute | solution.py:41
  248.1 3.1 %collective-permute-start.19 = (f32[32,40]{1,0:T(8,128)S(1)}, f32[32,40]{1,0:T(8,128)S(1)}, u32[]{:S(2)}, u32[]{:S(2)}) collective-permute-start(f32[32,40]{1,0:T(8,128)S(1)} %add.197), channel_id=1, source_target_pairs={{0,2},{1,3},{2,0},{3,1},{4,6},{5,7},{6,4},{7,5},{8,10},{9,11},{10,... | collective-permute-start | bytes 15368 | tf_op jit(solution)/shard_map/ppermute | solution.py:41
  251.1 26.4 %copy-start.22 = (bf16[160,2048]{1,0:T(8,128)(2,1)S(1)}, bf16[160,2048]{1,0:T(8,128)(2,1)}, u32[]{:S(2)}) copy-start(bf16[160,2048]{1,0:T(8,128)(2,1)} %copy-done.20) | copy-start | bytes 1966084
  251.1 26.4 %copy-start.23 = (bf16[640,512]{1,0:T(8,128)(2,1)S(1)}, bf16[640,512]{1,0:T(8,128)(2,1)}, u32[]{:S(2)}) copy-start(bf16[640,512]{1,0:T(8,128)(2,1)} %pad_maximum_fusion.4) | copy-start | bytes 1966084
  251.2 4.2 %collective-permute-start.20 = (f32[32,40]{1,0:T(8,128)S(1)}, f32[32,40]{1,0:T(8,128)S(1)}, u32[]{:S(2)}, u32[]{:S(2)}) collective-permute-start(f32[32,40]{1,0:T(8,128)S(1)} %add.198), channel_id=1, source_target_pairs={{0,4},{1,5},{2,6},{3,7},{4,0},{5,1},{6,2},{7,3},{8,12},{9,13},{10,... | collective-permute-start | bytes 15368 | tf_op jit(solution)/shard_map/ppermute | solution.py:41

commit v4 on v3

--- a/solution.py
+++ b/solution.py
@@ -15,7 +15,9 @@
 
 def permute_y(v, step, n_y):
     return lax.ppermute(
-        v, "expert", [(2 * y + c, 2 * ((y + step) % n_y) + c) for y in range(n_y) for c in range(2)]
+        v,
+        "expert",
+        [(2 * y + c, 2 * ((y + (2 * c - 1) * step) % n_y) + c) for y in range(n_y) for c in range(2)],
     )
 
 
@@ -81,67 +83,65 @@
     )(order, slab, slab, slab, slab, part, w_own, w_part)
 
 
-def spread_kernel(places, p0, p1, p2, p3, weight, out, held, *, turned):
-    rows = p0.shape[0]
-
-    @pl.when(pl.program_id(0) == 0)
-    def _():
-        for d, piece in enumerate((p0, p1, p2, p3)):
-            held[d * rows : (d + 1) * rows, :] = piece[...]
-
-    contract = (((1,), (1 if turned else 0,)), ((), ()))
-    total = lax.dot_general(held[...], weight[...], contract, preferred_element_type=F32).astype(BF)
-    for d in range(4):
-        start = pl.multiple_of(places[d] * rows, rows)
-        out[pl.ds(start, rows), :] = total[d * rows : (d + 1) * rows]
-
-
-def spread_product(pieces, weight, places, turned):
-    rows, k = pieces[0].shape
-    width = weight.shape[0] if turned else weight.shape[1]
-    chunk = width // 2
-    piece = pl.BlockSpec((rows, k), lambda j, places: (0, 0))
-    if turned:
-        w_spec = pl.BlockSpec((chunk, k), lambda j, places: (j, 0))
-    else:
-        w_spec = pl.BlockSpec((k, chunk), lambda j, places: (0, j))
+def halves_kernel(order, own0, own1, own2, own3, part, w_own, w_part, near, *far):
+    rows = near.shape[0]
+    half = rows // 2
+    own = jnp.concatenate([own0[...], own1[...], own2[...], own3[...]], axis=0)
+    total = jnp.dot(own, w_own[...], preferred_element_type=F32)
+    total = total + jnp.dot(part[...], w_part[...], preferred_element_type=F32)
+    near[...] = total[:rows]
+    for k, out in enumerate(far):
+        out[...] = total[rows + k * half : rows + (k + 1) * half].astype(out.dtype)
+
+
+def partial_halves(slab, part, w_own, w_part, order):
+    n_y = order.shape[0]
+    rows = part.shape[0] // n_y
+    k = slab.shape[1]
+    width = w_own.shape[1]
+    chunk = width // 4
+
+    def rows_of(d):
+        return pl.BlockSpec((rows, k), lambda j, order: (order[d], 0))
+
+    weight = pl.BlockSpec((k, chunk), lambda j, order: (0, j))
+    half = pl.BlockSpec((rows // 2, chunk), lambda j, order: (0, j))
+    kinds = [F32, BF, BF, BF, BF, F32]
     return pl.pallas_call(
-        functools.partial(spread_kernel, turned=turned),
+        halves_kernel,
         grid_spec=pltpu.PrefetchScalarGridSpec(
             num_scalar_prefetch=1,
-            grid=(2,),
-            in_specs=[piece, piece, piece, piece, w_spec],
-            out_specs=pl.BlockSpec((4 * rows, chunk), lambda j, places: (0, j)),
-            scratch_shapes=[pltpu.VMEM((4 * rows, k), BF)],
+            grid=(width // chunk,),
+            in_specs=[rows_of(d) for d in range(4)]
+            + [pl.BlockSpec(part.shape, lambda j, order: (0, 0)), weight, weight],
+            out_specs=[pl.BlockSpec((rows, chunk), lambda j, order: (0, j))] + [half] * 6,
         ),
-        out_shape=jax.ShapeDtypeStruct((4 * rows, width), BF),
-    )(places, *pieces, weight)
+        out_shape=[jax.ShapeDtypeStruct((rows, width), F32)]
+        + [jax.ShapeDtypeStruct((rows // 2, width), kind) for kind in kinds],
+    )(order, slab, slab, slab, slab, part, w_own, w_part)
 
 
 def send_far(far, n_y):
     return [permute_y(piece, d + 1, n_y) for d, piece in enumerate(far)]
 
 
-def hidden_kernel(near, first, second, third, gate_up, hidden):
-    width = hidden.shape[1]
-    total = near[...] + first[...].astype(F32) + second[...].astype(F32) + third[...].astype(F32)
-    gate_up[...] = total
-    gate, up = total[:, :width], total[:, width:]
-    hidden[...] = (gate * jax.nn.sigmoid(gate) * up).astype(BF)
+def hidden_kernel(near, up_a, dn_a, up_b, dn_b, gate_up, hidden):
+    half, width = up_a.shape
+    for k, (up, dn) in enumerate(((up_a, dn_a), (up_b, dn_b))):
+        rows = pl.ds(k * half, half)
+        total = near[rows, :] + up[...].astype(F32) + dn[...].astype(F32)
+        gate_up[rows, :] = total
+        gate, upward = total[:, : width // 2], total[:, width // 2 :]
+        hidden[rows, :] = gate * jax.nn.sigmoid(gate) * upward
 
 
 def hidden_rows(near, got):
     rows, width = near.shape
-    tile = rows // 2
-    wide = pl.BlockSpec((tile, width), lambda i: (i, 0))
     return pl.pallas_call(
         hidden_kernel,
-        grid=(2,),
-        in_specs=[wide, wide, wide, wide],
-        out_specs=[wide, pl.BlockSpec((tile, width // 2), lambda i: (i, 0))],
         out_shape=[
             jax.ShapeDtypeStruct((rows, width), F32),
-            jax.ShapeDtypeStruct((rows, width // 2), BF),
+            jax.ShapeDtypeStruct((rows, width // 2), F32),
         ],
     )(near, *got)
 
@@ -169,36 +169,28 @@
     )(near, *got, gate_up)
 
 
-def permute_by_core(v, n_y):
-    return lax.ppermute(
-        v,
-        "expert",
-        [(2 * y + c, 2 * ((y + 1 - 2 * c) % n_y) + c) for y in range(n_y) for c in range(2)],
-    )
-
-
-def gather_rows(v, core, n_y):
-    dn = permute_y(v, 1, n_y)
-    up = permute_y(v, -1, n_y)
-    far = permute_by_core(jnp.where(core == 0, dn, up), n_y)
-    return [v, up, far, dn]
+def gather_rows(v, n_y):
+    first = permute_y(v, -1, n_y)
+    far = permute_y(first, -1, n_y)
+    last = permute_y(v, 1, n_y)
+    return [v, first, far, last]
 
 
 def relative(slab, half, y, n_y):
     rows = slab.shape[0] // (2 * n_y)
     return jnp.concatenate(
         [
-            lax.dynamic_slice_in_dim(slab, (half * n_y + (y + d) % n_y) * rows, rows, 0)
+            lax.dynamic_slice_in_dim(slab, (half * n_y + (y + (2 * half - 1) * d) % n_y) * rows, rows, 0)
             for d in range(n_y)
         ],
         axis=0,
     )
 
 
-def absolute(part, y, n_y):
+def absolute(part, y, core, n_y):
     rows = part.shape[0] // n_y
     return jnp.concatenate(
-        [lax.dynamic_slice_in_dim(part, ((yy - y) % n_y) * rows, rows, 0) for yy in range(n_y)],
+        [lax.dynamic_slice_in_dim(part, (((2 * core - 1) * (yy - y)) % n_y) * rows, rows, 0) for yy in range(n_y)],
         axis=0,
     )
 
@@ -241,7 +233,7 @@
     in_part = permute_core(in_own, n_y)
     out_part = permute_core(out_own, n_y)
 
-    places = lax.rem(y + jnp.arange(n_y, dtype=jnp.int32), n_y)
+    places = lax.rem(y + n_y + (2 * core - 1) * jnp.arange(n_y, dtype=jnp.int32), n_y)
     order = core * n_y + places
     scores_t, places, order, _ = lax.optimization_barrier((scores_t, places, order, token_send))
     score_total = jnp.sum(scores_t, axis=0, keepdims=True)
@@ -256,11 +248,21 @@
 
     token_slab, _ = lax.optimization_barrier((token_slab, grad_send[:8]))
     tok_part = permute_core(relative(token_slab, 1 - core, y, n_y), n_y)
-    near, *far = partial_products(token_slab, tok_part, in_own, in_part, order, False)
-    got = send_far(far, n_y)
+    near, *far = partial_halves(token_slab, tok_part, in_own, in_part, order)
+    up_2 = permute_y(far[2], 1, n_y)
+    dn_2 = permute_y(far[3], -1, n_y)
+    up_b = permute_y(far[1], 1, n_y)
+    dn_a = permute_y(far[4], -1, n_y)
+    up_1 = (far[0] + up_2.astype(F32)).astype(BF)
+    dn_3 = (far[5] + dn_2.astype(F32)).astype(BF)
+    up_a = permute_y(up_1, 1, n_y)
+    dn_b = permute_y(dn_3, -1, n_y)
+    got = [up_a, dn_a, up_b, dn_b]
     gate_up, hidden = hidden_rows(near, got)
+    hidden = hidden.astype(BF)
     hid_parts = [permute_y(hidden, -d, n_y) for d in range(1, n_y)]
 
+    grad_slab, _ = lax.optimization_barrier((grad_slab, up_1))
     grad_part = permute_core(relative(grad_slab, 1 - core, y, n_y), n_y)
     near, *far = partial_products(grad_slab, grad_part, out_own, out_part, order, True)
     got = send_far(far, n_y)
@@ -270,16 +272,17 @@
     token_slab, _ = lax.optimization_barrier((token_slab, gate_up_grad))
     tok_own = relative(token_slab, core, y, n_y)
 
-    out_other = permute_core(spread_product([hidden] + hid_parts, out_part, places, False), n_y)
-    out_mine = spread_product([hidden] + hid_parts, out_own, places, False)
+    hid = jnp.concatenate([hidden] + hid_parts, axis=0)
+    out_other = permute_core(absolute(dot(hid, out_part).astype(BF), y, core, n_y), n_y)
+    out_mine = absolute(dot(hid, out_own).astype(BF), y, core, n_y)
     expert_out = both_halves(out_mine, out_other, core)
     out_back = exchange(expert_out)
 
-    gug = jnp.concatenate(gather_rows(gate_up_grad, core, n_y), axis=0)
-    grad_other = permute_core(absolute(dot_t(gug, in_part).astype(BF), y, n_y), n_y)
-    grad_mine = absolute(dot_t(gug, in_own).astype(BF), y, n_y)
-    hidden, hid_parts, _ = lax.optimization_barrier((hidden, hid_parts, gate_up_grad))
-    hid = jnp.concatenate([hidden] + hid_parts, axis=0)
+    gug = jnp.concatenate(gather_rows(gate_up_grad, n_y), axis=0)
+    other_rows = absolute(dot_t(gug, in_part).astype(BF), y, core, n_y)
+    grad_other = permute_core(other_rows, n_y)
+    in_late, _ = lax.optimization_barrier((in_own, other_rows))
+    grad_mine = absolute(dot_t(gug, in_late).astype(BF), y, core, n_y)
     choice_grad = both_halves(grad_mine, grad_other, core)
     grad_back = exchange(choice_grad)
 

time: 284 us -> 244 us (0.86)
  the two profiles are of different devices: /device:TPU:33 before, /device:TPU:32 now
where the time goes in v4:
time: 244 us; the launch traced here: 242 us
  waiting for transfers between devices  110 us (45%)
  starting transfers between devices  53.8 us (22%)
  matrix products  38.9 us (16%)
  Pallas kernels  19 us (8%)
  other arithmetic  10.9 us (4%)
  local copies, waits for them, and re-layouts  8.57 us (4%)
    all_to_all x4, waiting for transfers between devices, exchange(): lax.all_to_all(v, 'dp', split_axis=0, concat_axis=0, tiled=True)  65.4 us
    ppermute x15, waiting for transfers between devices, permute_y(): lax.ppermute(v, 'expert', [(2 * y + c, 2 * ((y + (2 * c - 1) * step) % n_...  34.8 us
    all_to_all x4, starting transfers between devices, exchange(): lax.all_to_all(v, 'dp', split_axis=0, concat_axis=0, tiled=True)  29 us
    ppermute x15, starting transfers between devices, permute_y(): lax.ppermute(v, 'expert', [(2 * y + c, 2 * ((y + (2 * c - 1) * step) % n_...  22.8 us
    dot_general x7, matrix products, gather_dot(): return jnp.einsum('rd,rf->df', a, b, preferred_element_type=F32)  22.5 us
    dot_general x5, matrix products, dot(): return jnp.dot(a, b, preferred_element_type=F32)  8.94 us
    ppermute x3, waiting for transfers between devices, permute_xor(): return lax.ppermute(v, 'expert', [(e, e ^ bit) for e in range(2 * n_y)])  7.55 us
    dot_general x2, matrix products, dot_t(): return jnp.einsum('rd,fd->rf', a, b, preferred_element_type=F32)  7.5 us
  transfers between devices with their start and end apart: 30, of which 14 were waited for; matrix products, arithmetic and copies ran while one was open for 17% of the time, Pallas kernels for 7%

profile of v4, /device:TPU:32, one launch (start us, length us, event | category | flops | bytes accessed | tf_op | source)
XLA Modules:
  0.0 242.3 jit_solution(7584022803576493931)
XLA Ops:
  0.6 0.7 convert_reduce_fusion
  1.9 2.5 %convolution_convert_fusion = bf16[1280,512]{1,0:T(8,128)(2,1)} fusion(pred[1280,128]{1,0:T(32,128)(4,1)S(1)} %bitcast_compare_fusion, bf16[128,512]{1,0:T(8,128)(2,1)} %param.6), kind=kOutput, calls=%fused_computation.1 | convolution fusion | flops 168427520 | bytes 1605632 | tf_op jit(solution)/shard_map/dot_general | solution.py:31
  4.3 11.3 %all-to-all-start = ((bf16[32,40,512]{2,1,0:T(8,128)(2,1)}), bf16[32,40,512]{2,1,0:T(8,128)(2,1)S(1)}, u32[]{:S(2)}, u32[]{:S(2)}) async-start(bf16[32,40,512]{2,1,0:T(8,128)(2,1)} %bitcast.3), calls=%async_computation | async-start | bytes 2621440 | tf_op jit(solution)/shard_map/all_to_all | solution.py:229
  15.8 0.5 broadcast_add_fusion
  16.7 2.0 fusion.33
  18.7 30.9 %all-to-all-done = bf16[32,40,512]{2,1,0:T(8,128)(2,1)S(1)} async-done(((bf16[32,40,512]{2,1,0:T(8,128)(2,1)}), bf16[32,40,512]{2,1,0:T(8,128)(2,1)S(1)}, u32[]{:S(2)}, u32[]{:S(2)}) %all-to-all-start) | async-done | bytes 1310752 | tf_op jit(solution)/shard_map/all_to_all | solution.py:229
  49.6 5.4 %all-to-all-start.2 = ((bf16[32,40,512]{2,1,0:T(8,128)(2,1)}), bf16[32,40,512]{2,1,0:T(8,128)(2,1)S(1)}, u32[]{:S(2)}, u32[]{:S(2)}) async-start(bf16[32,40,512]{2,1,0:T(8,128)(2,1)} %bitcast.66), calls=%async_computation.2 | async-start | bytes 2621440 | tf_op jit(solution)/shard_map/all_to_all | solution.py:229
  55.3 2.1 collective-permute-done.part
  57.4 0.8 copy-done.8
  58.3 7.3 %shard_map.101 = (f32[160,2048]{1,0:T(8,128)}, f32[80,2048]{1,0:T(8,128)}, bf16[80,2048]{1,0:T(8,128)(2,1)}, bf16[80,2048]{1,0:T(8,128)(2,1)}, bf16[80,2048]{1,0...) custom-call(s32[4]{0:T(128)} %broadcast_add_fusion, bf16[1280,512]{1,0:T(8,128)(2,1)} %bitcast.61, ...), custom_call_target="tpu_custom_call" | custom-call | tf_op jit(solution)/shard_map/pallas_call | solution.py:110
  65.5 3.1 %collective-permute-start.2 = (bf16[80,2048]{1,0:T(8,128)(2,1)}, bf16[80,2048]{1,0:T(8,128)(2,1)S(1)}, u32[]{:S(2)}, u32[]{:S(2)}) collective-permute-start(bf16[80,2048]{1,0:T(8,128)(2,1)} %get-tuple-element.32), channel_id=1, source_target_pairs={{0,6},{1,3},{2,0},{3,5},{4,2},{5,7},{6,4},{7,1},{8,14},{9,11},{10,... | collective-permute-start | bytes 983048 | tf_op jit(solution)/shard_map/ppermute | solution.py:17
  68.6 3.2 %collective-permute-start.5 = (bf16[80,2048]{1,0:T(8,128)(2,1)}, bf16[80,2048]{1,0:T(8,128)(2,1)}, u32[]{:S(2)}, u32[]{:S(2)}) collective-permute-start(bf16[80,2048]{1,0:T(8,128)(2,1)} %get-tuple-element.34), channel_id=1, source_target_pairs={{0,6},{1,3},{2,0},{3,5},{4,2},{5,7},{6,4},{7,1},{8,14},{9,11},{10,... | collective-permute-start | bytes 983048 | tf_op jit(solution)/shard_map/ppermute | solution.py:17
  71.9 4.9 %collective-permute-done.2 = bf16[80,2048]{1,0:T(8,128)(2,1)S(1)} collective-permute-done((bf16[80,2048]{1,0:T(8,128)(2,1)}, bf16[80,2048]{1,0:T(8,128)(2,1)S(1)}, u32[]{:S(2)}, u32[]{:S(2)}) %collective-permute-start.2) | collective-permute-done | bytes 327712 | tf_op jit(solution)/shard_map/ppermute | solution.py:17
  76.7 1.9 add_convert_fusion.3
  78.6 3.6 %collective-permute-start.3 = (bf16[80,2048]{1,0:T(8,128)(2,1)}, bf16[80,2048]{1,0:T(8,128)(2,1)}, u32[]{:S(2)}, u32[]{:S(2)}) collective-permute-start(bf16[80,2048]{1,0:T(8,128)(2,1)} %add_convert_fusion.3), channel_id=1, source_target_pairs={{0,6},{1,3},{2,0},{3,5},{4,2},{5,7},{6,4},{7,1},{8,14},{9,11},{10,... | collective-permute-start | bytes 983048 | tf_op jit(solution)/shard_map/ppermute | solution.py:17
  82.2 6.2 %all-to-all-done.2 = bf16[32,40,512]{2,1,0:T(8,128)(2,1)S(1)} async-done(((bf16[32,40,512]{2,1,0:T(8,128)(2,1)}), bf16[32,40,512]{2,1,0:T(8,128)(2,1)S(1)}, u32[]{:S(2)}, u32[]{:S(2)}) %all-to-all-start.2) | async-done | bytes 1310752 | tf_op jit(solution)/shard_map/all_to_all | solution.py:229
  88.5 1.0 copy-done.1
  89.9 1.0 add_convert_fusion.2
  91.0 1.7 collective-permute-start.7
  92.7 6.7 %collective-permute-done.7.dn_b = bf16[80,2048]{1,0:T(8,128)(2,1)S(1)} collective-permute-done((bf16[80,2048]{1,0:T(8,128)(2,1)S(1)}, bf16[80,2048]{1,0:T(8,128)(2,1)S(1)}, u32[]{:S(2)}, u32[]{:S(2)}) %collective-permute-start.7) | collective-permute-done | bytes 327712 | tf_op jit(solution)/shard_map/ppermute | solution.py:17
  99.4 0.7 copy-done.18
  100.1 3.2 %shard_map.102 = (f32[160,2048]{1,0:T(8,128)}, f32[160,1024]{1,0:T(8,128)}) custom-call(f32[160,2048]{1,0:T(8,128)} %get-tuple-element.30.near, bf16[80,2048]{1,0:T(8,128)(2,1)} %collective-permute-done.3.up_a, bf16[80,2048]{1,0:T(8,128)(2,1)} %collective-permute-done.4.dn_a, bf16[80,2048]{1,0:T(8,128)(2,1)} %collective-permute-done.5.up_b, ...), custom_call_target="tpu_custom_call" | custom-call | tf_op jit(solution)/shard_map/pallas_call | solution.py:140
  103.3 1.1 convert_element_type.85
  104.5 1.9 collective-permute-start.10
  106.3 0.6 collective-permute-start.9
  107.0 1.0 collective-permute-start.8
  108.0 0.8 copy-done.10
  108.8 5.7 %shard_map.103 = (f32[160,1024]{1,0:T(8,128)}, bf16[160,1024]{1,0:T(8,128)(2,1)}, bf16[160,1024]{1,0:T(8,128)(2,1)}, bf16[160,1024]{1,0:T(8,128)(2,1)}) custom-call(s32[4]{0:T(128)} %broadcast_add_fusion, bf16[1280,512]{1,0:T(8,128)(2,1)} %bitcast.55, bf16[1280,512]{1,0:T(8,128)(2,1)} %bitcast.56, bf16[1280,512]{1,0:T(8,128)(2,1)} %bitcast.57, ...), custom_call_target="tpu_custom_call" | custom-call | tf_op jit(solution)/shard_map/pallas_call | solution.py:72
  114.5 2.3 collective-permute-start.14
  116.8 1.7 collective-permute-start.15
  118.5 1.7 collective-permute-done.10
  120.3 4.9 %collective-permute-done.8 = bf16[160,1024]{1,0:T(8,128)(2,1)} collective-permute-done((bf16[160,1024]{1,0:T(8,128)(2,1)S(1)}, bf16[160,1024]{1,0:T(8,128)(2,1)}, u32[]{:S(2)}, u32[]{:S(2)}) %collective-permute-start.8) | collective-permute-done | bytes 327712 | tf_op jit(solution)/shard_map/ppermute | solution.py:17
  125.2 2.3 convolution_convert_fusion.3
  127.5 6.8 %collective-permute-done.14.first = bf16[160,1024]{1,0:T(8,128)(2,1)S(1)} collective-permute-done((bf16[160,1024]{1,0:T(8,128)(2,1)}, bf16[160,1024]{1,0:T(8,128)(2,1)S(1)}, u32[]{:S(2)}, u32[]{:S(2)}) %collective-permute-start.14) | collective-permute-done | bytes 327712 | tf_op jit(solution)/shard_map/ppermute | solution.py:17
  134.4 2.0 collective-permute-done.16.third
  136.4 0.7 copy-done.17
  137.1 2.8 %shard_map.104 = bf16[160,2048]{1,0:T(8,128)(2,1)} custom-call(f32[160,1024]{1,0:T(8,128)} %get-tuple-element.40.near, bf16[160,1024]{1,0:T(8,128)(2,1)} %copy-done.15, bf16[160,1024]{1,0:T(8,128)(2,1)} %copy-done.16, bf16[160,1024]{1,0:T(8,128)(2,1)} %copy-done.17, f32[160,2048]{1,0:T(8,128)} %get-tuple-element.44.gate_up), custom_call_target="tpu_custom_call" | custom-call | tf_op jit(solution)/shard_map/pallas_call | solution.py:163
  139.9 1.3 collective-permute-start.17
  141.2 1.0 collective-permute-start.12
  142.3 2.1 convolution_convert_fusion.4
  144.5 1.0 copy-done.12
  145.5 1.4 collective-permute-start.19
  146.8 7.7 %collective-permute-done.17 = bf16[160,2048]{1,0:T(8,128)(2,1)} collective-permute-done((bf16[160,2048]{1,0:T(8,128)(2,1)}, bf16[160,2048]{1,0:T(8,128)(2,1)}, u32[]{:S(2)}, u32[]{:S(2)}) %collective-permute-start.17) | collective-permute-done | bytes 655392 | tf_op jit(solution)/shard_map/ppermute | solution.py:17
  154.6 1.1 collective-permute-start.18
  155.6 1.3 maximum_select_fusion
  156.9 6.7 %all-to-all-start.1 = ((bf16[32,40,512]{2,1,0:T(8,128)(2,1)}), bf16[32,40,512]{2,1,0:T(8,128)(2,1)S(1)}, u32[]{:S(2)}, u32[]{:S(2)}) async-start(bf16[32,40,512]{2,1,0:T(8,128)(2,1)} %bitcast.9), calls=%async_computation.1 | async-start | bytes 2621440 | tf_op jit(solution)/shard_map/all_to_all | solution.py:229
  163.7 3.5 %fusion.31 = f32[1024,512]{1,0:T(8,128)} fusion(bf16[640,512]{1,0:T(8,128)(2,1)S(1)} %copy-done.11, bf16[160,1024]{1,0:T(8,128)(2,1)S(1)} %copy-done.29, bf16[160,1024]{1,0:T(8,128)(2,1)} %collective-permute-done.9, bf16[160,1024]{1,0:T(8,128)(2,1)} %collective-permute-done.8, bf16[160,1024]{1,0:T(8,128)(2,1)S(1)} %copy-done.20), kind=kOutput, calls=%fused_computation.104 | convolution fusion | flops 676331520 | bytes 4063232 | tf_op jit(solution)/shard_map/rd,rf->df/dot_general | solution.py:39
  167.3 0.9 pad_maximum_fusion.6
  168.4 5.4 %fusion.32 = f32[512,2048]{1,0:T(8,128)} fusion(bf16[640,512]{1,0:T(8,128)(2,1)S(1)} %copy-done.9, bf16[160,2048]{1,0:T(8,128)(2,1)} %collective-permute-done.19, bf16[160,2048]{1,0:T(8,128)(2,1)} %collective-permute-done.18, bf16[160,2048]{1,0:T(8,128)(2,1)} %collective-permute-done.17, bf16[160,2048]{1,0:T(8,128)(2,1)S(1)} %copy-done.12), kind=kOutput, calls=%fused_computation.105 | convolution fusion | flops 1352663040 | bytes 7471104 | tf_op jit(solution)/shard_map/rd,rf->df/dot_general | solution.py:39
  174.0 3.7 %convolution_convert_fusion.2 = bf16[640,512]{1,0:T(8,128)(2,1)S(1)} fusion(bf16[512,2048]{1,0:T(8,128)(2,1)} %collective-permute-done.1.w_part, bf16[160,2048]{1,0:T(8,128)(2,1)} %collective-permute-done.19, bf16[160,2048]{1,0:T(8,128)(2,1)} %collective-permute-done.18, bf16[160,2048]{1,0:T(8,128)(2,1)} %collective-permute-done.17, ...), kind=kOutput, calls=%fused_computation.10 | convolution fusion | flops 1352990720 | bytes 5373952 | tf_op jit(solution)/shard_map/rd,fd->rf/dot_general | solution.py:35
  178.3 3.7 %convolution_convert_fusion.1 = bf16[640,512]{1,0:T(8,128)(2,1)S(1)} fusion(bf16[512,2048]{1,0:T(8,128)(2,1)} %bitcast.5.w_own, bf16[160,2048]{1,0:T(8,128)(2,1)} %collective-permute-done.19, bf16[160,2048]{1,0:T(8,128)(2,1)} %collective-permute-done.18, bf16[160,2048]{1,0:T(8,128)(2,1)} %collective-permute-done.17, bf16[160,2048]{1,0:T(8,128)(2,1)S(1)} %copy-done.12), kind=kOutput, calls=%fused_computation.9 | convolution fusion | flops 1352990720 | bytes 5373952 | tf_op jit(solution)/shard_map/rd,fd->rf/dot_general | solution.py:35
  182.1 1.2 maximum_select_fusion.1
  183.4 12.8 %all-to-all-done.1 = bf16[32,40,512]{2,1,0:T(8,128)(2,1)S(1)} async-done(((bf16[32,40,512]{2,1,0:T(8,128)(2,1)}), bf16[32,40,512]{2,1,0:T(8,128)(2,1)S(1)}, u32[]{:S(2)}, u32[]{:S(2)}) %all-to-all-start.1) | async-done | bytes 1310752 | tf_op jit(solution)/shard_map/all_to_all | solution.py:229
  196.2 5.5 %all-to-all-start.3 = ((bf16[32,40,512]{2,1,0:T(8,128)(2,1)}), bf16[32,40,512]{2,1,0:T(8,128)(2,1)}, u32[]{:S(2)}, u32[]{:S(2)}) async-start(bf16[32,40,512]{2,1,0:T(8,128)(2,1)} %bitcast.67), calls=%async_computation.3 | async-start | bytes 2621440 | tf_op jit(solution)/shard_map/all_to_all | solution.py:229
  201.8 0.9 constant_dynamic-slice_fusion.3
  202.6 0.7 copy-done.5
  204.6 3.9 %fusion.2 = bf16[1,1024,512]{2,1,0:T(8,128)(2,1)} fusion(f32[1024,512]{1,0:T(8,128)} %collective-permute-done.25, bf16[160,512]{1,0:T(8,128)(2,1)S(1)} %copy-done.23, bf16[160,512]{1,0:T(8,128)(2,1)S(1)} %copy-done.24, bf16[160,512]{1,0:T(8,128)(2,1)S(1)} %copy-done.25, bf16[160,512]{1,0:T(8,128)(2,1)S(1)} %copy-done.22, bf16[160,1024]{1,0:T(8,128)(2,1)} %copy-done.28, ...), kind=kOutput, calls=%fused_computation.8 | convolution fusion | flops 680001536 | bytes 5111808 | tf_op jit(solution)/shard_map/rd,rf->df/dot_general | solution.py:39
  208.9 3.3 %collective-permute-done.22 = f32[32,40]{1,0:T(8,128)S(1)} collective-permute-done((f32[32,40]{1,0:T(8,128)S(1)}, f32[32,40]{1,0:T(8,128)S(1)}, u32[]{:S(2)}, u32[]{:S(2)}) %collective-permute-start.22) | collective-permute-done | bytes 5152 | tf_op jit(solution)/shard_map/ppermute | solution.py:43
  212.3 1.0 fusion.5
  213.3 4.2 %collective-permute-done.23 = f32[32,40]{1,0:T(8,128)S(1)} collective-permute-done((f32[32,40]{1,0:T(8,128)S(1)}, f32[32,40]{1,0:T(8,128)S(1)}, u32[]{:S(2)}, u32[]{:S(2)}) %collective-permute-start.23) | collective-permute-done | bytes 5152 | tf_op jit(solution)/shard_map/ppermute | solution.py:43
  217.9 0.6 divide_bitcast_fusion
  218.5 15.5 %all-to-all-done.3 = bf16[32,40,512]{2,1,0:T(8,128)(2,1)} async-done(((bf16[32,40,512]{2,1,0:T(8,128)(2,1)}), bf16[32,40,512]{2,1,0:T(8,128)(2,1)}, u32[]{:S(2)}, u32[]{:S(2)}) %all-to-all-start.3) | async-done | bytes 1310752 | tf_op jit(solution)/shard_map/all_to_all | solution.py:229
  233.9 2.4 fusion.4
  236.3 5.9 %fusion = bf16[1,512,2048]{2,1,0:T(8,128)(2,1)} fusion(f32[512,2048]{1,0:T(8,128)} %collective-permute-done.24, bf16[640,512]{1,0:T(8,128)(2,1)S(1)} %copy-done.13, bf16[160,2048]{1,0:T(8,128)(2,1)} %collective-permute-done.19, bf16[160,2048]{1,0:T(8,128)(2,1)} %collective-permute-done.18, bf16[160,2048]{1,0:T(8,128)(2,1)} %collective-permute-done.17, ...), kind=kOutput, calls=%fused_computation.2 | convolution fusion | flops 1354760192 | bytes 9568256 | tf_op jit(solution)/shard_map/rd,rf->df/dot_general | solution.py:39
  (113 shorter events, 5.1 us)
Async XLA Ops:
  0.6 16.1 %copy-start = (bf16[128,512]{1,0:T(8,128)(2,1)S(1)}, bf16[128,512]{1,0:T(8,128)(2,1)}, u32[]{:S(2)}) copy-start(bf16[128,512]{1,0:T(8,128)(2,1)} %param.11) | copy-start | bytes 393220
  4.3 12.0 %copy-start.26 = (f32[128,8]{0,1:T(8,128)S(1)}, f32[128,8]{0,1:T(8,128)}, u32[]{:S(2)}) copy-start(f32[128,8]{0,1:T(8,128)} %param.8) | copy-start | bytes 12292
  4.3 12.0 %copy-start.27 = (s32[128,8]{0,1:T(8,128)S(1)}, s32[128,8]{0,1:T(8,128)}, u32[]{:S(2)}) copy-start(s32[128,8]{0,1:T(8,128)} %param.7) | copy-start | bytes 12292
  4.3 45.2 %all-to-all-start = ((bf16[32,40,512]{2,1,0:T(8,128)(2,1)}), bf16[32,40,512]{2,1,0:T(8,128)(2,1)S(1)}, u32[]{:S(2)}, u32[]{:S(2)}) async-start(bf16[32,40,512]{2,1,0:T(8,128)(2,1)} %bitcast.3), calls=%async_computation | async-start | bytes 2621440 | tf_op jit(solution)/shard_map/all_to_all | solution.py:229
  15.7 39.7 %collective-permute-start.1 = (bf16[512,2048]{1,0:T(8,128)(2,1)}, bf16[512,2048]{1,0:T(8,128)(2,1)}, u32[]{:S(2)}, u32[]{:S(2)}) collective-permute-start(bf16[512,2048]{1,0:T(8,128)(2,1)} %bitcast.5.w_own), channel_id=1, source_target_pairs={{0,1},{1,0},{2,3},{3,2},{4,5},{5,4},{6,7},{7,6},{8,9},{9,8},{10,11... | collective-permute-start | bytes 6291464 | tf_op jit(solution)/shard_map/ppermute | solution.py:25
  49.6 5.5 %copy-start.3 = (bf16[32,40,512]{2,1,0:T(8,128)(2,1)}, bf16[32,40,512]{2,1,0:T(8,128)(2,1)S(1)}, u32[]{:S(2)}) copy-start(bf16[32,40,512]{2,1,0:T(8,128)(2,1)S(1)} %all-to-all-done) | copy-start | bytes 3932164
  49.6 38.8 %all-to-all-start.2 = ((bf16[32,40,512]{2,1,0:T(8,128)(2,1)}), bf16[32,40,512]{2,1,0:T(8,128)(2,1)S(1)}, u32[]{:S(2)}, u32[]{:S(2)}) async-start(bf16[32,40,512]{2,1,0:T(8,128)(2,1)} %bitcast.66), calls=%async_computation.2 | async-start | bytes 2621440 | tf_op jit(solution)/shard_map/all_to_all | solution.py:229
  55.2 13.4 %copy-start.6 = (bf16[1,1024,512]{2,1,0:T(8,128)(2,1)S(1)}, bf16[1,1024,512]{2,1,0:T(8,128)(2,1)}, u32[]{:S(2)}) copy-start(bf16[1,1024,512]{2,1,0:T(8,128)(2,1)} %param.10) | copy-start | bytes 3145732
  55.2 2.2 collective-permute-start
  57.4 0.8 copy-start.8
  65.5 11.2 %collective-permute-start.2 = (bf16[80,2048]{1,0:T(8,128)(2,1)}, bf16[80,2048]{1,0:T(8,128)(2,1)S(1)}, u32[]{:S(2)}, u32[]{:S(2)}) collective-permute-start(bf16[80,2048]{1,0:T(8,128)(2,1)} %get-tuple-element.32), channel_id=1, source_target_pairs={{0,6},{1,3},{2,0},{3,5},{4,2},{5,7},{6,4},{7,1},{8,14},{9,11},{10,... | collective-permute-start | bytes 983048 | tf_op jit(solution)/shard_map/ppermute | solution.py:17
  68.6 39.3 %collective-permute-start.11 = (bf16[1024,512]{1,0:T(8,128)(2,1)S(1)}, bf16[1024,512]{1,0:T(8,128)(2,1)}, u32[]{:S(2)}, u32[]{:S(2)}) collective-permute-start(bf16[1024,512]{1,0:T(8,128)(2,1)S(1)} %bitcast.69), channel_id=1, source_target_pairs={{0,1},{1,0},{2,3},{3,2},{4,5},{5,4},{6,7},{7,6},{8,9},{9,8},{10,11... | collective-permute-start | bytes 3145736 | tf_op jit(solution)/shard_map/ppermute | solution.py:25
  68.6 22.4 %collective-permute-start.4 = (bf16[80,2048]{1,0:T(8,128)(2,1)}, bf16[80,2048]{1,0:T(8,128)(2,1)}, u32[]{:S(2)}, u32[]{:S(2)}) collective-permute-start(bf16[80,2048]{1,0:T(8,128)(2,1)} %get-tuple-element.33), channel_id=1, source_target_pairs={{0,2},{1,7},{2,4},{3,1},{4,6},{5,3},{6,0},{7,5},{8,10},{9,15},{10,... | collective-permute-start | bytes 983048 | tf_op jit(solution)/shard_map/ppermute | solution.py:17
  68.6 24.0 %collective-permute-start.5 = (bf16[80,2048]{1,0:T(8,128)(2,1)}, bf16[80,2048]{1,0:T(8,128)(2,1)}, u32[]{:S(2)}, u32[]{:S(2)}) collective-permute-start(bf16[80,2048]{1,0:T(8,128)(2,1)} %get-tuple-element.34), channel_id=1, source_target_pairs={{0,6},{1,3},{2,0},{3,5},{4,2},{5,7},{6,4},{7,1},{8,14},{9,11},{10,... | collective-permute-start | bytes 983048 | tf_op jit(solution)/shard_map/ppermute | solution.py:17
  71.9 17.6 %collective-permute-start.6 = (bf16[80,2048]{1,0:T(8,128)(2,1)}, bf16[80,2048]{1,0:T(8,128)(2,1)}, u32[]{:S(2)}, u32[]{:S(2)}) collective-permute-start(bf16[80,2048]{1,0:T(8,128)(2,1)} %get-tuple-element.36), channel_id=1, source_target_pairs={{0,2},{1,7},{2,4},{3,1},{4,6},{5,3},{6,0},{7,5},{8,10},{9,15},{10,... | collective-permute-start | bytes 983048 | tf_op jit(solution)/shard_map/ppermute | solution.py:17
  78.6 14.0 %collective-permute-start.3 = (bf16[80,2048]{1,0:T(8,128)(2,1)}, bf16[80,2048]{1,0:T(8,128)(2,1)}, u32[]{:S(2)}, u32[]{:S(2)}) collective-permute-start(bf16[80,2048]{1,0:T(8,128)(2,1)} %add_convert_fusion.3), channel_id=1, source_target_pairs={{0,6},{1,3},{2,0},{3,5},{4,2},{5,7},{6,4},{7,1},{8,14},{9,11},{10,... | collective-permute-start | bytes 983048 | tf_op jit(solution)/shard_map/ppermute | solution.py:17
  88.4 1.1 copy-start.1
  88.4 1.5 copy-start.14
  89.5 18.5 %collective-permute-start.13 = (bf16[640,512]{1,0:T(8,128)(2,1)S(1)}, bf16[640,512]{1,0:T(8,128)(2,1)S(1)}, u32[]{:S(2)}, u32[]{:S(2)}) collective-permute-start(bf16[640,512]{1,0:T(8,128)(2,1)S(1)} %pad_maximum_fusion.4), channel_id=1, source_target_pairs={{0,1},{1,0},{2,3},{3,2},{4,5},{5,4},{6,7},{7,6},{8,9},{9,8},{10,11... | collective-permute-start | bytes 1966088 | tf_op jit(solution)/shard_map/ppermute | solution.py:25
  91.0 8.4 %collective-permute-start.7 = (bf16[80,2048]{1,0:T(8,128)(2,1)S(1)}, bf16[80,2048]{1,0:T(8,128)(2,1)S(1)}, u32[]{:S(2)}, u32[]{:S(2)}) collective-permute-start(bf16[80,2048]{1,0:T(8,128)(2,1)S(1)} %add_convert_fusion.2), channel_id=1, source_target_pairs={{0,2},{1,7},{2,4},{3,1},{4,6},{5,3},{6,0},{7,5},{8,10},{9,15},{10,... | collective-permute-start | bytes 983048 | tf_op jit(solution)/shard_map/ppermute | solution.py:17
  99.4 0.7 copy-start.18
  104.4 20.8 %copy-start.19 = (bf16[160,1024]{1,0:T(8,128)(2,1)}, bf16[160,1024]{1,0:T(8,128)(2,1)S(1)}, u32[]{:S(2)}) copy-start(bf16[160,1024]{1,0:T(8,128)(2,1)S(1)} %convert_element_type.85) | copy-start | bytes 983044
  104.5 15.8 %collective-permute-start.10 = (bf16[160,1024]{1,0:T(8,128)(2,1)S(1)}, bf16[160,1024]{1,0:T(8,128)(2,1)S(1)}, u32[]{:S(2)}, u32[]{:S(2)}) collective-permute-start(bf16[160,1024]{1,0:T(8,128)(2,1)S(1)} %convert_element_type.85), channel_id=1, source_target_pairs={{0,6},{1,3},{2,0},{3,5},{4,2},{5,7},{6,4},{7,1},{8,14},{9,11},{10,... | collective-permute-start | bytes 983048 | tf_op jit(solution)/shard_map/ppermute | solution.py:17
  106.3 13.9 %collective-permute-start.9 = (bf16[160,1024]{1,0:T(8,128)(2,1)S(1)}, bf16[160,1024]{1,0:T(8,128)(2,1)}, u32[]{:S(2)}, u32[]{:S(2)}) collective-permute-start(bf16[160,1024]{1,0:T(8,128)(2,1)S(1)} %convert_element_type.85), channel_id=1, source_target_pairs={{0,4},{1,5},{2,6},{3,7},{4,0},{5,1},{6,2},{7,3},{8,12},{9,13},{10,... | collective-permute-start | bytes 983048 | tf_op jit(solution)/shard_map/ppermute | solution.py:17
  107.0 18.2 %collective-permute-start.8 = (bf16[160,1024]{1,0:T(8,128)(2,1)S(1)}, bf16[160,1024]{1,0:T(8,128)(2,1)}, u32[]{:S(2)}, u32[]{:S(2)}) collective-permute-start(bf16[160,1024]{1,0:T(8,128)(2,1)S(1)} %convert_element_type.85), channel_id=1, source_target_pairs={{0,2},{1,7},{2,4},{3,1},{4,6},{5,3},{6,0},{7,5},{8,10},{9,15},{10,... | collective-permute-start | bytes 983048 | tf_op jit(solution)/shard_map/ppermute | solution.py:17
  107.9 0.8 copy-start.10
  114.5 19.9 %collective-permute-start.14 = (bf16[160,1024]{1,0:T(8,128)(2,1)}, bf16[160,1024]{1,0:T(8,128)(2,1)S(1)}, u32[]{:S(2)}, u32[]{:S(2)}) collective-permute-start(bf16[160,1024]{1,0:T(8,128)(2,1)} %get-tuple-element.41), channel_id=1, source_target_pairs={{0,6},{1,3},{2,0},{3,5},{4,2},{5,7},{6,4},{7,1},{8,14},{9,11},{10,... | collective-permute-start | bytes 983048 | tf_op jit(solution)/shard_map/ppermute | solution.py:17
  116.8 17.6 %collective-permute-start.15 = (bf16[160,1024]{1,0:T(8,128)(2,1)}, bf16[160,1024]{1,0:T(8,128)(2,1)S(1)}, u32[]{:S(2)}, u32[]{:S(2)}) collective-permute-start(bf16[160,1024]{1,0:T(8,128)(2,1)} %get-tuple-element.42), channel_id=1, source_target_pairs={{0,4},{1,5},{2,6},{3,7},{4,0},{5,1},{6,2},{7,3},{8,12},{9,13},{10,... | collective-permute-start | bytes 983048 | tf_op jit(solution)/shard_map/ppermute | solution.py:17
  120.2 7.2 %copy-start.28 = (bf16[160,1024]{1,0:T(8,128)(2,1)}, bf16[160,1024]{1,0:T(8,128)(2,1)S(1)}, u32[]{:S(2)}) copy-start(bf16[160,1024]{1,0:T(8,128)(2,1)S(1)} %collective-permute-done.10) | copy-start | bytes 983044
  120.2 16.1 %collective-permute-start.16 = (bf16[160,1024]{1,0:T(8,128)(2,1)}, bf16[160,1024]{1,0:T(8,128)(2,1)S(1)}, u32[]{:S(2)}, u32[]{:S(2)}) collective-permute-start(bf16[160,1024]{1,0:T(8,128)(2,1)} %get-tuple-element.43), channel_id=1, source_target_pairs={{0,2},{1,7},{2,4},{3,1},{4,6},{5,3},{6,0},{7,5},{8,10},{9,15},{10,... | collective-permute-start | bytes 983048 | tf_op jit(solution)/shard_map/ppermute | solution.py:17
  134.4 2.0 copy-start.15
  134.4 2.0 copy-start.16
  136.4 0.7 copy-start.17
  139.9 2.3 copy-start.7
  139.9 14.6 %collective-permute-start.17 = (bf16[160,2048]{1,0:T(8,128)(2,1)}, bf16[160,2048]{1,0:T(8,128)(2,1)}, u32[]{:S(2)}, u32[]{:S(2)}) collective-permute-start(bf16[160,2048]{1,0:T(8,128)(2,1)} %shard_map.104), channel_id=1, source_target_pairs={{0,2},{1,7},{2,4},{3,1},{4,6},{5,3},{6,0},{7,5},{8,10},{9,15},{10,... | collective-permute-start | bytes 1966088 | tf_op jit(solution)/shard_map/ppermute | solution.py:17
  141.2 14.4 %collective-permute-start.12 = (bf16[640,512]{1,0:T(8,128)(2,1)S(1)}, bf16[640,512]{1,0:T(8,128)(2,1)S(1)}, u32[]{:S(2)}, u32[]{:S(2)}) collective-permute-start(bf16[640,512]{1,0:T(8,128)(2,1)S(1)} %pad_maximum_fusion.3), channel_id=1, source_target_pairs={{0,1},{1,0},{2,3},{3,2},{4,5},{5,4},{6,7},{7,6},{8,9},{9,8},{10,11... | collective-permute-start | bytes 1966088 | tf_op jit(solution)/shard_map/ppermute | solution.py:25
  144.4 1.1 copy-start.12
  145.5 22.7 %collective-permute-start.19 = (bf16[160,2048]{1,0:T(8,128)(2,1)S(1)}, bf16[160,2048]{1,0:T(8,128)(2,1)}, u32[]{:S(2)}, u32[]{:S(2)}) collective-permute-start(bf16[160,2048]{1,0:T(8,128)(2,1)S(1)} %copy-done.12), channel_id=1, source_target_pairs={{0,6},{1,3},{2,0},{3,5},{4,2},{5,7},{6,4},{7,1},{8,14},{9,11},{10,... | collective-permute-start | bytes 1966088 | tf_op jit(solution)/shard_map/ppermute | solution.py:17
  154.6 13.6 %collective-permute-start.18 = (bf16[160,2048]{1,0:T(8,128)(2,1)}, bf16[160,2048]{1,0:T(8,128)(2,1)}, u32[]{:S(2)}, u32[]{:S(2)}) collective-permute-start(bf16[160,2048]{1,0:T(8,128)(2,1)} %collective-permute-done.17), channel_id=1, source_target_pairs={{0,2},{1,7},{2,4},{3,1},{4,6},{5,3},{6,0},{7,5},{8,10},{9,15},{10,... | collective-permute-start | bytes 1966088 | tf_op jit(solution)/shard_map/ppermute | solution.py:17
  156.9 6.8 %copy-start.11 = (bf16[640,512]{1,0:T(8,128)(2,1)S(1)}, bf16[640,512]{1,0:T(8,128)(2,1)}, u32[]{:S(2)}) copy-start(bf16[640,512]{1,0:T(8,128)(2,1)} %copy-done.10) | copy-start | bytes 1966084
  156.9 6.8 %copy-start.20 = (bf16[160,1024]{1,0:T(8,128)(2,1)S(1)}, bf16[160,1024]{1,0:T(8,128)(2,1)}, u32[]{:S(2)}) copy-start(bf16[160,1024]{1,0:T(8,128)(2,1)} %copy-done.19) | copy-start | bytes 983044
  156.9 6.8 %copy-start.29 = (bf16[160,1024]{1,0:T(8,128)(2,1)S(1)}, bf16[160,1024]{1,0:T(8,128)(2,1)}, u32[]{:S(2)}) copy-start(bf16[160,1024]{1,0:T(8,128)(2,1)} %copy-done.28) | copy-start | bytes 983044
  156.9 39.3 %all-to-all-start.1 = ((bf16[32,40,512]{2,1,0:T(8,128)(2,1)}), bf16[32,40,512]{2,1,0:T(8,128)(2,1)S(1)}, u32[]{:S(2)}, u32[]{:S(2)}) async-start(bf16[32,40,512]{2,1,0:T(8,128)(2,1)} %bitcast.9), calls=%async_computation.1 | async-start | bytes 2621440 | tf_op jit(solution)/shard_map/all_to_all | solution.py:229
  163.7 3.5 %copy-start.4 = (bf16[32,40,512]{2,1,0:T(8,128)(2,1)S(1)}, bf16[32,40,512]{2,1,0:T(8,128)(2,1)}, u32[]{:S(2)}) copy-start(bf16[32,40,512]{2,1,0:T(8,128)(2,1)} %copy-done.3) | copy-start | bytes 3932164
  167.2 1.2 copy-start.9
  167.2 36.8 %collective-permute-start.25 = (f32[1024,512]{1,0:T(8,128)}, f32[1024,512]{1,0:T(8,128)}, u32[]{:S(2)}, u32[]{:S(2)}) collective-permute-start(f32[1024,512]{1,0:T(8,128)} %fusion.31), channel_id=1, source_target_pairs={{0,1},{1,0},{2,3},{3,2},{4,5},{5,4},{6,7},{7,6},{8,9},{9,8},{10,11... | collective-permute-start | bytes 6291464 | tf_op jit(solution)/shard_map/ppermute | solution.py:25
  173.8 62.5 %collective-permute-start.24 = (f32[512,2048]{1,0:T(8,128)}, f32[512,2048]{1,0:T(8,128)}, u32[]{:S(2)}, u32[]{:S(2)}) collective-permute-start(f32[512,2048]{1,0:T(8,128)} %fusion.32), channel_id=1, source_target_pairs={{0,1},{1,0},{2,3},{3,2},{4,5},{5,4},{6,7},{7,6},{8,9},{9,8},{10,11... | collective-permute-start | bytes 12582920 | tf_op jit(solution)/shard_map/ppermute | solution.py:25
  177.9 4.2 %collective-permute-start.20 = (bf16[640,512]{1,0:T(8,128)(2,1)S(1)}, bf16[640,512]{1,0:T(8,128)(2,1)S(1)}, u32[]{:S(2)}, u32[]{:S(2)}) collective-permute-start(bf16[640,512]{1,0:T(8,128)(2,1)S(1)} %pad_maximum_fusion.5), channel_id=1, source_target_pairs={{0,1},{1,0},{2,3},{3,2},{4,5},{5,4},{6,7},{7,6},{8,9},{9,8},{10,11... | collective-permute-start | bytes 1966088 | tf_op jit(solution)/shard_map/ppermute | solution.py:25
  196.2 5.5 %copy-start.2 = (bf16[32,40,512]{2,1,0:T(8,128)(2,1)S(1)}, bf16[32,40,512]{2,1,0:T(8,128)(2,1)}, u32[]{:S(2)}) copy-start(bf16[32,40,512]{2,1,0:T(8,128)(2,1)} %copy-done.1) | copy-start | bytes 3932164
  196.2 37.7 %all-to-all-start.3 = ((bf16[32,40,512]{2,1,0:T(8,128)(2,1)}), bf16[32,40,512]{2,1,0:T(8,128)(2,1)}, u32[]{:S(2)}, u32[]{:S(2)}) async-start(bf16[32,40,512]{2,1,0:T(8,128)(2,1)} %bitcast.67), calls=%async_computation.3 | async-start | bytes 2621440 | tf_op jit(solution)/shard_map/all_to_all | solution.py:229
  201.8 1.6 copy-start.5
  203.3 1.0 copy-start.21
  203.3 1.0 copy-start.22
  203.3 1.1 copy-start.23
  203.3 1.2 copy-start.24
  203.3 1.2 copy-start.25
  203.9 4.6 %collective-permute-start.21 = (f32[32,40]{1,0:T(8,128)S(1)}, f32[32,40]{1,0:T(8,128)S(1)}, u32[]{:S(2)}, u32[]{:S(2)}) collective-permute-start(f32[32,40]{1,0:T(8,128)S(1)} %reshape.77), channel_id=1, source_target_pairs={{0,1},{1,0},{2,3},{3,2},{4,5},{5,4},{6,7},{7,6},{8,9},{9,8},{10,11... | collective-permute-start | bytes 15368 | tf_op jit(solution)/shard_map/ppermute | solution.py:43
  208.5 3.8 %collective-permute-start.22 = (f32[32,40]{1,0:T(8,128)S(1)}, f32[32,40]{1,0:T(8,128)S(1)}, u32[]{:S(2)}, u32[]{:S(2)}) collective-permute-start(f32[32,40]{1,0:T(8,128)S(1)} %add.239), channel_id=1, source_target_pairs={{0,2},{1,3},{2,0},{3,1},{4,6},{5,7},{6,4},{7,5},{8,10},{9,11},{10,... | collective-permute-start | bytes 15368 | tf_op jit(solution)/shard_map/ppermute | solution.py:43
  212.3 24.0 %copy-start.13 = (bf16[640,512]{1,0:T(8,128)(2,1)S(1)}, bf16[640,512]{1,0:T(8,128)(2,1)}, u32[]{:S(2)}) copy-start(bf16[640,512]{1,0:T(8,128)(2,1)} %pad_maximum_fusion.6) | copy-start | bytes 1966084
  212.3 5.2 %collective-permute-start.23 = (f32[32,40]{1,0:T(8,128)S(1)}, f32[32,40]{1,0:T(8,128)S(1)}, u32[]{:S(2)}, u32[]{:S(2)}) collective-permute-start(f32[32,40]{1,0:T(8,128)S(1)} %add.240), channel_id=1, source_target_pairs={{0,4},{1,5},{2,6},{3,7},{4,0},{5,1},{6,2},{7,3},{8,12},{9,13},{10,... | collective-permute-start | bytes 15368 | tf_op jit(solution)/shard_map/ppermute | solution.py:43

commit v5 on v4

--- a/solution.py
+++ b/solution.py
@@ -71,6 +71,7 @@
     out = pl.BlockSpec((rows, chunk), lambda j, order: (0, j))
     return pl.pallas_call(
         functools.partial(partial_kernel, turned=turned),
+        compiler_params=pltpu.CompilerParams(vmem_limit_bytes=24 * 1024 * 1024),
         grid_spec=pltpu.PrefetchScalarGridSpec(
             num_scalar_prefetch=1,
             grid=(width // chunk,),
@@ -109,6 +110,7 @@
     kinds = [F32, BF, BF, BF, BF, F32]
     return pl.pallas_call(
         halves_kernel,
+        compiler_params=pltpu.CompilerParams(vmem_limit_bytes=24 * 1024 * 1024),
         grid_spec=pltpu.PrefetchScalarGridSpec(
             num_scalar_prefetch=1,
             grid=(width // chunk,),
@@ -139,6 +141,7 @@
     rows, width = near.shape
     return pl.pallas_call(
         hidden_kernel,
+        compiler_params=pltpu.CompilerParams(vmem_limit_bytes=24 * 1024 * 1024),
         out_shape=[
             jax.ShapeDtypeStruct((rows, width), F32),
             jax.ShapeDtypeStruct((rows, width // 2), F32),
@@ -162,6 +165,7 @@
     wide = pl.BlockSpec((tile, 2 * width), lambda i: (i, 0))
     return pl.pallas_call(
         gate_grad_kernel,
+        compiler_params=pltpu.CompilerParams(vmem_limit_bytes=24 * 1024 * 1024),
         grid=(2,),
         in_specs=[narrow, narrow, narrow, narrow, wide],
         out_specs=wide,
@@ -281,8 +285,8 @@
     gug = jnp.concatenate(gather_rows(gate_up_grad, n_y), axis=0)
     other_rows = absolute(dot_t(gug, in_part).astype(BF), y, core, n_y)
     grad_other = permute_core(other_rows, n_y)
-    in_late, _ = lax.optimization_barrier((in_own, other_rows))
-    grad_mine = absolute(dot_t(gug, in_late).astype(BF), y, core, n_y)
+    y_late, _ = lax.optimization_barrier((y, other_rows))
+    grad_mine = absolute(dot_t(gug, in_own).astype(BF), y_late, core, n_y)
     choice_grad = both_halves(grad_mine, grad_other, core)
     grad_back = exchange(choice_grad)
 

time: 244 us -> 242 us (level)
  the two profiles are of different devices: /device:TPU:32 before, /device:TPU:33 now
where the time goes in v5:
time: 242 us; the launch traced here: 238 us
  waiting for transfers between devices  99.9 us (41%)
  starting transfers between devices  61.7 us (25%)
  matrix products  43.4 us (18%)
  other arithmetic  14.6 us (6%)
  Pallas kernels  13.5 us (6%)
  local copies, waits for them, and re-layouts  3.86 us (2%)
    all_to_all x4, waiting for transfers between devices, exchange(): lax.all_to_all(v, 'dp', split_axis=0, concat_axis=0, tiled=True)  66.1 us
    ppermute x15, waiting for transfers between devices, permute_y(): lax.ppermute(v, 'expert', [(2 * y + c, 2 * ((y + (2 * c - 1) * step) % n_...  28.8 us
    all_to_all x4, starting transfers between devices, exchange(): lax.all_to_all(v, 'dp', split_axis=0, concat_axis=0, tiled=True)  27 us
    dot_general x7, matrix products, gather_dot(): return jnp.einsum('rd,rf->df', a, b, preferred_element_type=F32)  26 us
    ppermute x15, starting transfers between devices, permute_y(): lax.ppermute(v, 'expert', [(2 * y + c, 2 * ((y + (2 * c - 1) * step) % n_...  22.7 us
    ppermute x8, starting transfers between devices, permute_core(): lax.ppermute(v, 'expert', [(2 * y + c, 2 * y + 1 - c) for y in range(n_y)...  10.1 us
    dot_general x5, matrix products, dot(): return jnp.dot(a, b, preferred_element_type=F32)  9.51 us
    dot_general x2, matrix products, dot_t(): return jnp.einsum('rd,fd->rf', a, b, preferred_element_type=F32)  7.9 us
  transfers between devices with their start and end apart: 30, of which 15 were waited for; matrix products, arithmetic and copies ran while one was open for 21% of the time, Pallas kernels for 5%

profile of v5, /device:TPU:33, one launch (start us, length us, event | category | flops | bytes accessed | tf_op | source)
XLA Modules:
  0.0 238.1 jit_solution(5841714541548702432)
XLA Ops:
  1.9 2.5 %convolution_convert_fusion = bf16[1280,512]{1,0:T(8,128)(2,1)} fusion(pred[1280,128]{1,0:T(32,128)(4,1)S(1)} %bitcast_compare_fusion, bf16[128,512]{1,0:T(8,128)(2,1)} %param.6), kind=kOutput, calls=%fused_computation.1 | convolution fusion | flops 168427520 | bytes 1605632 | tf_op jit(solution)/shard_map/dot_general | solution.py:31
  4.3 10.8 %all-to-all-start = ((bf16[32,40,512]{2,1,0:T(8,128)(2,1)}), bf16[32,40,512]{2,1,0:T(8,128)(2,1)S(1)}, u32[]{:S(2)}, u32[]{:S(2)}) async-start(bf16[32,40,512]{2,1,0:T(8,128)(2,1)} %bitcast.3), calls=%async_computation | async-start | bytes 2621440 | tf_op jit(solution)/shard_map/all_to_all | solution.py:233
  15.1 1.3 collective-permute-start.1
  16.9 2.0 fusion.34
  18.9 29.4 %all-to-all-done = bf16[32,40,512]{2,1,0:T(8,128)(2,1)S(1)} async-done(((bf16[32,40,512]{2,1,0:T(8,128)(2,1)}), bf16[32,40,512]{2,1,0:T(8,128)(2,1)S(1)}, u32[]{:S(2)}, u32[]{:S(2)}) %all-to-all-start) | async-done | bytes 1310752 | tf_op jit(solution)/shard_map/all_to_all | solution.py:233
  48.2 5.7 %all-to-all-start.2 = ((bf16[32,40,512]{2,1,0:T(8,128)(2,1)}), bf16[32,40,512]{2,1,0:T(8,128)(2,1)S(1)}, u32[]{:S(2)}, u32[]{:S(2)}) async-start(bf16[32,40,512]{2,1,0:T(8,128)(2,1)} %bitcast.70), calls=%async_computation.2 | async-start | bytes 2621440 | tf_op jit(solution)/shard_map/all_to_all | solution.py:233
  54.2 1.8 collective-permute-start
  56.0 1.7 collective-permute-done.part
  57.7 6.3 %shard_map.101 = (f32[160,2048]{1,0:T(8,128)S(1)}, f32[80,2048]{1,0:T(8,128)S(1)}, bf16[80,2048]{1,0:T(8,128)(2,1)}, bf16[80,2048]{1,0:T(8,128)(2,1)S(1)}, bf16[...) custom-call(s32[4]{0:T(128)S(1)} %broadcast_add_fusion, bf16[1280,512]{1,0:T(8,128)(2,1)S(1)} %bitcast.62, ...), custom_call_target="tpu_custom_call" | custom-call | tf_op jit(solution)/shard_map/pallas_call | solution.py:111
  64.0 0.8 copy-done.6
  64.8 1.3 collective-permute-start.2
  66.1 2.1 collective-permute-start.11
  68.7 1.0 collective-permute-start.5
  69.7 1.7 collective-permute-start.6
  71.4 1.0 collective-permute-done.2
  72.3 0.8 add_convert_fusion.3
  73.1 1.2 collective-permute-start.3
  74.3 11.7 %all-to-all-done.2 = bf16[32,40,512]{2,1,0:T(8,128)(2,1)S(1)} async-done(((bf16[32,40,512]{2,1,0:T(8,128)(2,1)}), bf16[32,40,512]{2,1,0:T(8,128)(2,1)S(1)}, u32[]{:S(2)}, u32[]{:S(2)}) %all-to-all-start.2) | async-done | bytes 1310752 | tf_op jit(solution)/shard_map/all_to_all | solution.py:233
  86.1 0.9 pad_maximum_fusion.4
  87.0 3.1 %collective-permute-start.13 = (bf16[640,512]{1,0:T(8,128)(2,1)}, bf16[640,512]{1,0:T(8,128)(2,1)}, u32[]{:S(2)}, u32[]{:S(2)}) collective-permute-start(bf16[640,512]{1,0:T(8,128)(2,1)} %pad_maximum_fusion.4), channel_id=1, source_target_pairs={{0,1},{1,0},{2,3},{3,2},{4,5},{5,4},{6,7},{7,6},{8,9},{9,8},{10,11... | collective-permute-start | bytes 1966088 | tf_op jit(solution)/shard_map/ppermute | solution.py:25
  90.0 1.0 add_convert_fusion.2
  91.1 2.8 %collective-permute-start.7 = (bf16[80,2048]{1,0:T(8,128)(2,1)S(1)}, bf16[80,2048]{1,0:T(8,128)(2,1)S(1)}, u32[]{:S(2)}, u32[]{:S(2)}) collective-permute-start(bf16[80,2048]{1,0:T(8,128)(2,1)S(1)} %add_convert_fusion.2), channel_id=1, source_target_pairs={{0,2},{1,7},{2,4},{3,1},{4,6},{5,3},{6,0},{7,5},{8,10},{9,15},{10,... | collective-permute-start | bytes 983048 | tf_op jit(solution)/shard_map/ppermute | solution.py:17
  93.9 4.0 %collective-permute-done.7.dn_b = bf16[80,2048]{1,0:T(8,128)(2,1)S(1)} collective-permute-done((bf16[80,2048]{1,0:T(8,128)(2,1)S(1)}, bf16[80,2048]{1,0:T(8,128)(2,1)S(1)}, u32[]{:S(2)}, u32[]{:S(2)}) %collective-permute-start.7) | collective-permute-done | bytes 327712 | tf_op jit(solution)/shard_map/ppermute | solution.py:17
  97.9 1.4 shard_map.102
  99.4 1.0 copy-done.2
  100.4 0.8 convert_element_type.85
  102.0 3.5 %collective-permute-start.9 = (bf16[160,1024]{1,0:T(8,128)(2,1)}, bf16[160,1024]{1,0:T(8,128)(2,1)}, u32[]{:S(2)}, u32[]{:S(2)}) collective-permute-start(bf16[160,1024]{1,0:T(8,128)(2,1)} %convert_element_type.85), channel_id=1, source_target_pairs={{0,4},{1,5},{2,6},{3,7},{4,0},{5,1},{6,2},{7,3},{8,12},{9,13},{10,... | collective-permute-start | bytes 983048 | tf_op jit(solution)/shard_map/ppermute | solution.py:17
  105.7 4.7 %shard_map.103 = (f32[160,1024]{1,0:T(8,128)S(1)}, bf16[160,1024]{1,0:T(8,128)(2,1)S(1)}, bf16[160,1024]{1,0:T(8,128)(2,1)S(1)}, bf16[160,1024]{1,0:T(8,128)(2,1)S(1)}) custom-call(s32[4]{0:T(128)S(1)} %broadcast_add_fusion, bf16[1280,512]{1,0:T(8,128)(2,1)S(1)} %bitcast.56, bf16[1280,512]{1,0:T(8,128)(2,1)S(1)} %bitcast.57, bf16[1280,512]{1,0:T(8,128)(2,1)S(1)} %bitcast.58, ...), custom_call_target="tpu_custom_call" | custom-call | tf_op jit(solution)/shard_map/pallas_call | solution.py:72
  110.3 1.4 collective-permute-start.14
  111.7 2.5 %collective-permute-start.16 = (bf16[160,1024]{1,0:T(8,128)(2,1)S(1)}, bf16[160,1024]{1,0:T(8,128)(2,1)S(1)}, u32[]{:S(2)}, u32[]{:S(2)}) collective-permute-start(bf16[160,1024]{1,0:T(8,128)(2,1)S(1)} %get-tuple-element.43), channel_id=1, source_target_pairs={{0,2},{1,7},{2,4},{3,1},{4,6},{5,3},{6,0},{7,5},{8,10},{9,15},{10,... | collective-permute-start | bytes 983048 | tf_op jit(solution)/shard_map/ppermute | solution.py:17
  114.2 3.9 %collective-permute-done.9 = bf16[160,1024]{1,0:T(8,128)(2,1)} collective-permute-done((bf16[160,1024]{1,0:T(8,128)(2,1)}, bf16[160,1024]{1,0:T(8,128)(2,1)}, u32[]{:S(2)}, u32[]{:S(2)}) %collective-permute-start.9) | collective-permute-done | bytes 327712 | tf_op jit(solution)/shard_map/ppermute | solution.py:17
  118.1 2.4 collective-permute-done.8
  120.4 2.5 %convolution_convert_fusion.3 = bf16[640,512]{1,0:T(8,128)(2,1)S(1)} fusion(bf16[1024,512]{1,0:T(8,128)(2,1)} %collective-permute-done.11.w_part, bf16[160,1024]{1,0:T(8,128)(2,1)} %collective-permute-done.10, bf16[160,1024]{1,0:T(8,128)(2,1)} %collective-permute-done.9, bf16[160,1024]{1,0:T(8,128)(2,1)} %collective-permute-done.8, ...), kind=kOutput, calls=%fused_computation.11 | convolution fusion | flops 676659200 | bytes 3014656 | tf_op jit(solution)/shard_map/dot_general | solution.py:31
  123.0 1.1 collective-permute-done.14.first
  124.0 8.0 %collective-permute-done.15.second = bf16[160,1024]{1,0:T(8,128)(2,1)S(1)} collective-permute-done((bf16[160,1024]{1,0:T(8,128)(2,1)S(1)}, bf16[160,1024]{1,0:T(8,128)(2,1)S(1)}, u32[]{:S(2)}, u32[]{:S(2)}) %collective-permute-start.15) | collective-permute-done | bytes 327712 | tf_op jit(solution)/shard_map/ppermute | solution.py:17
  132.1 2.3 collective-permute-done.16.third
  134.4 1.1 shard_map.104
  135.5 2.4 %collective-permute-start.17 = (bf16[160,2048]{1,0:T(8,128)(2,1)}, bf16[160,2048]{1,0:T(8,128)(2,1)}, u32[]{:S(2)}, u32[]{:S(2)}) collective-permute-start(bf16[160,2048]{1,0:T(8,128)(2,1)} %shard_map.104), channel_id=1, source_target_pairs={{0,2},{1,7},{2,4},{3,1},{4,6},{5,3},{6,0},{7,5},{8,10},{9,15},{10,... | collective-permute-start | bytes 1966088 | tf_op jit(solution)/shard_map/ppermute | solution.py:17
  138.0 0.9 pad_maximum_fusion.3
  138.8 2.5 %convolution_convert_fusion.4 = bf16[640,512]{1,0:T(8,128)(2,1)S(1)} fusion(bf16[1,1024,512]{2,1,0:T(8,128)(2,1)} %param.10, bf16[160,1024]{1,0:T(8,128)(2,1)} %collective-permute-done.10, bf16[160,1024]{1,0:T(8,128)(2,1)} %collective-permute-done.9, bf16[160,1024]{1,0:T(8,128)(2,1)} %collective-permute-done.8, bf16[160,1024]{1,0:T(8,128)(2,1)} %convert_element_type.85), kind=kOutput, calls=%fused_computation.12 | convolution fusion | flops 676659200 | bytes 3014656 | tf_op jit(solution)/shard_map/dot_general | solution.py:31
  141.5 6.2 %collective-permute-done.17 = bf16[160,2048]{1,0:T(8,128)(2,1)} collective-permute-done((bf16[160,2048]{1,0:T(8,128)(2,1)}, bf16[160,2048]{1,0:T(8,128)(2,1)}, u32[]{:S(2)}, u32[]{:S(2)}) %collective-permute-start.17) | collective-permute-done | bytes 655392 | tf_op jit(solution)/shard_map/ppermute | solution.py:17
  147.7 3.4 %collective-permute-start.18 = (bf16[160,2048]{1,0:T(8,128)(2,1)}, bf16[160,2048]{1,0:T(8,128)(2,1)}, u32[]{:S(2)}, u32[]{:S(2)}) collective-permute-start(bf16[160,2048]{1,0:T(8,128)(2,1)} %collective-permute-done.17), channel_id=1, source_target_pairs={{0,2},{1,7},{2,4},{3,1},{4,6},{5,3},{6,0},{7,5},{8,10},{9,15},{10,... | collective-permute-start | bytes 1966088 | tf_op jit(solution)/shard_map/ppermute | solution.py:17
  151.1 2.6 %maximum_select_fusion = bf16[2,640,512]{2,1,0:T(8,128)(2,1)} fusion(bf16[1,640,512]{2,1,0:T(8,128)(2,1)} %bitcast.8, bf16[1,640,512]{2,1,0:T(8,128)(2,1)S(1)} %maximum_bitcast_fusion, pred[]{:T(512)S(6)} %eq.89), kind=kLoop, calls=%fused_computation.14 | loop fusion | flops 1966080 | bytes 2621441 | tf_op jit(solution)/shard_map/jit(_where)/select_n | solution.py:203
  153.7 4.9 %all-to-all-start.1 = ((bf16[32,40,512]{2,1,0:T(8,128)(2,1)}), bf16[32,40,512]{2,1,0:T(8,128)(2,1)}, u32[]{:S(2)}, u32[]{:S(2)}) async-start(bf16[32,40,512]{2,1,0:T(8,128)(2,1)} %bitcast.69), calls=%async_computation.1 | async-start | bytes 2621440 | tf_op jit(solution)/shard_map/all_to_all | solution.py:233
  158.6 3.8 %fusion.32 = f32[1024,512]{1,0:T(8,128)} fusion(bf16[640,512]{1,0:T(8,128)(2,1)} %collective-permute-done.13.part, bf16[160,1024]{1,0:T(8,128)(2,1)} %collective-permute-done.10, bf16[160,1024]{1,0:T(8,128)(2,1)} %collective-permute-done.9, bf16[160,1024]{1,0:T(8,128)(2,1)} %collective-permute-done.8, bf16[160,1024]{1,0:T(8,128)(2,1)} %convert_element_type.85), kind=kOutput, calls=%fused_computation.105 | convolution fusion | flops 676331520 | bytes 4063232 | tf_op jit(solution)/shard_map/rd,rf->df/dot_general | solution.py:39
  162.4 1.2 collective-permute-start.25
  163.7 0.9 pad_maximum_fusion.6
  164.6 5.5 %fusion.33 = f32[512,2048]{1,0:T(8,128)} fusion(bf16[640,512]{1,0:T(8,128)(2,1)S(1)} %collective-permute-done.part, bf16[160,2048]{1,0:T(8,128)(2,1)} %collective-permute-done.19, bf16[160,2048]{1,0:T(8,128)(2,1)} %collective-permute-done.18, bf16[160,2048]{1,0:T(8,128)(2,1)} %collective-permute-done.17, bf16[160,2048]{1,0:T(8,128)(2,1)} %shard_map.104), kind=kOutput, calls=%fused_computation.106 | convolution fusion | flops 1352663040 | bytes 7471104 | tf_op jit(solution)/shard_map/rd,rf->df/dot_general | solution.py:39
  170.1 3.9 %convolution_convert_fusion.1 = bf16[640,512]{1,0:T(8,128)(2,1)S(1)} fusion(bf16[512,2048]{1,0:T(8,128)(2,1)} %collective-permute-done.1.w_part, bf16[160,2048]{1,0:T(8,128)(2,1)} %collective-permute-done.19, bf16[160,2048]{1,0:T(8,128)(2,1)} %collective-permute-done.18, bf16[160,2048]{1,0:T(8,128)(2,1)} %collective-permute-done.17, ...), kind=kOutput, calls=%fused_computation.9 | convolution fusion | flops 1352990720 | bytes 5373952 | tf_op jit(solution)/shard_map/rd,fd->rf/dot_general | solution.py:35
  174.9 3.9 %convolution_convert_fusion.2 = bf16[640,512]{1,0:T(8,128)(2,1)S(1)} fusion(bf16[1,512,2048]{2,1,0:T(8,128)(2,1)} %param.9, bf16[160,2048]{1,0:T(8,128)(2,1)} %collective-permute-done.19, bf16[160,2048]{1,0:T(8,128)(2,1)} %collective-permute-done.18, bf16[160,2048]{1,0:T(8,128)(2,1)} %collective-permute-done.17, bf16[160,2048]{1,0:T(8,128)(2,1)} %shard_map.104), kind=kOutput, calls=%fused_computation.10 | convolution fusion | flops 1352990720 | bytes 5373952 | tf_op jit(solution)/shard_map/rd,fd->rf/dot_general | solution.py:35
  178.9 2.6 %maximum_select_fusion.1 = bf16[2,640,512]{2,1,0:T(8,128)(2,1)} fusion(bf16[1,640,512]{2,1,0:T(8,128)(2,1)} %bitcast.15, bf16[1,640,512]{2,1,0:T(8,128)(2,1)S(1)} %maximum_bitcast_fusion.1, pred[]{:T(512)S(6)} %eq.89), kind=kLoop, calls=%fused_computation.15 | loop fusion | flops 1966080 | bytes 2621441 | tf_op jit(solution)/shard_map/jit(_where)/select_n | solution.py:203
  181.6 10.4 %all-to-all-done.1 = bf16[32,40,512]{2,1,0:T(8,128)(2,1)} async-done(((bf16[32,40,512]{2,1,0:T(8,128)(2,1)}), bf16[32,40,512]{2,1,0:T(8,128)(2,1)}, u32[]{:S(2)}, u32[]{:S(2)}) %all-to-all-start.1) | async-done | bytes 1310752 | tf_op jit(solution)/shard_map/all_to_all | solution.py:233
  192.0 5.6 %all-to-all-start.3 = ((bf16[32,40,512]{2,1,0:T(8,128)(2,1)}), bf16[32,40,512]{2,1,0:T(8,128)(2,1)}, u32[]{:S(2)}, u32[]{:S(2)}) async-start(bf16[32,40,512]{2,1,0:T(8,128)(2,1)} %bitcast.16), calls=%async_computation.3 | async-start | bytes 2621440 | tf_op jit(solution)/shard_map/all_to_all | solution.py:233
  197.6 1.2 copy-done.8
  198.9 1.7 fusion.1
  200.7 1.8 collective-permute-start.21
  202.5 4.0 %fusion.2 = bf16[1,1024,512]{2,1,0:T(8,128)(2,1)} fusion(f32[1024,512]{1,0:T(8,128)} %collective-permute-done.25, bf16[160,512]{1,0:T(8,128)(2,1)S(1)} %get-tuple-element.56, bf16[160,512]{1,0:T(8,128)(2,1)S(1)} %get-tuple-element.57, bf16[160,512]{1,0:T(8,128)(2,1)S(1)} %get-tuple-element.58, bf16[160,512]{1,0:T(8,128)(2,1)S(1)} %get-tuple-element.55, ...), kind=kOutput, calls=%fused_computation.8 | convolution fusion | flops 680001536 | bytes 5111808 | tf_op jit(solution)/shard_map/rd,rf->df/dot_general | solution.py:39
  206.6 1.7 convolution_bitcast_fusion.1
  208.3 1.3 collective-permute-done.22
  209.6 2.4 %fusion.5 = bf16[128,512]{1,0:T(8,128)(2,1)} fusion(f32[128,512]{1,0:T(8,128)S(1)} %convolution_bitcast_fusion.1, bf16[32,40,512]{2,1,0:T(8,128)(2,1)} %all-to-all-done.1, f32[32,128]{1,0:T(8,128)S(1)} %select_reduce_fusion.3, s32[32,128]{1,0:T(8,128)S(1)} %fusion.6), kind=kOutput, calls=%fused_computation.21 | convolution fusion | flops 168558592 | bytes 1736704 | tf_op jit(solution)/shard_map/rd,rf->df/dot_general | solution.py:39
  212.0 2.1 collective-permute-done.23
  215.0 14.6 %all-to-all-done.3 = bf16[32,40,512]{2,1,0:T(8,128)(2,1)} async-done(((bf16[32,40,512]{2,1,0:T(8,128)(2,1)}), bf16[32,40,512]{2,1,0:T(8,128)(2,1)}, u32[]{:S(2)}, u32[]{:S(2)}) %all-to-all-start.3) | async-done | bytes 1310752 | tf_op jit(solution)/shard_map/all_to_all | solution.py:233
  229.6 2.4 fusion.4
  232.0 6.2 %fusion = bf16[1,512,2048]{2,1,0:T(8,128)(2,1)} fusion(f32[512,2048]{1,0:T(8,128)} %collective-permute-done.24, bf16[640,512]{1,0:T(8,128)(2,1)S(1)} %copy-done.9, bf16[160,2048]{1,0:T(8,128)(2,1)} %collective-permute-done.19, bf16[160,2048]{1,0:T(8,128)(2,1)} %collective-permute-done.18, bf16[160,2048]{1,0:T(8,128)(2,1)} %collective-permute-done.17, ...), kind=kOutput, calls=%fused_computation.2 | convolution fusion | flops 1354760192 | bytes 9568256 | tf_op jit(solution)/shard_map/rd,rf->df/dot_general | solution.py:39
  (77 shorter events, 5.5 us)
Async XLA Ops:
  0.6 16.2 %copy-start = (bf16[128,512]{1,0:T(8,128)(2,1)S(1)}, bf16[128,512]{1,0:T(8,128)(2,1)}, u32[]{:S(2)}) copy-start(bf16[128,512]{1,0:T(8,128)(2,1)} %param.11) | copy-start | bytes 393220
  4.3 12.1 %copy-start.10 = (f32[128,8]{0,1:T(8,128)S(1)}, f32[128,8]{0,1:T(8,128)}, u32[]{:S(2)}) copy-start(f32[128,8]{0,1:T(8,128)} %param.8) | copy-start | bytes 12292
  4.3 12.1 %copy-start.11 = (s32[128,8]{0,1:T(8,128)S(1)}, s32[128,8]{0,1:T(8,128)}, u32[]{:S(2)}) copy-start(s32[128,8]{0,1:T(8,128)} %param.7) | copy-start | bytes 12292
  4.3 43.9 %all-to-all-start = ((bf16[32,40,512]{2,1,0:T(8,128)(2,1)}), bf16[32,40,512]{2,1,0:T(8,128)(2,1)S(1)}, u32[]{:S(2)}, u32[]{:S(2)}) async-start(bf16[32,40,512]{2,1,0:T(8,128)(2,1)} %bitcast.3), calls=%async_computation | async-start | bytes 2621440 | tf_op jit(solution)/shard_map/all_to_all | solution.py:233
  15.1 40.9 %collective-permute-start.1 = (bf16[512,2048]{1,0:T(8,128)(2,1)}, bf16[512,2048]{1,0:T(8,128)(2,1)}, u32[]{:S(2)}, u32[]{:S(2)}) collective-permute-start(bf16[512,2048]{1,0:T(8,128)(2,1)} %bitcast.67), channel_id=1, source_target_pairs={{0,1},{1,0},{2,3},{3,2},{4,5},{5,4},{6,7},{7,6},{8,9},{9,8},{10,11... | collective-permute-start | bytes 6291464 | tf_op jit(solution)/shard_map/ppermute | solution.py:25
  48.2 37.7 %all-to-all-start.2 = ((bf16[32,40,512]{2,1,0:T(8,128)(2,1)}), bf16[32,40,512]{2,1,0:T(8,128)(2,1)S(1)}, u32[]{:S(2)}, u32[]{:S(2)}) async-start(bf16[32,40,512]{2,1,0:T(8,128)(2,1)} %bitcast.70), calls=%async_computation.2 | async-start | bytes 2621440 | tf_op jit(solution)/shard_map/all_to_all | solution.py:233
  54.1 3.7 %copy-start.1 = (bf16[1,512,2048]{2,1,0:T(8,128)(2,1)S(1)}, bf16[1,512,2048]{2,1,0:T(8,128)(2,1)}, u32[]{:S(2)}) copy-start(bf16[1,512,2048]{2,1,0:T(8,128)(2,1)} %param.9) | copy-start | bytes 6291460
  54.2 3.5 %collective-permute-start = (bf16[640,512]{1,0:T(8,128)(2,1)S(1)}, bf16[640,512]{1,0:T(8,128)(2,1)S(1)}, u32[]{:S(2)}, u32[]{:S(2)}) collective-permute-start(bf16[640,512]{1,0:T(8,128)(2,1)S(1)} %pad_maximum_fusion.2), channel_id=1, source_target_pairs={{0,1},{1,0},{2,3},{3,2},{4,5},{5,4},{6,7},{7,6},{8,9},{9,8},{10,11... | collective-permute-start | bytes 1966088 | tf_op jit(solution)/shard_map/ppermute | solution.py:25
  64.0 0.8 copy-start.6
  64.8 8.3 %copy-start.4 = (f32[160,2048]{1,0:T(8,128)}, f32[160,2048]{1,0:T(8,128)S(1)}, u32[]{:S(2)}) copy-start(f32[160,2048]{1,0:T(8,128)S(1)} %get-tuple-element.30.near) | copy-start | bytes 3932164
  64.8 7.5 %collective-permute-start.2 = (bf16[80,2048]{1,0:T(8,128)(2,1)S(1)}, bf16[80,2048]{1,0:T(8,128)(2,1)S(1)}, u32[]{:S(2)}, u32[]{:S(2)}) collective-permute-start(bf16[80,2048]{1,0:T(8,128)(2,1)S(1)} %get-tuple-element.32), channel_id=1, source_target_pairs={{0,6},{1,3},{2,0},{3,5},{4,2},{5,7},{6,4},{7,1},{8,14},{9,11},{10,... | collective-permute-start | bytes 983048 | tf_op jit(solution)/shard_map/ppermute | solution.py:17
  66.1 39.5 %collective-permute-start.11 = (bf16[1024,512]{1,0:T(8,128)(2,1)}, bf16[1024,512]{1,0:T(8,128)(2,1)}, u32[]{:S(2)}, u32[]{:S(2)}) collective-permute-start(bf16[1024,512]{1,0:T(8,128)(2,1)} %bitcast.6.w_own), channel_id=1, source_target_pairs={{0,1},{1,0},{2,3},{3,2},{4,5},{5,4},{6,7},{7,6},{8,9},{9,8},{10,11... | collective-permute-start | bytes 3145736 | tf_op jit(solution)/shard_map/ppermute | solution.py:25
  68.2 22.9 %collective-permute-start.4 = (bf16[80,2048]{1,0:T(8,128)(2,1)}, bf16[80,2048]{1,0:T(8,128)(2,1)}, u32[]{:S(2)}, u32[]{:S(2)}) collective-permute-start(bf16[80,2048]{1,0:T(8,128)(2,1)} %get-tuple-element.33), channel_id=1, source_target_pairs={{0,2},{1,7},{2,4},{3,1},{4,6},{5,3},{6,0},{7,5},{8,10},{9,15},{10,... | collective-permute-start | bytes 983048 | tf_op jit(solution)/shard_map/ppermute | solution.py:17
  68.7 25.2 %collective-permute-start.5 = (bf16[80,2048]{1,0:T(8,128)(2,1)}, bf16[80,2048]{1,0:T(8,128)(2,1)}, u32[]{:S(2)}, u32[]{:S(2)}) collective-permute-start(bf16[80,2048]{1,0:T(8,128)(2,1)} %get-tuple-element.34), channel_id=1, source_target_pairs={{0,6},{1,3},{2,0},{3,5},{4,2},{5,7},{6,4},{7,1},{8,14},{9,11},{10,... | collective-permute-start | bytes 983048 | tf_op jit(solution)/shard_map/ppermute | solution.py:17
  69.7 17.3 %collective-permute-start.6 = (bf16[80,2048]{1,0:T(8,128)(2,1)}, bf16[80,2048]{1,0:T(8,128)(2,1)}, u32[]{:S(2)}, u32[]{:S(2)}) collective-permute-start(bf16[80,2048]{1,0:T(8,128)(2,1)} %get-tuple-element.36), channel_id=1, source_target_pairs={{0,2},{1,7},{2,4},{3,1},{4,6},{5,3},{6,0},{7,5},{8,10},{9,15},{10,... | collective-permute-start | bytes 983048 | tf_op jit(solution)/shard_map/ppermute | solution.py:17
  73.1 20.8 %collective-permute-start.3 = (bf16[80,2048]{1,0:T(8,128)(2,1)}, bf16[80,2048]{1,0:T(8,128)(2,1)}, u32[]{:S(2)}, u32[]{:S(2)}) collective-permute-start(bf16[80,2048]{1,0:T(8,128)(2,1)} %add_convert_fusion.3), channel_id=1, source_target_pairs={{0,6},{1,3},{2,0},{3,5},{4,2},{5,7},{6,4},{7,1},{8,14},{9,11},{10,... | collective-permute-start | bytes 983048 | tf_op jit(solution)/shard_map/ppermute | solution.py:17
  86.0 4.0 %copy-start.7 = (f32[80,2048]{1,0:T(8,128)S(1)}, f32[80,2048]{1,0:T(8,128)}, u32[]{:S(2)}) copy-start(f32[80,2048]{1,0:T(8,128)} %copy-done.6) | copy-start | bytes 1966084
  86.1 11.9 %copy-start.5 = (f32[160,2048]{1,0:T(8,128)S(1)}, f32[160,2048]{1,0:T(8,128)}, u32[]{:S(2)}) copy-start(f32[160,2048]{1,0:T(8,128)} %copy-done.4) | copy-start | bytes 3932164
  87.0 18.7 %collective-permute-start.13 = (bf16[640,512]{1,0:T(8,128)(2,1)}, bf16[640,512]{1,0:T(8,128)(2,1)}, u32[]{:S(2)}, u32[]{:S(2)}) collective-permute-start(bf16[640,512]{1,0:T(8,128)(2,1)} %pad_maximum_fusion.4), channel_id=1, source_target_pairs={{0,1},{1,0},{2,3},{3,2},{4,5},{5,4},{6,7},{7,6},{8,9},{9,8},{10,11... | collective-permute-start | bytes 1966088 | tf_op jit(solution)/shard_map/ppermute | solution.py:25
  91.1 6.8 %collective-permute-start.7 = (bf16[80,2048]{1,0:T(8,128)(2,1)S(1)}, bf16[80,2048]{1,0:T(8,128)(2,1)S(1)}, u32[]{:S(2)}, u32[]{:S(2)}) collective-permute-start(bf16[80,2048]{1,0:T(8,128)(2,1)S(1)} %add_convert_fusion.2), channel_id=1, source_target_pairs={{0,2},{1,7},{2,4},{3,1},{4,6},{5,3},{6,0},{7,5},{8,10},{9,15},{10,... | collective-permute-start | bytes 983048 | tf_op jit(solution)/shard_map/ppermute | solution.py:17
  99.4 1.1 copy-start.2
  101.2 10.5 %collective-permute-start.10 = (bf16[160,1024]{1,0:T(8,128)(2,1)}, bf16[160,1024]{1,0:T(8,128)(2,1)}, u32[]{:S(2)}, u32[]{:S(2)}) collective-permute-start(bf16[160,1024]{1,0:T(8,128)(2,1)} %convert_element_type.85), channel_id=1, source_target_pairs={{0,6},{1,3},{2,0},{3,5},{4,2},{5,7},{6,4},{7,1},{8,14},{9,11},{10,... | collective-permute-start | bytes 983048 | tf_op jit(solution)/shard_map/ppermute | solution.py:17
  102.0 16.1 %collective-permute-start.9 = (bf16[160,1024]{1,0:T(8,128)(2,1)}, bf16[160,1024]{1,0:T(8,128)(2,1)}, u32[]{:S(2)}, u32[]{:S(2)}) collective-permute-start(bf16[160,1024]{1,0:T(8,128)(2,1)} %convert_element_type.85), channel_id=1, source_target_pairs={{0,4},{1,5},{2,6},{3,7},{4,0},{5,1},{6,2},{7,3},{8,12},{9,13},{10,... | collective-permute-start | bytes 983048 | tf_op jit(solution)/shard_map/ppermute | solution.py:17
  105.5 14.9 %collective-permute-start.8 = (bf16[160,1024]{1,0:T(8,128)(2,1)}, bf16[160,1024]{1,0:T(8,128)(2,1)}, u32[]{:S(2)}, u32[]{:S(2)}) collective-permute-start(bf16[160,1024]{1,0:T(8,128)(2,1)} %convert_element_type.85), channel_id=1, source_target_pairs={{0,2},{1,7},{2,4},{3,1},{4,6},{5,3},{6,0},{7,5},{8,10},{9,15},{10,... | collective-permute-start | bytes 983048 | tf_op jit(solution)/shard_map/ppermute | solution.py:17
  110.3 13.7 %collective-permute-start.14 = (bf16[160,1024]{1,0:T(8,128)(2,1)S(1)}, bf16[160,1024]{1,0:T(8,128)(2,1)S(1)}, u32[]{:S(2)}, u32[]{:S(2)}) collective-permute-start(bf16[160,1024]{1,0:T(8,128)(2,1)S(1)} %get-tuple-element.41), channel_id=1, source_target_pairs={{0,6},{1,3},{2,0},{3,5},{4,2},{5,7},{6,4},{7,1},{8,14},{9,11},{10,... | collective-permute-start | bytes 983048 | tf_op jit(solution)/shard_map/ppermute | solution.py:17
  111.7 20.4 %collective-permute-start.15 = (bf16[160,1024]{1,0:T(8,128)(2,1)S(1)}, bf16[160,1024]{1,0:T(8,128)(2,1)S(1)}, u32[]{:S(2)}, u32[]{:S(2)}) collective-permute-start(bf16[160,1024]{1,0:T(8,128)(2,1)S(1)} %get-tuple-element.42), channel_id=1, source_target_pairs={{0,4},{1,5},{2,6},{3,7},{4,0},{5,1},{6,2},{7,3},{8,12},{9,13},{10,... | collective-permute-start | bytes 983048 | tf_op jit(solution)/shard_map/ppermute | solution.py:17
  111.7 22.7 %collective-permute-start.16 = (bf16[160,1024]{1,0:T(8,128)(2,1)S(1)}, bf16[160,1024]{1,0:T(8,128)(2,1)S(1)}, u32[]{:S(2)}, u32[]{:S(2)}) collective-permute-start(bf16[160,1024]{1,0:T(8,128)(2,1)S(1)} %get-tuple-element.43), channel_id=1, source_target_pairs={{0,2},{1,7},{2,4},{3,1},{4,6},{5,3},{6,0},{7,5},{8,10},{9,15},{10,... | collective-permute-start | bytes 983048 | tf_op jit(solution)/shard_map/ppermute | solution.py:17
  122.9 11.5 %copy-start.3 = (f32[160,2048]{1,0:T(8,128)S(1)}, f32[160,2048]{1,0:T(8,128)}, u32[]{:S(2)}) copy-start(f32[160,2048]{1,0:T(8,128)} %copy-done.2) | copy-start | bytes 3932164
  135.5 12.2 %collective-permute-start.17 = (bf16[160,2048]{1,0:T(8,128)(2,1)}, bf16[160,2048]{1,0:T(8,128)(2,1)}, u32[]{:S(2)}, u32[]{:S(2)}) collective-permute-start(bf16[160,2048]{1,0:T(8,128)(2,1)} %shard_map.104), channel_id=1, source_target_pairs={{0,2},{1,7},{2,4},{3,1},{4,6},{5,3},{6,0},{7,5},{8,10},{9,15},{10,... | collective-permute-start | bytes 1966088 | tf_op jit(solution)/shard_map/ppermute | solution.py:17
  138.8 12.3 %collective-permute-start.12 = (bf16[640,512]{1,0:T(8,128)(2,1)}, bf16[640,512]{1,0:T(8,128)(2,1)}, u32[]{:S(2)}, u32[]{:S(2)}) collective-permute-start(bf16[640,512]{1,0:T(8,128)(2,1)} %pad_maximum_fusion.3), channel_id=1, source_target_pairs={{0,1},{1,0},{2,3},{3,2},{4,5},{5,4},{6,7},{7,6},{8,9},{9,8},{10,11... | collective-permute-start | bytes 1966088 | tf_op jit(solution)/shard_map/ppermute | solution.py:25
  141.4 23.1 %collective-permute-start.19 = (bf16[160,2048]{1,0:T(8,128)(2,1)}, bf16[160,2048]{1,0:T(8,128)(2,1)}, u32[]{:S(2)}, u32[]{:S(2)}) collective-permute-start(bf16[160,2048]{1,0:T(8,128)(2,1)} %shard_map.104), channel_id=1, source_target_pairs={{0,6},{1,3},{2,0},{3,5},{4,2},{5,7},{6,4},{7,1},{8,14},{9,11},{10,... | collective-permute-start | bytes 1966088 | tf_op jit(solution)/shard_map/ppermute | solution.py:17
  147.7 16.9 %collective-permute-start.18 = (bf16[160,2048]{1,0:T(8,128)(2,1)}, bf16[160,2048]{1,0:T(8,128)(2,1)}, u32[]{:S(2)}, u32[]{:S(2)}) collective-permute-start(bf16[160,2048]{1,0:T(8,128)(2,1)} %collective-permute-done.17), channel_id=1, source_target_pairs={{0,2},{1,7},{2,4},{3,1},{4,6},{5,3},{6,0},{7,5},{8,10},{9,15},{10,... | collective-permute-start | bytes 1966088 | tf_op jit(solution)/shard_map/ppermute | solution.py:17
  153.7 38.3 %all-to-all-start.1 = ((bf16[32,40,512]{2,1,0:T(8,128)(2,1)}), bf16[32,40,512]{2,1,0:T(8,128)(2,1)}, u32[]{:S(2)}, u32[]{:S(2)}) async-start(bf16[32,40,512]{2,1,0:T(8,128)(2,1)} %bitcast.69), calls=%async_computation.1 | async-start | bytes 2621440 | tf_op jit(solution)/shard_map/all_to_all | solution.py:233
  162.4 40.1 %collective-permute-start.25 = (f32[1024,512]{1,0:T(8,128)}, f32[1024,512]{1,0:T(8,128)}, u32[]{:S(2)}, u32[]{:S(2)}) collective-permute-start(f32[1024,512]{1,0:T(8,128)} %fusion.32), channel_id=1, source_target_pairs={{0,1},{1,0},{2,3},{3,2},{4,5},{5,4},{6,7},{7,6},{8,9},{9,8},{10,11... | collective-permute-start | bytes 6291464 | tf_op jit(solution)/shard_map/ppermute | solution.py:25
  170.1 61.9 %collective-permute-start.24 = (f32[512,2048]{1,0:T(8,128)}, f32[512,2048]{1,0:T(8,128)}, u32[]{:S(2)}, u32[]{:S(2)}) collective-permute-start(f32[512,2048]{1,0:T(8,128)} %fusion.33), channel_id=1, source_target_pairs={{0,1},{1,0},{2,3},{3,2},{4,5},{5,4},{6,7},{7,6},{8,9},{9,8},{10,11... | collective-permute-start | bytes 12582920 | tf_op jit(solution)/shard_map/ppermute | solution.py:25
  174.3 4.7 %collective-permute-start.20 = (bf16[640,512]{1,0:T(8,128)(2,1)S(1)}, bf16[640,512]{1,0:T(8,128)(2,1)}, u32[]{:S(2)}, u32[]{:S(2)}) collective-permute-start(bf16[640,512]{1,0:T(8,128)(2,1)S(1)} %pad_maximum_fusion.5), channel_id=1, source_target_pairs={{0,1},{1,0},{2,3},{3,2},{4,5},{5,4},{6,7},{7,6},{8,9},{9,8},{10,11... | collective-permute-start | bytes 1966088 | tf_op jit(solution)/shard_map/ppermute | solution.py:25
  192.0 37.6 %all-to-all-start.3 = ((bf16[32,40,512]{2,1,0:T(8,128)(2,1)}), bf16[32,40,512]{2,1,0:T(8,128)(2,1)}, u32[]{:S(2)}, u32[]{:S(2)}) async-start(bf16[32,40,512]{2,1,0:T(8,128)(2,1)} %bitcast.16), calls=%async_computation.3 | async-start | bytes 2621440 | tf_op jit(solution)/shard_map/all_to_all | solution.py:233
  197.6 1.3 copy-start.8
  200.7 5.8 %collective-permute-start.21 = (f32[32,40]{1,0:T(8,128)S(1)}, f32[32,40]{1,0:T(8,128)S(1)}, u32[]{:S(2)}, u32[]{:S(2)}) collective-permute-start(f32[32,40]{1,0:T(8,128)S(1)} %reshape.77), channel_id=1, source_target_pairs={{0,1},{1,0},{2,3},{3,2},{4,5},{5,4},{6,7},{7,6},{8,9},{9,8},{10,11... | collective-permute-start | bytes 15368 | tf_op jit(solution)/shard_map/ppermute | solution.py:43
  206.5 3.1 %collective-permute-start.22 = (f32[32,40]{1,0:T(8,128)S(1)}, f32[32,40]{1,0:T(8,128)S(1)}, u32[]{:S(2)}, u32[]{:S(2)}) collective-permute-start(f32[32,40]{1,0:T(8,128)S(1)} %add.263), channel_id=1, source_target_pairs={{0,2},{1,3},{2,0},{3,1},{4,6},{5,7},{6,4},{7,5},{8,10},{9,11},{10,... | collective-permute-start | bytes 15368 | tf_op jit(solution)/shard_map/ppermute | solution.py:43
  209.6 22.4 %copy-start.9 = (bf16[640,512]{1,0:T(8,128)(2,1)S(1)}, bf16[640,512]{1,0:T(8,128)(2,1)}, u32[]{:S(2)}) copy-start(bf16[640,512]{1,0:T(8,128)(2,1)} %pad_maximum_fusion.6) | copy-start | bytes 1966084
  209.6 4.5 %collective-permute-start.23 = (f32[32,40]{1,0:T(8,128)S(1)}, f32[32,40]{1,0:T(8,128)S(1)}, u32[]{:S(2)}, u32[]{:S(2)}) collective-permute-start(f32[32,40]{1,0:T(8,128)S(1)} %add.264), channel_id=1, source_target_pairs={{0,4},{1,5},{2,6},{3,7},{4,0},{5,1},{6,2},{7,3},{8,12},{9,13},{10,... | collective-permute-start | bytes 15368 | tf_op jit(solution)/shard_map/ppermute | solution.py:43

commit v6 on v5

--- a/solution.py
+++ b/solution.py
@@ -15,9 +15,7 @@
 
 def permute_y(v, step, n_y):
     return lax.ppermute(
-        v,
-        "expert",
-        [(2 * y + c, 2 * ((y + (2 * c - 1) * step) % n_y) + c) for y in range(n_y) for c in range(2)],
+        v, "expert", [(2 * y + c, 2 * ((y + step) % n_y) + c) for y in range(n_y) for c in range(2)]
     )
 
 
@@ -173,28 +171,36 @@
     )(near, *got, gate_up)
 
 
-def gather_rows(v, n_y):
-    first = permute_y(v, -1, n_y)
-    far = permute_y(first, -1, n_y)
-    last = permute_y(v, 1, n_y)
-    return [v, first, far, last]
+def permute_by_core(v, n_y):
+    return lax.ppermute(
+        v,
+        "expert",
+        [(2 * y + c, 2 * ((y + 1 - 2 * c) % n_y) + c) for y in range(n_y) for c in range(2)],
+    )
+
+
+def gather_rows(v, core, n_y):
+    dn = permute_y(v, 1, n_y)
+    up = permute_y(v, -1, n_y)
+    far = permute_by_core(jnp.where(core == 0, dn, up), n_y)
+    return [v, up, far, dn]
 
 
 def relative(slab, half, y, n_y):
     rows = slab.shape[0] // (2 * n_y)
     return jnp.concatenate(
         [
-            lax.dynamic_slice_in_dim(slab, (half * n_y + (y + (2 * half - 1) * d) % n_y) * rows, rows, 0)
+            lax.dynamic_slice_in_dim(slab, (half * n_y + (y + d) % n_y) * rows, rows, 0)
             for d in range(n_y)
         ],
         axis=0,
     )
 
 
-def absolute(part, y, core, n_y):
+def absolute(part, y, n_y):
     rows = part.shape[0] // n_y
     return jnp.concatenate(
-        [lax.dynamic_slice_in_dim(part, (((2 * core - 1) * (yy - y)) % n_y) * rows, rows, 0) for yy in range(n_y)],
+        [lax.dynamic_slice_in_dim(part, ((yy - y) % n_y) * rows, rows, 0) for yy in range(n_y)],
         axis=0,
     )
 
@@ -237,7 +243,7 @@
     in_part = permute_core(in_own, n_y)
     out_part = permute_core(out_own, n_y)
 
-    places = lax.rem(y + n_y + (2 * core - 1) * jnp.arange(n_y, dtype=jnp.int32), n_y)
+    places = lax.rem(y + jnp.arange(n_y, dtype=jnp.int32), n_y)
     order = core * n_y + places
     scores_t, places, order, _ = lax.optimization_barrier((scores_t, places, order, token_send))
     score_total = jnp.sum(scores_t, axis=0, keepdims=True)
@@ -277,16 +283,14 @@
     tok_own = relative(token_slab, core, y, n_y)
 
     hid = jnp.concatenate([hidden] + hid_parts, axis=0)
-    out_other = permute_core(absolute(dot(hid, out_part).astype(BF), y, core, n_y), n_y)
-    out_mine = absolute(dot(hid, out_own).astype(BF), y, core, n_y)
+    out_other = permute_core(absolute(dot(hid, out_part).astype(BF), y, n_y), n_y)
+    out_mine = absolute(dot(hid, out_own).astype(BF), y, n_y)
     expert_out = both_halves(out_mine, out_other, core)
     out_back = exchange(expert_out)
 
-    gug = jnp.concatenate(gather_rows(gate_up_grad, n_y), axis=0)
-    other_rows = absolute(dot_t(gug, in_part).astype(BF), y, core, n_y)
-    grad_other = permute_core(other_rows, n_y)
-    y_late, _ = lax.optimization_barrier((y, other_rows))
-    grad_mine = absolute(dot_t(gug, in_own).astype(BF), y_late, core, n_y)
+    gug = jnp.concatenate(gather_rows(gate_up_grad, core, n_y), axis=0)
+    grad_other = permute_core(absolute(dot_t(gug, in_part).astype(BF), y, n_y), n_y)
+    grad_mine = absolute(dot_t(gug, in_own).astype(BF), y, n_y)
     choice_grad = both_halves(grad_mine, grad_other, core)
     grad_back = exchange(choice_grad)
 

time: 242 us -> 247 us (1.021)
  waiting for transfers between devices: 99.9 us -> 108 us
  starting transfers between devices: 61.7 us -> 65.7 us
  matrix products: 43.4 us -> 40.5 us
  other arithmetic: 14.6 us -> 12.1 us
    ppermute x15, waiting for transfers between devices: 28.8 us -> 34.2 us  [the longest x14 33.4 us: permute_y(): lax.ppermute(v, 'expert', [(2 * y + c, 2 * ((y + step) % n_y) + c) for y...]
    ppermute x8, starting transfers between devices: 10.1 us -> 12.8 us  [permute_core(): lax.ppermute(v, 'expert', [(2 * y + c, 2 * y + 1 - c) for y in range(n_y)...]
    select_n x2, other arithmetic: 5.19 us -> 2.53 us  [both_halves(): jnp.where(core == 0, jnp.stack([own, other]), jnp.stack([other, own]))]
  transfers between devices with their start and end apart: 30 -> 30, of which waited for: 15 -> 17; matrix products, arithmetic and copies ran while one was open for 21% -> 18% of each run, Pallas kernels for 5% -> 5%
where the time goes in v6:
time: 247 us; the launch traced here: 244 us
  waiting for transfers between devices  108 us (44%)
  starting transfers between devices  65.7 us (27%)
  matrix products  40.5 us (16%)
  Pallas kernels  12.8 us (5%)
  other arithmetic  12.1 us (5%)
  local copies, waits for them, and re-layouts  3.87 us (2%)
    all_to_all x4, waiting for transfers between devices, exchange(): lax.all_to_all(v, 'dp', split_axis=0, concat_axis=0, tiled=True)  67.4 us
    ppermute x14, waiting for transfers between devices, permute_y(): lax.ppermute(v, 'expert', [(2 * y + c, 2 * ((y + step) % n_y) + c) for y...  33.4 us
    all_to_all x4, starting transfers between devices, exchange(): lax.all_to_all(v, 'dp', split_axis=0, concat_axis=0, tiled=True)  27.7 us
    dot_general x7, matrix products, gather_dot(): return jnp.einsum('rd,rf->df', a, b, preferred_element_type=F32)  25 us
    ppermute x14, starting transfers between devices, permute_y(): lax.ppermute(v, 'expert', [(2 * y + c, 2 * ((y + step) % n_y) + c) for y...  20.3 us
    ppermute x8, starting transfers between devices, permute_core(): lax.ppermute(v, 'expert', [(2 * y + c, 2 * y + 1 - c) for y in range(n_y)...  12.8 us
    dot_general x5, matrix products, dot(): return jnp.dot(a, b, preferred_element_type=F32)  9.49 us
    pallas_call x1, Pallas kernels, partial_halves(): pl.pallas_call(halves_kernel, compiler_params=pltpu.CompilerParams(vmem_l...  6.24 us
  transfers between devices with their start and end apart: 30, of which 17 were waited for; matrix products, arithmetic and copies ran while one was open for 18% of the time, Pallas kernels for 5%

profile of v6, /device:TPU:33, one launch (start us, length us, event | category | flops | bytes accessed | tf_op | source)
XLA Modules:
  0.0 243.7 jit_solution(2071858597137944694)
XLA Ops:
  1.9 2.5 %convolution_convert_fusion = bf16[1280,512]{1,0:T(8,128)(2,1)} fusion(pred[1280,128]{1,0:T(32,128)(4,1)S(1)} %bitcast_compare_fusion, bf16[128,512]{1,0:T(8,128)(2,1)} %param.6), kind=kOutput, calls=%fused_computation.1 | convolution fusion | flops 168427520 | bytes 1605632 | tf_op jit(solution)/shard_map/dot_general | solution.py:29
  4.3 10.8 %all-to-all-start = ((bf16[32,40,512]{2,1,0:T(8,128)(2,1)}), bf16[32,40,512]{2,1,0:T(8,128)(2,1)S(1)}, u32[]{:S(2)}, u32[]{:S(2)}) async-start(bf16[32,40,512]{2,1,0:T(8,128)(2,1)} %bitcast.3), calls=%async_computation | async-start | bytes 2621440 | tf_op jit(solution)/shard_map/all_to_all | solution.py:239
  15.1 1.3 collective-permute-start.1
  16.9 2.0 fusion.34
  18.8 29.4 %all-to-all-done = bf16[32,40,512]{2,1,0:T(8,128)(2,1)S(1)} async-done(((bf16[32,40,512]{2,1,0:T(8,128)(2,1)}), bf16[32,40,512]{2,1,0:T(8,128)(2,1)S(1)}, u32[]{:S(2)}, u32[]{:S(2)}) %all-to-all-start) | async-done | bytes 1310752 | tf_op jit(solution)/shard_map/all_to_all | solution.py:239
  48.2 5.7 %all-to-all-start.2 = ((bf16[32,40,512]{2,1,0:T(8,128)(2,1)}), bf16[32,40,512]{2,1,0:T(8,128)(2,1)S(1)}, u32[]{:S(2)}, u32[]{:S(2)}) async-start(bf16[32,40,512]{2,1,0:T(8,128)(2,1)} %bitcast.69), calls=%async_computation.2 | async-start | bytes 2621440 | tf_op jit(solution)/shard_map/all_to_all | solution.py:239
  54.2 1.8 collective-permute-start
  56.0 1.7 collective-permute-done.part
  57.7 6.2 %shard_map.101 = (f32[160,2048]{1,0:T(8,128)S(1)}, f32[80,2048]{1,0:T(8,128)S(1)}, bf16[80,2048]{1,0:T(8,128)(2,1)}, bf16[80,2048]{1,0:T(8,128)(2,1)S(1)}, bf16[...) custom-call(s32[4]{0:T(128)S(1)} %broadcast_add_fusion.order, ...), custom_call_target="tpu_custom_call" | custom-call | tf_op jit(solution)/shard_map/pallas_call | solution.py:109
  64.0 0.8 copy-done.9
  64.8 1.3 collective-permute-start.2
  66.8 1.4 collective-permute-start.4
  68.2 2.6 %collective-permute-start.6 = (bf16[80,2048]{1,0:T(8,128)(2,1)}, bf16[80,2048]{1,0:T(8,128)(2,1)}, u32[]{:S(2)}, u32[]{:S(2)}) collective-permute-start(bf16[80,2048]{1,0:T(8,128)(2,1)} %get-tuple-element.35), channel_id=1, source_target_pairs={{0,6},{1,7},{2,0},{3,1},{4,2},{5,3},{6,4},{7,5},{8,14},{9,15},{10,... | collective-permute-start | bytes 983048 | tf_op jit(solution)/shard_map/ppermute | solution.py:17
  70.8 4.2 %collective-permute-done.2 = bf16[80,2048]{1,0:T(8,128)(2,1)S(1)} collective-permute-done((bf16[80,2048]{1,0:T(8,128)(2,1)S(1)}, bf16[80,2048]{1,0:T(8,128)(2,1)S(1)}, u32[]{:S(2)}, u32[]{:S(2)}) %collective-permute-start.2) | collective-permute-done | bytes 327712 | tf_op jit(solution)/shard_map/ppermute | solution.py:17
  75.0 0.8 add_convert_fusion.3
  75.9 10.1 %all-to-all-done.2 = bf16[32,40,512]{2,1,0:T(8,128)(2,1)S(1)} async-done(((bf16[32,40,512]{2,1,0:T(8,128)(2,1)}), bf16[32,40,512]{2,1,0:T(8,128)(2,1)S(1)}, u32[]{:S(2)}, u32[]{:S(2)}) %all-to-all-start.2) | async-done | bytes 1310752 | tf_op jit(solution)/shard_map/all_to_all | solution.py:239
  86.1 0.9 pad_maximum_fusion.4
  86.9 3.1 %collective-permute-start.13 = (bf16[640,512]{1,0:T(8,128)(2,1)}, bf16[640,512]{1,0:T(8,128)(2,1)}, u32[]{:S(2)}, u32[]{:S(2)}) collective-permute-start(bf16[640,512]{1,0:T(8,128)(2,1)} %pad_maximum_fusion.4), channel_id=1, source_target_pairs={{0,1},{1,0},{2,3},{3,2},{4,5},{5,4},{6,7},{7,6},{8,9},{9,8},{10,11... | collective-permute-start | bytes 1966088 | tf_op jit(solution)/shard_map/ppermute | solution.py:23
  90.0 1.1 add_convert_fusion.2
  91.1 2.8 %collective-permute-start.7 = (bf16[80,2048]{1,0:T(8,128)(2,1)S(1)}, bf16[80,2048]{1,0:T(8,128)(2,1)S(1)}, u32[]{:S(2)}, u32[]{:S(2)}) collective-permute-start(bf16[80,2048]{1,0:T(8,128)(2,1)S(1)} %add_convert_fusion.2), channel_id=1, source_target_pairs={{0,6},{1,7},{2,0},{3,1},{4,2},{5,3},{6,4},{7,5},{8,14},{9,15},{10,... | collective-permute-start | bytes 983048 | tf_op jit(solution)/shard_map/ppermute | solution.py:17
  93.9 6.7 %collective-permute-done.7.dn_b = bf16[80,2048]{1,0:T(8,128)(2,1)S(1)} collective-permute-done((bf16[80,2048]{1,0:T(8,128)(2,1)S(1)}, bf16[80,2048]{1,0:T(8,128)(2,1)S(1)}, u32[]{:S(2)}, u32[]{:S(2)}) %collective-permute-start.7) | collective-permute-done | bytes 327712 | tf_op jit(solution)/shard_map/ppermute | solution.py:17
  100.7 1.5 shard_map.102
  102.2 1.0 copy-done.3
  103.2 0.8 convert_element_type.85
  104.8 3.8 %collective-permute-start.9 = (bf16[160,1024]{1,0:T(8,128)(2,1)}, bf16[160,1024]{1,0:T(8,128)(2,1)}, u32[]{:S(2)}, u32[]{:S(2)}) collective-permute-start(bf16[160,1024]{1,0:T(8,128)(2,1)} %convert_element_type.85), channel_id=1, source_target_pairs={{0,4},{1,5},{2,6},{3,7},{4,0},{5,1},{6,2},{7,3},{8,12},{9,13},{10,... | collective-permute-start | bytes 983048 | tf_op jit(solution)/shard_map/ppermute | solution.py:17
  108.6 4.7 %shard_map.103 = (f32[160,1024]{1,0:T(8,128)S(1)}, bf16[160,1024]{1,0:T(8,128)(2,1)S(1)}, bf16[160,1024]{1,0:T(8,128)(2,1)S(1)}, bf16[160,1024]{1,0:T(8,128)(2,1)S(1)}) custom-call(s32[4]{0:T(128)S(1)} %broadcast_add_fusion.order, bf16[1280,512]{1,0:T(8,128)(2,1)S(1)} %bitcast.56, bf16[1280,512]{1,0:T(8,128)(2,1)S(1)} %bitcast.57, ...), custom_call_target="tpu_custom_call" | custom-call | tf_op jit(solution)/shard_map/pallas_call | solution.py:70
  113.3 1.5 collective-permute-start.14
  114.8 2.5 %collective-permute-start.16 = (bf16[160,1024]{1,0:T(8,128)(2,1)S(1)}, bf16[160,1024]{1,0:T(8,128)(2,1)S(1)}, u32[]{:S(2)}, u32[]{:S(2)}) collective-permute-start(bf16[160,1024]{1,0:T(8,128)(2,1)S(1)} %get-tuple-element.42), channel_id=1, source_target_pairs={{0,6},{1,7},{2,0},{3,1},{4,2},{5,3},{6,4},{7,5},{8,14},{9,15},{10,... | collective-permute-start | bytes 983048 | tf_op jit(solution)/shard_map/ppermute | solution.py:17
  117.3 5.3 %collective-permute-done.9 = bf16[160,1024]{1,0:T(8,128)(2,1)} collective-permute-done((bf16[160,1024]{1,0:T(8,128)(2,1)}, bf16[160,1024]{1,0:T(8,128)(2,1)}, u32[]{:S(2)}, u32[]{:S(2)}) %collective-permute-start.9) | collective-permute-done | bytes 327712 | tf_op jit(solution)/shard_map/ppermute | solution.py:17
  122.6 0.9 collective-permute-done.8
  123.5 2.5 %convolution_convert_fusion.3 = bf16[640,512]{1,0:T(8,128)(2,1)S(1)} fusion(bf16[1024,512]{1,0:T(8,128)(2,1)} %collective-permute-done.11.w_part, bf16[160,1024]{1,0:T(8,128)(2,1)} %collective-permute-done.10, bf16[160,1024]{1,0:T(8,128)(2,1)} %collective-permute-done.9, bf16[160,1024]{1,0:T(8,128)(2,1)} %collective-permute-done.8, ...), kind=kOutput, calls=%fused_computation.11 | convolution fusion | flops 676659200 | bytes 3014656 | tf_op jit(solution)/shard_map/dot_general | solution.py:29
  126.0 3.6 %collective-permute-done.14.first = bf16[160,1024]{1,0:T(8,128)(2,1)S(1)} collective-permute-done((bf16[160,1024]{1,0:T(8,128)(2,1)S(1)}, bf16[160,1024]{1,0:T(8,128)(2,1)S(1)}, u32[]{:S(2)}, u32[]{:S(2)}) %collective-permute-start.14) | collective-permute-done | bytes 327712 | tf_op jit(solution)/shard_map/ppermute | solution.py:17
  129.6 6.9 %collective-permute-done.15.second = bf16[160,1024]{1,0:T(8,128)(2,1)S(1)} collective-permute-done((bf16[160,1024]{1,0:T(8,128)(2,1)S(1)}, bf16[160,1024]{1,0:T(8,128)(2,1)S(1)}, u32[]{:S(2)}, u32[]{:S(2)}) %collective-permute-start.15) | collective-permute-done | bytes 327712 | tf_op jit(solution)/shard_map/ppermute | solution.py:17
  137.0 2.0 collective-permute-start.18
  139.0 1.4 collective-permute-start.17
  140.5 2.0 collective-permute-start.12
  142.5 3.8 %fusion.32 = f32[1024,512]{1,0:T(8,128)} fusion(bf16[640,512]{1,0:T(8,128)(2,1)} %collective-permute-done.13.part, bf16[160,1024]{1,0:T(8,128)(2,1)} %collective-permute-done.10, bf16[160,1024]{1,0:T(8,128)(2,1)} %collective-permute-done.9, bf16[160,1024]{1,0:T(8,128)(2,1)} %collective-permute-done.8, bf16[160,1024]{1,0:T(8,128)(2,1)} %convert_element_type.85), kind=kOutput, calls=%fused_computation.106 | convolution fusion | flops 676331520 | bytes 4063232 | tf_op jit(solution)/shard_map/rd,rf->df/dot_general | solution.py:37
  146.3 2.5 %convolution_convert_fusion.4 = bf16[640,512]{1,0:T(8,128)(2,1)S(1)} fusion(bf16[1,1024,512]{2,1,0:T(8,128)(2,1)} %param.10, bf16[160,1024]{1,0:T(8,128)(2,1)} %collective-permute-done.10, bf16[160,1024]{1,0:T(8,128)(2,1)} %collective-permute-done.9, bf16[160,1024]{1,0:T(8,128)(2,1)} %collective-permute-done.8, bf16[160,1024]{1,0:T(8,128)(2,1)} %convert_element_type.85), kind=kOutput, calls=%fused_computation.12 | convolution fusion | flops 676659200 | bytes 3014656 | tf_op jit(solution)/shard_map/dot_general | solution.py:29
  148.8 5.0 %collective-permute-done.18 = bf16[160,2048]{1,0:T(8,128)(2,1)S(1)} collective-permute-done((bf16[160,2048]{1,0:T(8,128)(2,1)S(1)}, bf16[160,2048]{1,0:T(8,128)(2,1)S(1)}, u32[]{:S(2)}, u32[]{:S(2)}) %collective-permute-start.18) | collective-permute-done | bytes 655392 | tf_op jit(solution)/shard_map/ppermute | solution.py:17
  154.5 1.0 broadcast_select_fusion
  155.5 1.8 collective-permute-start.19
  157.5 0.9 pad_maximum_fusion.6
  158.4 1.3 maximum_select_fusion
  159.7 5.1 %all-to-all-start.1 = ((bf16[32,40,512]{2,1,0:T(8,128)(2,1)}), bf16[32,40,512]{2,1,0:T(8,128)(2,1)}, u32[]{:S(2)}, u32[]{:S(2)}) async-start(bf16[32,40,512]{2,1,0:T(8,128)(2,1)} %bitcast.71), calls=%async_computation.1 | async-start | bytes 2621440 | tf_op jit(solution)/shard_map/all_to_all | solution.py:239
  165.6 5.2 %fusion.33 = f32[512,2048]{1,0:T(8,128)} fusion(bf16[640,512]{1,0:T(8,128)(2,1)S(1)} %collective-permute-done.part, bf16[160,2048]{1,0:T(8,128)(2,1)S(1)} %copy-done.13, bf16[160,2048]{1,0:T(8,128)(2,1)} %collective-permute-done.19, bf16[160,2048]{1,0:T(8,128)(2,1)} %copy-done.15, bf16[160,2048]{1,0:T(8,128)(2,1)S(1)} %copy-done.8), kind=kOutput, calls=%fused_computation.107 | convolution fusion | flops 1352663040 | bytes 7471104 | tf_op jit(solution)/shard_map/rd,rf->df/dot_general | solution.py:37
  170.7 3.8 %collective-permute-start.24 = (f32[512,2048]{1,0:T(8,128)}, f32[512,2048]{1,0:T(8,128)}, u32[]{:S(2)}, u32[]{:S(2)}) collective-permute-start(f32[512,2048]{1,0:T(8,128)} %fusion.33), channel_id=1, source_target_pairs={{0,1},{1,0},{2,3},{3,2},{4,5},{5,4},{6,7},{7,6},{8,9},{9,8},{10,11... | collective-permute-start | bytes 12582920 | tf_op jit(solution)/shard_map/ppermute | solution.py:23
  174.5 3.4 %convolution_convert_fusion.1 = bf16[640,512]{1,0:T(8,128)(2,1)S(1)} fusion(bf16[512,2048]{1,0:T(8,128)(2,1)} %collective-permute-done.1.w_part, bf16[160,2048]{1,0:T(8,128)(2,1)S(1)} %copy-done.13, bf16[160,2048]{1,0:T(8,128)(2,1)} %collective-permute-done.19, bf16[160,2048]{1,0:T(8,128)(2,1)S(1)} %copy-done.16, bf16[160,2048]{1,0:T(8,128)(2,1)S(1)} %copy-done.8), kind=kOutput, calls=%fused_computation.9 | convolution fusion | flops 1352990720 | bytes 5373952 | tf_op jit(solution)/shard_map/rd,fd->rf/dot_general | solution.py:33
  177.9 2.6 %convolution_convert_fusion.2 = bf16[640,512]{1,0:T(8,128)(2,1)S(1)} fusion(bf16[1,512,2048]{2,1,0:T(8,128)(2,1)S(1)} %copy-done.2, bf16[160,2048]{1,0:T(8,128)(2,1)S(1)} %copy-done.13, bf16[160,2048]{1,0:T(8,128)(2,1)} %collective-permute-done.19, bf16[160,2048]{1,0:T(8,128)(2,1)S(1)} %copy-done.16, bf16[160,2048]{1,0:T(8,128)(2,1)S(1)} %copy-done.8), kind=kOutput, calls=%fused_computation.10 | convolution fusion | flops 1352990720 | bytes 5373952 | tf_op jit(solution)/shard_map/rd,fd->rf/dot_general | solution.py:33
  180.9 1.9 collective-permute-done.20
  182.9 1.3 maximum_select_fusion.1
  184.1 13.4 %all-to-all-done.1 = bf16[32,40,512]{2,1,0:T(8,128)(2,1)} async-done(((bf16[32,40,512]{2,1,0:T(8,128)(2,1)}), bf16[32,40,512]{2,1,0:T(8,128)(2,1)}, u32[]{:S(2)}, u32[]{:S(2)}) %all-to-all-start.1) | async-done | bytes 1310752 | tf_op jit(solution)/shard_map/all_to_all | solution.py:239
  197.5 6.2 %all-to-all-start.3 = ((bf16[32,40,512]{2,1,0:T(8,128)(2,1)}), bf16[32,40,512]{2,1,0:T(8,128)(2,1)}, u32[]{:S(2)}, u32[]{:S(2)}) async-start(bf16[32,40,512]{2,1,0:T(8,128)(2,1)} %bitcast.70), calls=%async_computation.3 | async-start | bytes 2621440 | tf_op jit(solution)/shard_map/all_to_all | solution.py:239
  203.8 1.2 copy-done.11
  205.0 1.7 fusion.1
  206.9 1.8 collective-permute-start.21
  208.7 4.0 %fusion.2 = bf16[1,1024,512]{2,1,0:T(8,128)(2,1)} fusion(f32[1024,512]{1,0:T(8,128)} %collective-permute-done.25, bf16[160,512]{1,0:T(8,128)(2,1)S(1)} %get-tuple-element.52, bf16[160,512]{1,0:T(8,128)(2,1)S(1)} %get-tuple-element.53, bf16[160,512]{1,0:T(8,128)(2,1)S(1)} %get-tuple-element.54, bf16[160,512]{1,0:T(8,128)(2,1)S(1)} %get-tuple-element.51, ...), kind=kOutput, calls=%fused_computation.8 | convolution fusion | flops 680001536 | bytes 5111808 | tf_op jit(solution)/shard_map/rd,rf->df/dot_general | solution.py:37
  212.8 1.7 convolution_bitcast_fusion.1
  214.5 1.3 collective-permute-done.22
  215.8 1.1 collective-permute-start.23
  216.8 2.4 fusion.5
  219.2 1.2 collective-permute-done.23
  221.3 14.5 %all-to-all-done.3 = bf16[32,40,512]{2,1,0:T(8,128)(2,1)} async-done(((bf16[32,40,512]{2,1,0:T(8,128)(2,1)}), bf16[32,40,512]{2,1,0:T(8,128)(2,1)}, u32[]{:S(2)}, u32[]{:S(2)}) %all-to-all-start.3) | async-done | bytes 1310752 | tf_op jit(solution)/shard_map/all_to_all | solution.py:239
  235.8 2.4 fusion.4
  238.2 5.5 %fusion = bf16[1,512,2048]{2,1,0:T(8,128)(2,1)} fusion(f32[512,2048]{1,0:T(8,128)} %collective-permute-done.24, bf16[640,512]{1,0:T(8,128)(2,1)S(1)} %copy-done.18, bf16[160,2048]{1,0:T(8,128)(2,1)S(1)} %copy-done.14, bf16[160,2048]{1,0:T(8,128)(2,1)} %collective-permute-done.19, bf16[160,2048]{1,0:T(8,128)(2,1)S(1)} %copy-done.17, ...), kind=kOutput, calls=%fused_computation.2 | convolution fusion | flops 1354760192 | bytes 9568256 | tf_op jit(solution)/shard_map/rd,rf->df/dot_general | solution.py:37
  (95 shorter events, 7.3 us)
Async XLA Ops:
  0.6 16.2 %copy-start = (bf16[128,512]{1,0:T(8,128)(2,1)S(1)}, bf16[128,512]{1,0:T(8,128)(2,1)}, u32[]{:S(2)}) copy-start(bf16[128,512]{1,0:T(8,128)(2,1)} %param.11) | copy-start | bytes 393220
  4.3 12.1 %copy-start.19 = (f32[128,8]{0,1:T(8,128)S(1)}, f32[128,8]{0,1:T(8,128)}, u32[]{:S(2)}) copy-start(f32[128,8]{0,1:T(8,128)} %param.8) | copy-start | bytes 12292
  4.3 12.1 %copy-start.20 = (s32[128,8]{0,1:T(8,128)S(1)}, s32[128,8]{0,1:T(8,128)}, u32[]{:S(2)}) copy-start(s32[128,8]{0,1:T(8,128)} %param.7) | copy-start | bytes 12292
  4.3 43.9 %all-to-all-start = ((bf16[32,40,512]{2,1,0:T(8,128)(2,1)}), bf16[32,40,512]{2,1,0:T(8,128)(2,1)S(1)}, u32[]{:S(2)}, u32[]{:S(2)}) async-start(bf16[32,40,512]{2,1,0:T(8,128)(2,1)} %bitcast.3), calls=%async_computation | async-start | bytes 2621440 | tf_op jit(solution)/shard_map/all_to_all | solution.py:239
  15.1 40.9 %collective-permute-start.1 = (bf16[512,2048]{1,0:T(8,128)(2,1)}, bf16[512,2048]{1,0:T(8,128)(2,1)}, u32[]{:S(2)}, u32[]{:S(2)}) collective-permute-start(bf16[512,2048]{1,0:T(8,128)(2,1)} %bitcast.67), channel_id=1, source_target_pairs={{0,1},{1,0},{2,3},{3,2},{4,5},{5,4},{6,7},{7,6},{8,9},{9,8},{10,11... | collective-permute-start | bytes 6291464 | tf_op jit(solution)/shard_map/ppermute | solution.py:23
  48.2 37.8 %all-to-all-start.2 = ((bf16[32,40,512]{2,1,0:T(8,128)(2,1)}), bf16[32,40,512]{2,1,0:T(8,128)(2,1)S(1)}, u32[]{:S(2)}, u32[]{:S(2)}) async-start(bf16[32,40,512]{2,1,0:T(8,128)(2,1)} %bitcast.69), calls=%async_computation.2 | async-start | bytes 2621440 | tf_op jit(solution)/shard_map/all_to_all | solution.py:239
  54.1 3.7 %copy-start.1 = (bf16[1,512,2048]{2,1,0:T(8,128)(2,1)S(1)}, bf16[1,512,2048]{2,1,0:T(8,128)(2,1)}, u32[]{:S(2)}) copy-start(bf16[1,512,2048]{2,1,0:T(8,128)(2,1)} %param.9) | copy-start | bytes 6291460
  54.2 3.5 %collective-permute-start = (bf16[640,512]{1,0:T(8,128)(2,1)S(1)}, bf16[640,512]{1,0:T(8,128)(2,1)S(1)}, u32[]{:S(2)}, u32[]{:S(2)}) collective-permute-start(bf16[640,512]{1,0:T(8,128)(2,1)S(1)} %pad_maximum_fusion.2), channel_id=1, source_target_pairs={{0,1},{1,0},{2,3},{3,2},{4,5},{5,4},{6,7},{7,6},{8,9},{9,8},{10,11... | collective-permute-start | bytes 1966088 | tf_op jit(solution)/shard_map/ppermute | solution.py:23
  64.0 0.8 copy-start.9
  64.8 11.0 %copy-start.5 = (f32[160,2048]{1,0:T(8,128)}, f32[160,2048]{1,0:T(8,128)S(1)}, u32[]{:S(2)}) copy-start(f32[160,2048]{1,0:T(8,128)S(1)} %get-tuple-element.29.near) | copy-start | bytes 3932164
  64.8 10.2 %collective-permute-start.2 = (bf16[80,2048]{1,0:T(8,128)(2,1)S(1)}, bf16[80,2048]{1,0:T(8,128)(2,1)S(1)}, u32[]{:S(2)}, u32[]{:S(2)}) collective-permute-start(bf16[80,2048]{1,0:T(8,128)(2,1)S(1)} %get-tuple-element.31), channel_id=1, source_target_pairs={{0,2},{1,3},{2,4},{3,5},{4,6},{5,7},{6,0},{7,1},{8,10},{9,11},{10,... | collective-permute-start | bytes 983048 | tf_op jit(solution)/shard_map/ppermute | solution.py:17
  66.1 42.5 %collective-permute-start.11 = (bf16[1024,512]{1,0:T(8,128)(2,1)}, bf16[1024,512]{1,0:T(8,128)(2,1)}, u32[]{:S(2)}, u32[]{:S(2)}) collective-permute-start(bf16[1024,512]{1,0:T(8,128)(2,1)} %bitcast.6.w_own), channel_id=1, source_target_pairs={{0,1},{1,0},{2,3},{3,2},{4,5},{5,4},{6,7},{7,6},{8,9},{9,8},{10,11... | collective-permute-start | bytes 3145736 | tf_op jit(solution)/shard_map/ppermute | solution.py:23
  66.8 24.3 %collective-permute-start.4 = (bf16[80,2048]{1,0:T(8,128)(2,1)}, bf16[80,2048]{1,0:T(8,128)(2,1)}, u32[]{:S(2)}, u32[]{:S(2)}) collective-permute-start(bf16[80,2048]{1,0:T(8,128)(2,1)} %get-tuple-element.32), channel_id=1, source_target_pairs={{0,6},{1,7},{2,0},{3,1},{4,2},{5,3},{6,4},{7,5},{8,14},{9,15},{10,... | collective-permute-start | bytes 983048 | tf_op jit(solution)/shard_map/ppermute | solution.py:17
  68.1 25.8 %collective-permute-start.5 = (bf16[80,2048]{1,0:T(8,128)(2,1)}, bf16[80,2048]{1,0:T(8,128)(2,1)}, u32[]{:S(2)}, u32[]{:S(2)}) collective-permute-start(bf16[80,2048]{1,0:T(8,128)(2,1)} %get-tuple-element.33), channel_id=1, source_target_pairs={{0,2},{1,3},{2,4},{3,5},{4,6},{5,7},{6,0},{7,1},{8,10},{9,11},{10,... | collective-permute-start | bytes 983048 | tf_op jit(solution)/shard_map/ppermute | solution.py:17
  68.2 18.7 %collective-permute-start.6 = (bf16[80,2048]{1,0:T(8,128)(2,1)}, bf16[80,2048]{1,0:T(8,128)(2,1)}, u32[]{:S(2)}, u32[]{:S(2)}) collective-permute-start(bf16[80,2048]{1,0:T(8,128)(2,1)} %get-tuple-element.35), channel_id=1, source_target_pairs={{0,6},{1,7},{2,0},{3,1},{4,2},{5,3},{6,4},{7,5},{8,14},{9,15},{10,... | collective-permute-start | bytes 983048 | tf_op jit(solution)/shard_map/ppermute | solution.py:17
  75.8 18.1 %collective-permute-start.3 = (bf16[80,2048]{1,0:T(8,128)(2,1)}, bf16[80,2048]{1,0:T(8,128)(2,1)}, u32[]{:S(2)}, u32[]{:S(2)}) collective-permute-start(bf16[80,2048]{1,0:T(8,128)(2,1)} %add_convert_fusion.3), channel_id=1, source_target_pairs={{0,2},{1,3},{2,4},{3,5},{4,6},{5,7},{6,0},{7,1},{8,10},{9,11},{10,... | collective-permute-start | bytes 983048 | tf_op jit(solution)/shard_map/ppermute | solution.py:17
  86.0 4.0 %copy-start.10 = (f32[80,2048]{1,0:T(8,128)S(1)}, f32[80,2048]{1,0:T(8,128)}, u32[]{:S(2)}) copy-start(f32[80,2048]{1,0:T(8,128)} %copy-done.9) | copy-start | bytes 1966084
  86.0 14.6 %copy-start.6 = (f32[160,2048]{1,0:T(8,128)S(1)}, f32[160,2048]{1,0:T(8,128)}, u32[]{:S(2)}) copy-start(f32[160,2048]{1,0:T(8,128)} %copy-done.5) | copy-start | bytes 3932164
  86.9 21.7 %collective-permute-start.13 = (bf16[640,512]{1,0:T(8,128)(2,1)}, bf16[640,512]{1,0:T(8,128)(2,1)}, u32[]{:S(2)}, u32[]{:S(2)}) collective-permute-start(bf16[640,512]{1,0:T(8,128)(2,1)} %pad_maximum_fusion.4), channel_id=1, source_target_pairs={{0,1},{1,0},{2,3},{3,2},{4,5},{5,4},{6,7},{7,6},{8,9},{9,8},{10,11... | collective-permute-start | bytes 1966088 | tf_op jit(solution)/shard_map/ppermute | solution.py:23
  91.1 9.6 %collective-permute-start.7 = (bf16[80,2048]{1,0:T(8,128)(2,1)S(1)}, bf16[80,2048]{1,0:T(8,128)(2,1)S(1)}, u32[]{:S(2)}, u32[]{:S(2)}) collective-permute-start(bf16[80,2048]{1,0:T(8,128)(2,1)S(1)} %add_convert_fusion.2), channel_id=1, source_target_pairs={{0,6},{1,7},{2,0},{3,1},{4,2},{5,3},{6,4},{7,5},{8,14},{9,15},{10,... | collective-permute-start | bytes 983048 | tf_op jit(solution)/shard_map/ppermute | solution.py:17
  102.1 1.1 copy-start.3
  104.0 10.8 %collective-permute-start.10 = (bf16[160,1024]{1,0:T(8,128)(2,1)}, bf16[160,1024]{1,0:T(8,128)(2,1)}, u32[]{:S(2)}, u32[]{:S(2)}) collective-permute-start(bf16[160,1024]{1,0:T(8,128)(2,1)} %convert_element_type.85), channel_id=1, source_target_pairs={{0,2},{1,3},{2,4},{3,5},{4,6},{5,7},{6,0},{7,1},{8,10},{9,11},{10,... | collective-permute-start | bytes 983048 | tf_op jit(solution)/shard_map/ppermute | solution.py:17
  104.8 17.8 %collective-permute-start.9 = (bf16[160,1024]{1,0:T(8,128)(2,1)}, bf16[160,1024]{1,0:T(8,128)(2,1)}, u32[]{:S(2)}, u32[]{:S(2)}) collective-permute-start(bf16[160,1024]{1,0:T(8,128)(2,1)} %convert_element_type.85), channel_id=1, source_target_pairs={{0,4},{1,5},{2,6},{3,7},{4,0},{5,1},{6,2},{7,3},{8,12},{9,13},{10,... | collective-permute-start | bytes 983048 | tf_op jit(solution)/shard_map/ppermute | solution.py:17
  108.6 14.9 %collective-permute-start.8 = (bf16[160,1024]{1,0:T(8,128)(2,1)}, bf16[160,1024]{1,0:T(8,128)(2,1)}, u32[]{:S(2)}, u32[]{:S(2)}) collective-permute-start(bf16[160,1024]{1,0:T(8,128)(2,1)} %convert_element_type.85), channel_id=1, source_target_pairs={{0,6},{1,7},{2,0},{3,1},{4,2},{5,3},{6,4},{7,5},{8,14},{9,15},{10,... | collective-permute-start | bytes 983048 | tf_op jit(solution)/shard_map/ppermute | solution.py:17
  113.3 16.4 %collective-permute-start.14 = (bf16[160,1024]{1,0:T(8,128)(2,1)S(1)}, bf16[160,1024]{1,0:T(8,128)(2,1)S(1)}, u32[]{:S(2)}, u32[]{:S(2)}) collective-permute-start(bf16[160,1024]{1,0:T(8,128)(2,1)S(1)} %get-tuple-element.40), channel_id=1, source_target_pairs={{0,2},{1,3},{2,4},{3,5},{4,6},{5,7},{6,0},{7,1},{8,10},{9,11},{10,... | collective-permute-start | bytes 983048 | tf_op jit(solution)/shard_map/ppermute | solution.py:17
  114.8 21.7 %collective-permute-start.15 = (bf16[160,1024]{1,0:T(8,128)(2,1)S(1)}, bf16[160,1024]{1,0:T(8,128)(2,1)S(1)}, u32[]{:S(2)}, u32[]{:S(2)}) collective-permute-start(bf16[160,1024]{1,0:T(8,128)(2,1)S(1)} %get-tuple-element.41), channel_id=1, source_target_pairs={{0,4},{1,5},{2,6},{3,7},{4,0},{5,1},{6,2},{7,3},{8,12},{9,13},{10,... | collective-permute-start | bytes 983048 | tf_op jit(solution)/shard_map/ppermute | solution.py:17
  114.8 21.7 %collective-permute-start.16 = (bf16[160,1024]{1,0:T(8,128)(2,1)S(1)}, bf16[160,1024]{1,0:T(8,128)(2,1)S(1)}, u32[]{:S(2)}, u32[]{:S(2)}) collective-permute-start(bf16[160,1024]{1,0:T(8,128)(2,1)S(1)} %get-tuple-element.42), channel_id=1, source_target_pairs={{0,6},{1,7},{2,0},{3,1},{4,2},{5,3},{6,4},{7,5},{8,14},{9,15},{10,... | collective-permute-start | bytes 983048 | tf_op jit(solution)/shard_map/ppermute | solution.py:17
  126.0 10.6 %copy-start.4 = (f32[160,2048]{1,0:T(8,128)S(1)}, f32[160,2048]{1,0:T(8,128)}, u32[]{:S(2)}) copy-start(f32[160,2048]{1,0:T(8,128)} %copy-done.3) | copy-start | bytes 3932164
  137.0 9.3 %copy-start.7 = (bf16[160,2048]{1,0:T(8,128)(2,1)}, bf16[160,2048]{1,0:T(8,128)(2,1)S(1)}, u32[]{:S(2)}) copy-start(bf16[160,2048]{1,0:T(8,128)(2,1)S(1)} %shard_map.104) | copy-start | bytes 1966084
  137.0 16.8 %collective-permute-start.18 = (bf16[160,2048]{1,0:T(8,128)(2,1)S(1)}, bf16[160,2048]{1,0:T(8,128)(2,1)S(1)}, u32[]{:S(2)}, u32[]{:S(2)}) collective-permute-start(bf16[160,2048]{1,0:T(8,128)(2,1)S(1)} %shard_map.104), channel_id=1, source_target_pairs={{0,2},{1,3},{2,4},{3,5},{4,6},{5,7},{6,0},{7,1},{8,10},{9,11},{10,... | collective-permute-start | bytes 1966088 | tf_op jit(solution)/shard_map/ppermute | solution.py:17
  139.0 15.5 %collective-permute-start.17 = (bf16[160,2048]{1,0:T(8,128)(2,1)S(1)}, bf16[160,2048]{1,0:T(8,128)(2,1)S(1)}, u32[]{:S(2)}, u32[]{:S(2)}) collective-permute-start(bf16[160,2048]{1,0:T(8,128)(2,1)S(1)} %shard_map.104), channel_id=1, source_target_pairs={{0,6},{1,7},{2,0},{3,1},{4,2},{5,3},{6,4},{7,5},{8,14},{9,15},{10,... | collective-permute-start | bytes 1966088 | tf_op jit(solution)/shard_map/ppermute | solution.py:17
  140.5 17.9 %collective-permute-start.12 = (bf16[640,512]{1,0:T(8,128)(2,1)S(1)}, bf16[640,512]{1,0:T(8,128)(2,1)S(1)}, u32[]{:S(2)}, u32[]{:S(2)}) collective-permute-start(bf16[640,512]{1,0:T(8,128)(2,1)S(1)} %pad_maximum_fusion.3), channel_id=1, source_target_pairs={{0,1},{1,0},{2,3},{3,2},{4,5},{5,4},{6,7},{7,6},{8,9},{9,8},{10,11... | collective-permute-start | bytes 1966088 | tf_op jit(solution)/shard_map/ppermute | solution.py:23
  146.3 62.4 %collective-permute-start.25 = (f32[1024,512]{1,0:T(8,128)}, f32[1024,512]{1,0:T(8,128)}, u32[]{:S(2)}, u32[]{:S(2)}) collective-permute-start(f32[1024,512]{1,0:T(8,128)} %fusion.32), channel_id=1, source_target_pairs={{0,1},{1,0},{2,3},{3,2},{4,5},{5,4},{6,7},{7,6},{8,9},{9,8},{10,11... | collective-permute-start | bytes 6291464 | tf_op jit(solution)/shard_map/ppermute | solution.py:23
  153.8 3.6 %copy-start.12 = (bf16[160,2048]{1,0:T(8,128)(2,1)}, bf16[160,2048]{1,0:T(8,128)(2,1)S(1)}, u32[]{:S(2)}) copy-start(bf16[160,2048]{1,0:T(8,128)(2,1)S(1)} %collective-permute-done.18) | copy-start | bytes 1966084
  154.5 2.9 %copy-start.15 = (bf16[160,2048]{1,0:T(8,128)(2,1)}, bf16[160,2048]{1,0:T(8,128)(2,1)S(1)}, u32[]{:S(2)}) copy-start(bf16[160,2048]{1,0:T(8,128)(2,1)S(1)} %collective-permute-done.17) | copy-start | bytes 1966084
  155.5 10.0 %collective-permute-start.19 = (bf16[160,2048]{1,0:T(8,128)(2,1)}, bf16[160,2048]{1,0:T(8,128)(2,1)}, u32[]{:S(2)}, u32[]{:S(2)}) collective-permute-start(bf16[160,2048]{1,0:T(8,128)(2,1)} %broadcast_select_fusion), channel_id=1, source_target_pairs={{0,2},{1,7},{2,4},{3,1},{4,6},{5,3},{6,0},{7,5},{8,10},{9,15},{10,... | collective-permute-start | bytes 1966088 | tf_op jit(solution)/shard_map/ppermute | solution.py:175
  159.7 5.9 %copy-start.8 = (bf16[160,2048]{1,0:T(8,128)(2,1)S(1)}, bf16[160,2048]{1,0:T(8,128)(2,1)}, u32[]{:S(2)}) copy-start(bf16[160,2048]{1,0:T(8,128)(2,1)} %copy-done.7) | copy-start | bytes 1966084
  159.7 5.9 %copy-start.13 = (bf16[160,2048]{1,0:T(8,128)(2,1)S(1)}, bf16[160,2048]{1,0:T(8,128)(2,1)}, u32[]{:S(2)}) copy-start(bf16[160,2048]{1,0:T(8,128)(2,1)} %copy-done.12) | copy-start | bytes 1966084
  159.7 37.8 %all-to-all-start.1 = ((bf16[32,40,512]{2,1,0:T(8,128)(2,1)}), bf16[32,40,512]{2,1,0:T(8,128)(2,1)}, u32[]{:S(2)}, u32[]{:S(2)}) async-start(bf16[32,40,512]{2,1,0:T(8,128)(2,1)} %bitcast.71), calls=%async_computation.1 | async-start | bytes 2621440 | tf_op jit(solution)/shard_map/all_to_all | solution.py:239
  164.8 9.7 %copy-start.16 = (bf16[160,2048]{1,0:T(8,128)(2,1)S(1)}, bf16[160,2048]{1,0:T(8,128)(2,1)}, u32[]{:S(2)}) copy-start(bf16[160,2048]{1,0:T(8,128)(2,1)} %copy-done.15) | copy-start | bytes 1966084
  170.7 7.1 %copy-start.2 = (bf16[1,512,2048]{2,1,0:T(8,128)(2,1)S(1)}, bf16[1,512,2048]{2,1,0:T(8,128)(2,1)}, u32[]{:S(2)}) copy-start(bf16[1,512,2048]{2,1,0:T(8,128)(2,1)} %param.9) | copy-start | bytes 6291460
  170.7 67.5 %collective-permute-start.24 = (f32[512,2048]{1,0:T(8,128)}, f32[512,2048]{1,0:T(8,128)}, u32[]{:S(2)}, u32[]{:S(2)}) collective-permute-start(f32[512,2048]{1,0:T(8,128)} %fusion.33), channel_id=1, source_target_pairs={{0,1},{1,0},{2,3},{3,2},{4,5},{5,4},{6,7},{7,6},{8,9},{9,8},{10,11... | collective-permute-start | bytes 12582920 | tf_op jit(solution)/shard_map/ppermute | solution.py:23
  180.7 2.2 collective-permute-start.20
  197.5 38.3 %all-to-all-start.3 = ((bf16[32,40,512]{2,1,0:T(8,128)(2,1)}), bf16[32,40,512]{2,1,0:T(8,128)(2,1)}, u32[]{:S(2)}, u32[]{:S(2)}) async-start(bf16[32,40,512]{2,1,0:T(8,128)(2,1)} %bitcast.70), calls=%async_computation.3 | async-start | bytes 2621440 | tf_op jit(solution)/shard_map/all_to_all | solution.py:239
  203.7 1.3 copy-start.11
  206.9 5.8 %collective-permute-start.21 = (f32[32,40]{1,0:T(8,128)S(1)}, f32[32,40]{1,0:T(8,128)S(1)}, u32[]{:S(2)}, u32[]{:S(2)}) collective-permute-start(f32[32,40]{1,0:T(8,128)S(1)} %reshape.77), channel_id=1, source_target_pairs={{0,1},{1,0},{2,3},{3,2},{4,5},{5,4},{6,7},{7,6},{8,9},{9,8},{10,11... | collective-permute-start | bytes 15368 | tf_op jit(solution)/shard_map/ppermute | solution.py:41
  212.7 3.1 %collective-permute-start.22 = (f32[32,40]{1,0:T(8,128)S(1)}, f32[32,40]{1,0:T(8,128)S(1)}, u32[]{:S(2)}, u32[]{:S(2)}) collective-permute-start(f32[32,40]{1,0:T(8,128)S(1)} %add.221), channel_id=1, source_target_pairs={{0,2},{1,3},{2,0},{3,1},{4,6},{5,7},{6,4},{7,5},{8,10},{9,11},{10,... | collective-permute-start | bytes 15368 | tf_op jit(solution)/shard_map/ppermute | solution.py:41
  215.8 22.4 %copy-start.14 = (bf16[160,2048]{1,0:T(8,128)(2,1)S(1)}, bf16[160,2048]{1,0:T(8,128)(2,1)}, u32[]{:S(2)}) copy-start(bf16[160,2048]{1,0:T(8,128)(2,1)} %copy-done.12) | copy-start | bytes 1966084
  215.8 22.4 %copy-start.17 = (bf16[160,2048]{1,0:T(8,128)(2,1)S(1)}, bf16[160,2048]{1,0:T(8,128)(2,1)}, u32[]{:S(2)}) copy-start(bf16[160,2048]{1,0:T(8,128)(2,1)} %copy-done.15) | copy-start | bytes 1966084
  215.8 22.4 %copy-start.18 = (bf16[640,512]{1,0:T(8,128)(2,1)S(1)}, bf16[640,512]{1,0:T(8,128)(2,1)}, u32[]{:S(2)}) copy-start(bf16[640,512]{1,0:T(8,128)(2,1)} %pad_maximum_fusion.6) | copy-start | bytes 1966084
  215.8 4.6 %collective-permute-start.23 = (f32[32,40]{1,0:T(8,128)S(1)}, f32[32,40]{1,0:T(8,128)S(1)}, u32[]{:S(2)}, u32[]{:S(2)}) collective-permute-start(f32[32,40]{1,0:T(8,128)S(1)} %add.222), channel_id=1, source_target_pairs={{0,4},{1,5},{2,6},{3,7},{4,0},{5,1},{6,2},{7,3},{8,12},{9,13},{10,... | collective-permute-start | bytes 15368 | tf_op jit(solution)/shard_map/ppermute | solution.py:41
